TPU v7x, 256 devices: a whole 4x4x8 slice. The times are simulated.
256 devices in a mesh: dp: 64 (over z, x, core), section: 4 (over y).
Axes of the slice: x: 4, y: 4, z: 8, core: 2. Of those that a mesh axis runs over, the one named last changes fastest.
Arguments:
- token_ids: int32 [4, 64, 128], P('section', 'dp'), may hold values from 0 to 511
- segment_ids: int32 [4, 64, 128], P('section', 'dp'), may hold values from 0 to 3, never falling along the last dimension, each value on 1 to 64 neighbouring positions
- row_order: int32 [4, 64], P('section', 'dp'), may hold values from 0 to 63, each once within a row
- embed_table: bfloat16 [4, 512, 4096], P('section'), may hold values from -6 to 6
- norm_gain: float32 [4, 4096], P('section'), may hold values from 0.5 to 2
- position_bias: float32 [4, 32, 64], P('section'), may hold values from -4 to 4
- returned_grad: bfloat16 [4, 8192, 4096], P('section', 'dp'), may hold values from -6 to 6
Outputs:
- handed: bfloat16 [4, 8192, 4096], P('section', 'dp')
- grad_table: float32 [4, 512, 4096], P('section', 'dp')
- grad_gain: float32 [4, 4096], P('section')
- grad_bias: float32 [4, 32, 64], P('section')
All inputs are finite; a program needn't handle non-finite values.
Results may differ from a plain program's by a relative error of at most 0.014.
Values may be sent and summed in bfloat16 or wider, within the bound.
No kernel may reach another device: no remote copies, remote signals or barrier semaphores. Data moves between devices by JAX's collectives and lax.ppermute only.
A program may use at most 128 MiB of HBM per device.

v0:
```python
import jax
import jax.numpy as jnp
from jax import lax
from jax.sharding import PartitionSpec as P

limits = (12, 16, 23, 32, 45, 64, 91)


def passed_along(value, axis, steps):
    count = lax.axis_size(axis)
    pairs = [(source, (source + steps) % count) for source in range(count)]
    return lax.ppermute(value, axis, pairs)


def bucket_table(length):
    places = jnp.arange(length, dtype=jnp.int32)
    offset = places[None, :] - places[:, None]
    apart = jnp.abs(offset)
    bucket = jnp.minimum(apart, 8)
    for limit in limits:
        bucket = bucket + (apart >= limit).astype(jnp.int32)
    bucket = bucket + 16 * (offset > 0).astype(jnp.int32)
    return bucket


def attend_row(row_normed, row_segs, bias_full, heads, head_size):
    length = row_normed.shape[0]
    split = row_normed.reshape(length, heads, head_size).astype(jnp.float32)
    scores = jnp.einsum("qhd,khd->hqk", split, split) / head_size + bias_full
    same = row_segs[:, None] == row_segs[None, :]
    scores = jnp.where(same[None, :, :], scores, -1e30)
    top = jnp.max(scores, axis=-1, keepdims=True)
    expo = jnp.exp(scores - top)
    probs = (expo / jnp.sum(expo, axis=-1, keepdims=True)).astype(jnp.bfloat16)
    mixed = jnp.einsum("hqk,khd->qhd", probs.astype(jnp.float32), split)
    return mixed.reshape(length, heads * head_size)


def layer(embedded, gain, bias, segs):
    rows_count, length = segs.shape
    width = embedded.shape[1]
    heads = bias.shape[1]
    head_size = width // heads
    wide = embedded.astype(jnp.float32)
    meansq = jnp.mean(wide * wide, axis=-1, keepdims=True)
    normed = (wide * lax.rsqrt(meansq + 1e-06) * gain).astype(jnp.bfloat16)
    picks = (bucket_table(length)[:, :, None] == jnp.arange(bias.shape[0], dtype=jnp.int32)).astype(
        jnp.float32
    )
    bias_full = jnp.einsum("qkb,bh->hqk", picks, bias)
    blocks = normed.reshape(rows_count, length, width)
    mixed = jax.vmap(
        lambda row_block, row_segs: attend_row(row_block, row_segs, bias_full, heads, head_size)
    )(blocks, segs)
    return (wide + mixed.reshape(rows_count * length, width)).astype(jnp.bfloat16)


def local(token_ids, segment_ids, row_order, embed_table, norm_gain, position_bias, returned_grad):
    all_ids, all_segs = (
        lax.all_gather(token_ids[0], "dp", axis=0, tiled=True),
        lax.all_gather(segment_ids[0], "dp", axis=0, tiled=True),
    )
    order = row_order[0]
    packed = jnp.take(all_ids, order, axis=0)
    row_segs = jnp.take(all_segs, order, axis=0)
    vocab = embed_table.shape[1]
    onehot = (packed.reshape(-1)[:, None] == jnp.arange(vocab, dtype=jnp.int32)[None, :]).astype(
        jnp.bfloat16
    )
    embedded = jnp.dot(onehot, embed_table[0], preferred_element_type=jnp.float32).astype(
        jnp.bfloat16
    )
    result, pullback = jax.vjp(
        lambda first, second, third: layer(first, second, third, row_segs),
        embedded,
        norm_gain[0],
        position_bias[0],
    )
    handed = passed_along(result, "section", 1)
    incoming = passed_along(returned_grad[0], "section", -1)
    grad_rows, grad_g, grad_b = pullback(incoming)
    table_term = lax.dot_general(
        onehot, grad_rows, (((0,), (0,)), ((), ())), preferred_element_type=jnp.float32
    )
    grad_tab = lax.psum_scatter(table_term, "dp", scatter_dimension=0, tiled=True)
    grad_g, grad_b = lax.psum((grad_g, grad_b), "dp")
    return (handed[None], grad_tab[None], grad_g[None], grad_b[None])


def solution(mesh):
    placed = (
        P("section", "dp", None),
        P("section", "dp", None),
        P("section", "dp"),
        P("section", None, None),
        P("section", None),
        P("section", None, None),
        P("section", "dp", None),
    )
    return jax.shard_map(
        local,
        mesh=mesh,
        in_specs=placed,
        out_specs=(
            P("section", "dp", None),
            P("section", "dp", None),
            P("section", None),
            P("section", None, None),
        ),
        check_vma=False,
    )
```

profile of v0, /device:TPU:1, one launch (start us, length us, event | category | flops | bytes accessed | tf_op | source)
XLA Modules:
  0.0 406.1 jit_solution(6703125069498743781)
XLA Ops:
  7.2 3.6 collective-permute-start.1
  11.6 43.4 %all-gather = s32[64,1,128]{2,1,0:T(1,128)S(1)} all-gather(s32[1,1,128]{2,1,0:T(1,128)} %param.9), channel_id=2, replica_groups=mesh['dp'=64,'section'=4] {'dp'}, dimensions={0}, use_global_device_ids=true | all-gather | bytes 33280 | tf_op jit(solution)/shard_map/all_gather | solution.py:60
  55.1 3.0 multiply_reduce_fusion.2
  58.1 37.3 %all-gather.1 = s32[64,1,128]{2,1,0:T(1,128)S(1)} all-gather(s32[1,1,128]{2,1,0:T(1,128)S(1)} %copy-done.8), channel_id=3, replica_groups=mesh['dp'=64,'section'=4] {'dp'}, dimensions={0}, use_global_device_ids=true | all-gather | bytes 33280 | tf_op jit(solution)/shard_map/all_gather | solution.py:61
  95.5 2.7 fusion.17
  98.2 1.2 multiply_convert_fusion
  99.4 0.1 broadcast_compare_fusion.1
  99.5 1.6 copy.37
  101.1 5.4 %copy.38 = f32[128,128,64]{0,1,2:T(8,128)} copy(f32[128,128,64]{1,2,0:T(8,128)} %fusion.17) | data formatting | bytes 8388608 | tf_op jit(solution)/shard_map/jvp(qkb,bh->hqk)/dot_general | solution.py:50
  106.5 3.3 fusion.47
  109.8 1.9 copy-done.2
  111.7 0.9 fusion.13
  112.7 2.3 copy.41
  115.0 4.1 fusion.6
  119.1 2.6 convert_reduce_fusion
  121.7 2.2 add_select_fusion
  123.8 1.5 fusion.11
  125.4 0.7 fusion.9
  126.1 2.0 fusion.50
  128.0 1.5 fusion.15
  129.6 1.5 bitcast_convert_fusion
  131.1 2.9 copy.45
  134.0 2.9 copy.40
  136.9 4.0 multiply_reduce_fusion
  141.0 5.9 %fusion.21 = f32[512,4096]{1,0:T(8,128)} fusion(f32[128,4096]{1,0:T(8,128)S(1)} %get-tuple-element.27, bf16[128,4096]{1,0:T(8,128)(2,1)} %collective-permute-done.1, f32[128,4096]{1,0:T(8,128)S(1)} %copy-done.5, f32[128]{0:T(128)S(1)} %multiply_multiply_fusion, f32[4096]{0:T(1024)S(1)} %bitcast.114, f32[128]{0:T(128)S(1)} %fusion.42, s32[128]{0:T(128)S(1)} %fusion.40), kind=kOutput, calls=%fused_computation.40 | convolution fusion | flops 541130752 | bytes 13649408 | tf_op jit(solution)/shard_map/dot_general | solution.py:82
  147.0 0.6 copy-done.9
  147.5 0.6 dynamic-slice.7
  148.8 4.1 %copy.47 = bf16[64,128,128]{2,0,1:T(8,128)(2,1)S(1)} copy(f32[64,128,128]{1,2,0:T(8,128)} %copy-done.4) | data formatting | bytes 6291456 | tf_op jit(solution)/shard_map/transpose(jvp(vmap(jit(_where))))/select_n | solution.py:31
  152.9 0.7 fusion.20
  153.5 243.2 %all-reduce.1 = (f32[1,4096]{1,0:T(1,128)}, f32[1,32,64]{2,1,0:T(8,128)}) all-reduce(f32[1,4096]{1,0:T(1,128)S(1)} %bitcast.115, f32[1,32,64]{2,1,0:T(8,128)S(1)} %fusion.20), channel_id=1, replica_groups=mesh['dp'=64,'section'=4] {'dp'}, use_global_device_ids=true, to_apply=%region_9.11 | all-reduce | flops 6144 | bytes 49152 | tf_op jit(solution)/shard_map/psum | solution.py:86
  396.7 1.6 dynamic-slice_bitcast_fusion
  398.3 1.0 copy.55
  (32 shorter events, 0.3 us)
Async XLA Ops:
  7.2 88.3 %copy-start = (f32[1,32,64]{2,1,0:T(8,128)S(1)}, f32[1,32,64]{2,1,0:T(8,128)}, u32[]{:S(2)}) copy-start(f32[1,32,64]{2,1,0:T(8,128)} %param.14) | copy-start | bytes 24580
  7.2 50.9 %copy-start.8 = (s32[1,1,128]{2,1,0:T(1,128)S(1)}, s32[1,1,128]{2,1,0:T(1,128)}, u32[]{:S(2)}) copy-start(s32[1,1,128]{2,1,0:T(1,128)} %param.10) | copy-start | bytes 1540
  7.2 389.5 %all-reduce.4.cloned.1.call-start = ((), (), s32[]{:S(2)}) async-start(), calls=%async_computation | async-start | bytes 16777216
  7.2 105.5 %collective-permute-start.1 = (bf16[128,4096]{1,0:T(8,128)(2,1)}, bf16[128,4096]{1,0:T(8,128)(2,1)}, u32[]{:S(2)}, u32[]{:S(2)}) collective-permute-start(bf16[128,4096]{1,0:T(8,128)(2,1)} %bitcast.118), channel_id=1, source_target_pairs={{0,3},{1,0},{2,1},{3,2},{4,7},{5,4},{6,5},{7,6},{8,11},{9,8},{10,9... | collective-permute-start | bytes 3145736 | tf_op jit(solution)/shard_map/ppermute | solution.py:12
  55.1 43.1 %copy-start.7 = (f32[1,4096]{1,0:T(1,128)S(1)}, f32[1,4096]{1,0:T(1,128)}, u32[]{:S(2)}) copy-start(f32[1,4096]{1,0:T(1,128)} %param.13) | copy-start | bytes 49156
  109.8 1.9 copy-start.2
  115.0 4.1 %copy-start.3 = (f32[64,128,128]{1,2,0:T(8,128)S(1)}, f32[64,128,128]{1,2,0:T(8,128)}, u32[]{:S(2)}) copy-start(f32[64,128,128]{1,2,0:T(8,128)} %copy-done.2) | copy-start | bytes 12582916
  123.8 2.2 copy-start.4
  126.0 2.0 copy-start.6
  136.9 4.0 copy-start.5
  146.9 0.7 copy-start.9
  146.9 249.8 %collective-permute-start = (bf16[128,4096]{1,0:T(8,128)(2,1)}, bf16[128,4096]{1,0:T(8,128)(2,1)S(1)}, u32[]{:S(2)}, u32[]{:S(2)}) collective-permute-start(bf16[128,4096]{1,0:T(8,128)(2,1)} %get-tuple-element.25), channel_id=1, source_target_pairs={{0,1},{1,2},{2,3},{3,0},{4,5},{5,6},{6,7},{7,4},{8,9},{9,10},{10,1... | collective-permute-start | bytes 3145736 | tf_op jit(solution)/shard_map/ppermute | solution.py:12
  148.1 251.1 %copy-start.1 = (f32[1,32,64]{2,1,0:T(8,128)S(1)}, f32[1,32,64]{2,1,0:T(8,128)}, u32[]{:S(2)}) copy-start(f32[1,32,64]{2,1,0:T(8,128)} %param.14) | copy-start | bytes 24580
Sparse Core Ops, SparseCore 0:
  147.0 198.7 all-reduce.3
where the time goes:
time: 410 us; the launch traced here: 406 us
  blocking collectives  324 us (79%)
  matrix products  25.3 us (6%)
  local copies, waits for them, and re-layouts  24.8 us (6%)
  between operations  15.6 us (4%)
  other arithmetic  12.7 us (3%)
    psum x1, blocking collectives, local(): grad_g, grad_b = lax.psum((grad_g, grad_b), 'dp')  243 us
    all_gather x1, blocking collectives, local(): lax.all_gather(token_ids[0], 'dp', axis=0, tiled=True)  43.4 us
    all_gather x1, blocking collectives, local(): lax.all_gather(segment_ids[0], 'dp', axis=0, tiled=True)  37.3 us
  transfers between devices with their start and end apart: 3, of which 0 were waited for; matrix products, arithmetic and copies ran while one was open for 6% of the time, Pallas kernels for 0%

commit v1 on v0

v1 whole, which is shorter than its diff:
```python
import functools

import jax
import jax.numpy as jnp
import numpy as np
from jax import lax
from jax.experimental import pallas as pl
from jax.experimental.pallas import tpu as pltpu
from jax.sharding import Mesh, PartitionSpec as P

F32, BF16 = jnp.float32, jnp.bfloat16
LIMITS = (12, 16, 23, 32, 45, 64, 91)
LOG2E = 1.4426950408889634
L = 128
NX = 4
BIG = 56 * 1024 * 1024


def bucket_picks():
    c = np.arange(L)
    r = np.where(c < 64, c, c - L)
    a = np.abs(r)
    b = np.minimum(a, 8) + sum((a >= t).astype(np.int64) for t in LIMITS) + 16 * (r > 0)
    return (np.arange(32)[:, None] == b[None, :]).astype(np.float32)


def dot(a, b, dims, precision=None):
    return lax.dot_general(a, b, (dims, ((), ())), precision=precision, preferred_element_type=F32)


NN, NT, TN = ((1,), (0,)), ((1,), (1,)), ((0,), (0,))


def halves(tile):
    low = lax.broadcasted_iota(jnp.int32, tile.shape, 1) < 64
    zero = jnp.zeros_like(tile)
    return jnp.concatenate([jnp.where(low, tile, zero), jnp.where(low, zero, tile)], axis=0)


def offset_sums(square):
    acc = square[:8]
    for k in range(8, L, 8):
        acc = acc + pltpu.roll(square[k : k + 8], L - k, 1)
    row = lax.broadcasted_iota(jnp.int32, acc.shape, 0)
    for bit in (1, 2, 4):
        acc = jnp.where((row & bit) != 0, pltpu.roll(acc, L - bit, 1), acc)
    return jnp.sum(acc, axis=0, keepdims=True)


def pre_kernel(x_ref, table_ref, gain_ref, pos_ref, picks_ref, ne_ref, r_ref, bvec_ref):
    width = table_ref.shape[1]
    part = width // NX
    wide = table_ref[...].astype(F32)
    r = lax.rsqrt(jnp.sum(wide * wide, axis=1, keepdims=True) * (1.0 / width) + 1e-06)
    r_ref[...] = jnp.broadcast_to(r, r_ref.shape)
    cols = pl.ds(pl.multiple_of(x_ref[0] * part, L), part)
    own = table_ref[:, cols]
    ne_ref[:, :part] = (own.astype(F32) * r * gain_ref[:, cols]).astype(BF16)
    ne_ref[:, part:] = own
    bvec_ref[...] = dot(pos_ref[...], picks_ref[...], TN, lax.Precision.HIGHEST) * LOG2E


def prepare(x, table, gain, pos, picks):
    vocab, width = table.shape
    part = width // NX
    rows = 64
    heads = pos.shape[1]
    return pl.pallas_call(
        pre_kernel,
        grid_spec=pltpu.PrefetchScalarGridSpec(
            num_scalar_prefetch=1,
            grid=(vocab // rows,),
            in_specs=[
                pl.BlockSpec((rows, width), lambda i, x: (i, 0)),
                pl.BlockSpec((1, width), lambda i, x: (0, 0)),
                pl.BlockSpec(pos.shape, lambda i, x: (0, 0)),
                pl.BlockSpec(picks.shape, lambda i, x: (0, 0)),
            ],
            out_specs=[
                pl.BlockSpec((rows, 2 * part), lambda i, x: (i, 0)),
                pl.BlockSpec((rows, L), lambda i, x: (i, 0)),
                pl.BlockSpec((heads, L), lambda i, x: (0, 0)),
            ],
        ),
        out_shape=[
            jax.ShapeDtypeStruct((vocab, 2 * part), BF16),
            jax.ShapeDtypeStruct((vocab, L), F32),
            jax.ShapeDtypeStruct((heads, L), F32),
        ],
        cost_estimate=pl.CostEstimate(flops=vocab * width * 4, bytes_accessed=7 << 20, transcendentals=0),
        name="prepare",
    )(x, table, gain, pos, picks)


def onehot_t(ids_row, vocab):
    v = lax.broadcasted_iota(jnp.int32, (vocab, ids_row.shape[1]), 0)
    return jnp.where(v == ids_row, 1.0, 0.0).astype(BF16)


def fwd_kernel(where_ref, order_ref, ids_ref, segs_ref, ne_ref, bvec_ref, *rest):
    a_refs, (n_ref, p_ref), (e_ref, m_ref) = rest[:NX], rest[NX : NX + 2], rest[NX + 2 :]
    part = ne_ref.shape[1] // 2
    vocab = ne_ref.shape[0]
    pairs = part // L
    for s in range(NX):
        row = order_ref[where_ref[1 + s]]
        both = dot(onehot_t(ids_ref[pl.ds(row, 1), :], vocab), ne_ref[...], TN)
        n_ref[s] = both[:, :part].astype(BF16)
        e_ref[s] = both[:, part:].astype(BF16)
        seg = jnp.broadcast_to(segs_ref[pl.ds(row, 1), :], (L, L)).astype(F32)
        m_ref[s] = jnp.where(seg == seg.T, 0.0, -1e30)

    @pl.loop(0, pairs)
    def _(p):
        cols = pl.ds(pl.multiple_of(p * L, L), L)
        head = where_ref[0] * (2 * pairs) + 2 * p
        biases = [
            pltpu.roll(
                jnp.broadcast_to(bvec_ref[pl.ds(head + k, 1), :], (L, L)), 0, 1, stride=1, stride_axis=0
            )
            for k in range(2)
        ]
        for s in range(NX):
            tile = n_ref[s, :, cols]
            two = halves(tile)
            mask = m_ref[s]
            scores = dot(two, tile, NT) * (LOG2E / 64.0)
            scores = scores + jnp.concatenate([biases[0] + mask, biases[1] + mask], axis=0)
            expo = jnp.exp2(scores - jnp.max(scores, axis=1, keepdims=True))
            probs = (expo * (1.0 / jnp.sum(expo, axis=1, keepdims=True))).astype(BF16)
            p_ref[p, s] = probs
            mixed = dot(jnp.concatenate([probs[:L], probs[L:]], axis=1), two, NN)
            a_refs[s][:, cols] = (e_ref[s, :, cols].astype(F32) + mixed).astype(BF16)


def forward(where, order, ids, segs, ne, bvec):
    part = ne.shape[1] // 2
    pairs = part // L
    smem, vmem = pl.BlockSpec(memory_space=pltpu.SMEM), pl.BlockSpec(memory_space=pltpu.VMEM)
    return pl.pallas_call(
        fwd_kernel,
        in_specs=[smem, smem, vmem, vmem, vmem, vmem],
        out_specs=[vmem] * (NX + 2),
        out_shape=[jax.ShapeDtypeStruct((L, part), BF16)] * NX
        + [
            jax.ShapeDtypeStruct((NX, L, part), BF16),
            jax.ShapeDtypeStruct((pairs, NX, 2 * L, L), BF16),
        ],
        scratch_shapes=[pltpu.VMEM((NX, L, part), BF16), pltpu.VMEM((NX, L, L), F32)],
        compiler_params=pltpu.CompilerParams(vmem_limit_bytes=BIG),
        cost_estimate=pl.CostEstimate(flops=2 << 30, bytes_accessed=8 << 20, transcendentals=1 << 20),
        name="forward",
    )(where, order, ids, segs, ne, bvec)


def bwd_kernel(where_ref, order_ref, ids_ref, ne_ref, r_ref, gain_ref, picks_ref, n_ref, p_ref, *rest):
    g_refs, (mine_ref, other_ref), (d_ref, rg_ref, o_ref, diag_ref) = rest[:NX], rest[NX : NX + 2], rest[NX + 2 :]
    vocab, part = ne_ref.shape[0], ne_ref.shape[1] // 2
    pairs = part // L
    blocks = vocab // 16
    core = where_ref[5]

    @pl.loop(0, pairs)
    def _(p):
        cols = pl.ds(pl.multiple_of(p * L, L), L)
        total = jnp.zeros((2 * L, L), F32)
        for s in range(NX):
            tile, up = n_ref[s, :, cols], g_refs[s][:, cols]
            rg_ref[pl.ds(s * L, L), cols] = up
            two, ups = halves(tile), halves(up)
            probs = p_ref[p, s]
            wide = probs.astype(F32)
            d_probs = dot(ups, tile, NT).astype(BF16).astype(F32)
            both = wide * d_probs
            d_scores = both - wide * jnp.sum(both, axis=1, keepdims=True)
            total = total + d_scores
            small = (d_scores * (1.0 / 64.0)).astype(BF16)
            left = jnp.concatenate([probs, small], axis=0)
            right = jnp.concatenate([ups, two], axis=0)
            d_norm = dot(left, right, TN)
            d_norm = d_norm + dot(jnp.concatenate([small[:L], small[L:]], axis=1), two, NN)
            d_ref[pl.ds(s * L, L), cols] = d_norm.astype(BF16)
        for k in range(2):
            diag_ref[pl.ds(2 * p + k, 1), :] = offset_sums(total[k * L : (k + 1) * L])

    for s in range(NX):
        row = order_ref[where_ref[1 + s]]
        o_ref[:, s * L : (s + 1) * L] = onehot_t(ids_ref[pl.ds(row, 1), :], vocab)

    def put(tile, value):
        value = value.reshape(blocks, 2, 8, L)
        first, second = value[:, 0], value[:, 1]
        mine_ref[0:blocks, tile] = jnp.where(core == 0, first, second)
        other_ref[0:blocks, tile] = jnp.where(core == 0, second, first)

    r = r_ref[...]
    along = jnp.zeros((vocab, L), F32)
    for f in range(pairs):
        cols = slice(f * L, (f + 1) * L)
        d_act = dot(o_ref[...], rg_ref[:, cols], NN)
        d_norm = dot(o_ref[...], d_ref[:, cols], NN)
        gain = gain_ref[:, cols]
        own = ne_ref[:, part + f * L : part + (f + 1) * L].astype(F32)
        scaled = d_norm * r
        put(f, d_act + scaled * gain)
        along = along + own * (d_norm * gain)
        g_row = jnp.sum(own * scaled, axis=0, keepdims=True)
        mine_ref[blocks, 0, pl.ds(f, 1), :] = g_row
        other_ref[blocks, 0, pl.ds(f, 1), :] = g_row
    put(pairs, along)
    sums = dot(diag_ref[...], picks_ref[...], NT, lax.Precision.HIGHEST)
    for ref in (mine_ref, other_ref):
        ref[blocks, 1] = sums[:8]
        ref[blocks, 2] = sums[8:]
        for tile in range(3, pairs + 1):
            ref[blocks, tile] = jnp.zeros((8, L), F32)


def backward(where, order, ids, ne, r, gain, picks, n, probs, grads):
    vocab, part = ne.shape[0], ne.shape[1] // 2
    pairs = part // L
    smem, vmem = pl.BlockSpec(memory_space=pltpu.SMEM), pl.BlockSpec(memory_space=pltpu.VMEM)
    out = jax.ShapeDtypeStruct((vocab // 16 + 1, pairs + 1, 8, L), F32)
    return pl.pallas_call(
        bwd_kernel,
        in_specs=[smem, smem] + [vmem] * (7 + NX),
        out_specs=[vmem, vmem],
        out_shape=[out, out],
        scratch_shapes=[
            pltpu.VMEM((NX * L, part), BF16),
            pltpu.VMEM((NX * L, part), BF16),
            pltpu.VMEM((vocab, NX * L), BF16),
            pltpu.VMEM((2 * pairs, L), F32),
        ],
        compiler_params=pltpu.CompilerParams(vmem_limit_bytes=BIG),
        cost_estimate=pl.CostEstimate(flops=4 << 30, bytes_accessed=10 << 20, transcendentals=0),
        name="backward",
    )(where, order, ids, ne, r, gain, picks, n, probs, *grads)


def join_kernel(mine_ref, came_ref, out_ref):
    blocks, tiles = mine_ref.shape[0] - 1, mine_ref.shape[1]
    for t in range(tiles):
        out_ref[:, t] = (mine_ref[0:blocks, t] + came_ref[0:blocks, t]).astype(BF16)
    for t in range(3):
        value = mine_ref[blocks, t] + came_ref[blocks, t]
        high = value.astype(BF16)
        out_ref[:, tiles + t] = jnp.broadcast_to(high[None], (blocks, 8, L))
        low = (value - high.astype(F32)).astype(BF16)
        out_ref[:, tiles + 3 + t] = jnp.broadcast_to(low[None], (blocks, 8, L))


def join(mine, came):
    blocks, tiles = mine.shape[0] - 1, mine.shape[1]
    vmem = pl.BlockSpec(memory_space=pltpu.VMEM)
    return pl.pallas_call(
        join_kernel,
        in_specs=[vmem, vmem],
        out_specs=vmem,
        out_shape=jax.ShapeDtypeStruct((blocks, tiles + 6, 8, L), BF16),
        compiler_params=pltpu.CompilerParams(vmem_limit_bytes=BIG),
        cost_estimate=pl.CostEstimate(flops=1 << 20, bytes_accessed=4 << 20, transcendentals=0),
        name="join",
    )(mine, came)


def last_kernel(where_ref, parts_ref, table_ref, r_ref, t_ref, g_ref, b_ref, h_ref):
    sources, tiles = parts_ref.shape[0], parts_ref.shape[1]
    feats = tiles - 7
    width = table_ref.shape[1]

    def total(x, tile):
        value = parts_ref[x, tile].astype(F32)
        for z in range(1, sources // NX):
            value = value + parts_ref[z * NX + x, tile].astype(F32)
        return value

    along = total(0, feats)
    for x in range(1, NX):
        along = along + total(x, feats)
    along = jnp.sum(along, axis=1, keepdims=True)
    at = pl.multiple_of(where_ref[6] * 8, 8)
    r = r_ref[pl.ds(at, 8), :][:, :1]
    own = table_ref[...].astype(F32) * (along * (r * r * r) * (1.0 / width))
    for x in range(NX):
        for f in range(feats):
            c = (x * feats + f) * L
            t_ref[0, :, c : c + L] = total(x, f) - own[:, c : c + L]
        gains = total(x, feats + 1) + total(x, feats + 4)
        for f in range(feats):
            c = (x * feats + f) * L
            g_ref[0:1, c : c + L] = gains[f : f + 1]
        h_ref[x * 16 : x * 16 + 8, :] = total(x, feats + 2) + total(x, feats + 5)
        h_ref[x * 16 + 8 : x * 16 + 16, :] = total(x, feats + 3) + total(x, feats + 6)
    b_ref[0] = h_ref[...].T[:32]


def finish(where, parts, table, r):
    width = table.shape[1]
    smem, vmem = pl.BlockSpec(memory_space=pltpu.SMEM), pl.BlockSpec(memory_space=pltpu.VMEM)
    return pl.pallas_call(
        last_kernel,
        in_specs=[smem, vmem, vmem, vmem],
        out_specs=[vmem] * 3,
        out_shape=[
            jax.ShapeDtypeStruct((1, 8, width), F32),
            jax.ShapeDtypeStruct((1, width), F32),
            jax.ShapeDtypeStruct((1, 32, 64), F32),
        ],
        scratch_shapes=[pltpu.VMEM((64, L), F32)],
        compiler_params=pltpu.CompilerParams(vmem_limit_bytes=BIG),
        cost_estimate=pl.CostEstimate(flops=1 << 20, bytes_accessed=2 << 20, transcendentals=0),
        name="finish",
    )(where, parts, table, r)


def local(picks, token_ids, segment_ids, row_order, embed_table, norm_gain, position_bias, returned_grad):
    x, z, c = lax.axis_index("x"), lax.axis_index("z"), lax.axis_index("c")
    table, gain, pos, grad = embed_table[0], norm_gain, position_bias[0], returned_grad[0]
    part = table.shape[1] // NX
    sections = lax.axis_size("section")
    slots = [lax.rem(x + NX - s, NX) for s in range(NX)]
    me = (z * NX + x) * 2 + c
    where = jnp.stack([x] + [(z * NX + k) * 2 + c for k in slots] + [c, me]).astype(jnp.int32)

    def send(value, steps, along):
        pairs = [
            (i * sections + j, (i + steps) % NX * sections + (j + along) % sections)
            for i in range(NX)
            for j in range(sections)
        ]
        return lax.ppermute(value, ("x", "section"), pairs)

    grads = [
        send(lax.dynamic_slice(grad, (0, lax.rem(x + s, NX) * part), (L, part)), s, -1) for s in range(NX)
    ]

    ne, r, bvec = prepare(x[None], table, gain, pos, picks)
    count = 64
    note = jnp.concatenate([token_ids[0], segment_ids[0], jnp.broadcast_to(row_order, (1, L))], axis=0)
    notes = lax.all_to_all(jnp.broadcast_to(note[None], (count, 3, L)), ("z", "x", "c"), 0, 0)
    ids, segs, order = notes[:, 0], notes[:, 1], notes[:, 2, 0]

    *acts, normed, probs = forward(where, order, ids, segs, ne, bvec)
    pieces = [send(acts[s], -s, 1) for s in range(NX)]
    handed = jnp.zeros((L, NX * part), BF16)
    for s in range(NX):
        handed = lax.dynamic_update_slice(handed, pieces[s], (0, lax.rem(x + s, NX) * part))

    own_gain = lax.dynamic_slice(gain, (0, x * part), (1, part))
    wide_picks = jnp.concatenate([picks, jnp.zeros((L - picks.shape[0], L), F32)], axis=0)
    mine, other = backward(where, order, ids, ne, r, own_gain, wide_picks, normed, probs, grads)
    came = lax.ppermute(other, "c", [(0, 1), (1, 0)])
    parts = lax.all_to_all(join(mine, came), ("z", "x"), 0, 0)
    rows = lax.dynamic_slice(table, (me * 8, 0), (8, table.shape[1]))
    return (handed[None],) + tuple(finish(where, parts, rows, r))


def solution(mesh):
    fine = Mesh(mesh.devices.reshape(8, NX, 2, 4), ("z", "x", "c", "section"))
    dp = ("z", "x", "c")
    placed = (
        P(),
        P("section", dp, None),
        P("section", dp, None),
        P("section", dp),
        P("section", None, None),
        P("section", None),
        P("section", None, None),
        P("section", dp, None),
    )
    mapped = jax.shard_map(
        local,
        mesh=fine,
        in_specs=placed,
        out_specs=(
            P("section", dp, None),
            P("section", dp, None),
            P("section", None),
            P("section", None, None),
        ),
        check_vma=False,
    )
    return lambda *args: mapped(jnp.asarray(bucket_picks()), *args)
```

time: 410 us -> 115 us (0.28)
  blocking collectives: 324 us -> 0 us
  Pallas kernels: 0 us -> 39.5 us
  starting transfers between devices: 3.76 us -> 35.8 us
  waiting for transfers between devices: 0.02 us -> 26.1 us
  matrix products: 25.3 us -> 0 us
  between operations: 15.6 us -> 1.48 us
  local copies, waits for them, and re-layouts: 24.8 us -> 11.1 us
  other arithmetic: 12.7 us -> 0.74 us
    psum x1 -> x0, blocking collectives: 243 us -> none  [local(): grad_g, grad_b = lax.psum((grad_g, grad_b), 'dp')]
    all_gather x2 -> x0, blocking collectives: 80.8 us -> none  [the longest x1 43.4 us: local(): lax.all_gather(token_ids[0], 'dp', axis=0, tiled=True)]
    pallas_call x0 -> x5, Pallas kernels: none -> 39.5 us  [the longest x1 15.5 us: backward(): pl.pallas_call(bwd_kernel, in_specs=[smem, smem] + [vmem] * (7 + NX), out...]
    ppermute x2 -> x9, waiting for transfers between devices: 0.01 us -> 26.1 us  [the longest x8 23.4 us: send(): return lax.ppermute(value, ('x', 'section'), pairs)]
    dot_general x10 -> x0, matrix products: 25.3 us -> none  [the longest x3 7.57 us: attend_row(): mixed = jnp.einsum('hqk,khd->qhd', probs.astype(jnp.float32), split)]
    all_to_all x0 -> x2, starting transfers between devices: none -> 19.9 us  [the longest x1 13 us: local(): lax.all_to_all(jnp.broadcast_to(note[None], (count, 3, L)), ('z', 'x', 'c...]
    ppermute x2 -> x9, starting transfers between devices: 3.72 us -> 15.9 us  [the longest x8 14.4 us: send(): return lax.ppermute(value, ('x', 'section'), pairs)]
    reduce_sum x3 -> x0, other arithmetic: 7.52 us -> none  [the longest x1 4.02 us: layer(): normed = (wide * lax.rsqrt(meansq + 1e-06) * gain).astype(jnp.bfloat16)]
  transfers between devices with their start and end apart: 3 -> 11, of which waited for: 0 -> 5; matrix products, arithmetic and copies ran while one was open for 6% -> 6% of each run, Pallas kernels for 0% -> 17%
where the time goes in v1:
time: 115 us
  Pallas kernels  39.5 us (34%)
  starting transfers between devices  35.8 us (31%)
  waiting for transfers between devices  26.1 us (23%)
  local copies, waits for them, and re-layouts  11.1 us (10%)
  between operations  1.48 us (1%)
    ppermute x8, waiting for transfers between devices, send(): return lax.ppermute(value, ('x', 'section'), pairs)  23.4 us
    pallas_call x1, Pallas kernels, backward(): pl.pallas_call(bwd_kernel, in_specs=[smem, smem] + [vmem] * (7 + NX), out...  15.5 us
    ppermute x8, starting transfers between devices, send(): return lax.ppermute(value, ('x', 'section'), pairs)  14.4 us
    all_to_all x1, starting transfers between devices, local(): lax.all_to_all(jnp.broadcast_to(note[None], (count, 3, L)), ('z', 'x', 'c...  13 us
    pallas_call x1, Pallas kernels, forward(): pl.pallas_call(fwd_kernel, in_specs=[smem, smem, vmem, vmem, vmem, vmem],...  12.1 us
    pallas_call x1, Pallas kernels, prepare(): pl.pallas_call(pre_kernel, grid_spec=pltpu.PrefetchScalarGridSpec(num_sca...  6.92 us
    all_to_all x1, starting transfers between devices, local(): parts = lax.all_to_all(join(mine, came), ('z', 'x'), 0, 0)  6.89 us
    unnamed x22, local copies, waits for them, and re-layouts  3.05 us
  transfers between devices with their start and end apart: 11, of which 5 were waited for; matrix products, arithmetic and copies ran while one was open for 6% of the time, Pallas kernels for 17%

profile of v1, /device:TPU:1, one launch (start us, length us, event | category | flops | bytes accessed | tf_op | source)
XLA Modules:
  0.0 114.7 jit_solution(3644310473680974080)
XLA Ops:
  1.4 0.7 add_add_fusion
  2.1 0.7 broadcast_in_dim.30
  2.8 13.0 %all-to-all-start = ((s32[64,3,128]{2,1,0:T(4,128)}), s32[64,3,128]{2,1,0:T(4,128)S(1)}, u32[]{:S(2)}, u32[]{:S(2)}) async-start(s32[64,3,128]{2,1,0:T(4,128)} %broadcast_in_dim.30), calls=%async_computation | async-start | bytes 262144 | tf_op jit(solution)/shard_map/all_to_all | solution.py:341
  15.8 1.3 %dynamic-slice_bitcast_fusion = (bf16[128,1024]{1,0:T(8,128)(2,1)S(1)}, bf16[128,1024]{1,0:T(8,128)(2,1)S(1)}, bf16[128,1024]{1,0:T(8,128)(2,1)S(1)}, bf16[128,1024]{1,0:T(8,128)(2,1)S(1)}) fusion(bf16[1,128,4096]{2,1,0:T(8,128)(2,1)} %param.14, s32[]{:T(128)S(6)} %select_n.25, s32[]{:T(128)S(6)} %select_n.23, s32[]{:T(128)S(6)} %select_n.22, s32[]{:T(128)S(6)} %select_n.24), kind=kLoop, calls=%fused_computation.4 | loop fusion | bytes 2097168 | tf_op jit(solution)/shard_map/dynamic_slice | solution.py:335
  17.1 2.8 %collective-permute-start.4 = (bf16[128,1024]{1,0:T(8,128)(2,1)S(1)}, bf16[128,1024]{1,0:T(8,128)(2,1)S(1)}, u32[]{:S(2)}, u32[]{:S(2)}) collective-permute-start(bf16[128,1024]{1,0:T(8,128)(2,1)S(1)} %get-tuple-element.34), channel_id=1, source_target_pairs={{0,3},{1,0},{2,1},{3,2},{8,11},{9,8},{10,9},{11,10},{16,19},{17,16... | collective-permute-start | bytes 786440 | tf_op jit(solution)/shard_map/ppermute | solution.py:332
  19.9 1.6 %collective-permute-start.5 = (bf16[128,1024]{1,0:T(8,128)(2,1)S(1)}, bf16[128,1024]{1,0:T(8,128)(2,1)S(1)}, u32[]{:S(2)}, u32[]{:S(2)}) collective-permute-start(bf16[128,1024]{1,0:T(8,128)(2,1)S(1)} %get-tuple-element.33), channel_id=1, source_target_pairs={{0,11},{1,8},{2,9},{3,10},{8,19},{9,16},{10,17},{11,18},{16,27},{1... | collective-permute-start | bytes 786440 | tf_op jit(solution)/shard_map/ppermute | solution.py:332
  21.4 2.3 %collective-permute-start.6 = (bf16[128,1024]{1,0:T(8,128)(2,1)S(1)}, bf16[128,1024]{1,0:T(8,128)(2,1)S(1)}, u32[]{:S(2)}, u32[]{:S(2)}) collective-permute-start(bf16[128,1024]{1,0:T(8,128)(2,1)S(1)} %get-tuple-element.35), channel_id=1, source_target_pairs={{0,19},{1,16},{2,17},{3,18},{8,27},{9,24},{10,25},{11,26},{16,3},{... | collective-permute-start | bytes 786440 | tf_op jit(solution)/shard_map/ppermute | solution.py:332
  23.7 1.1 collective-permute-start.7
  24.8 0.7 stack.31.where_ref
  25.4 6.9 %prepare.1 = (bf16[512,2048]{1,0:T(8,128)(2,1)}, f32[512,128]{1,0:T(8,128)}, f32[64,128]{1,0:T(8,128)}) custom-call(s32[1]{0:T(128)} %bitcast.x_ref, bf16[512,4096]{1,0:T(8,128)(2,1)} %bitcast.39, f32[1,4096]{1,0:T(1,128)} %gain_ref.1, f32[32,64]{1,0:T(8,128)} %bitcast.43, f32[32,128]{1,0:T(8,128)} %constant.70.clone.picks_ref), custom_call_target="tpu_custom_call" | custom-call | flops 8388608 | bytes 7340032 | tf_op jit(solution)/shard_map/prepare/pallas_call | solution.py:68
  32.4 1.3 %constant_dynamic-slice_fusion.gain_ref = f32[1,1024]{1,0:T(1,128)} fusion(f32[1,4096]{1,0:T(1,128)} %gain_ref.1, s32[]{:T(128)S(6)} %select_n.26), kind=kLoop, calls=%fused_computation.10 | loop fusion | bytes 8196 | tf_op jit(solution)/shard_map/dynamic_slice | solution.py:350
  33.7 0.7 fusion
  34.3 1.7 %slice_reduce_fusion.order_ref = s32[64]{0:T(128)} fusion(s32[64,3,128]{2,1,0:T(4,128)S(1)} %all-to-all-done), kind=kLoop, calls=%fused_computation.9 | loop fusion | bytes 512 | tf_op jit(solution)/shard_map/slice | solution.py:342
  36.1 12.1 %forward.1 = (bf16[128,1024]{1,0:T(8,128)(2,1)}, bf16[128,1024]{1,0:T(8,128)(2,1)}, bf16[128,1024]{1,0:T(8,128)(2,1)}, bf16[128,1024]{1,0:T(8,128)(2,1)}, bf16[4...) custom-call(s32[7]{0:T(128)} %stack.31.where_ref, s32[64]{0:T(128)} %slice_reduce_fusion.order_ref, ...), custom_call_target="tpu_custom_call" | custom-call | flops 2147483648 | bytes 8388608 | tf_op jit(solution)/shard_map/forward/pallas_call | solution.py:140
  48.3 0.7 copy-done.3
  49.2 15.5 %backward.1 = (f32[33,9,8,128]{3,2,1,0:T(8,128)}, f32[33,9,8,128]{3,2,1,0:T(8,128)}) custom-call(s32[7]{0:T(128)} %stack.31.where_ref, s32[64]{0:T(128)} %slice_reduce_fusion.order_ref, s32[64,128]{1,0:T(8,128)} %bitcast.41, bf16[512,2048]{1,0:T(8,128)(2,1)} %get-tuple-element.18.ne_ref, f32[512,128]{1,0:T(8,128)} %get-tuple-element.24.r_ref, ...), custom_call_target="tpu_custom_call" | custom-call | flops 4294967296 | bytes 10485760 | tf_op jit(solution)/shard_map/backward/pallas_call | solution.py:224
  64.8 1.5 %collective-permute-start.8 = (f32[33,9,8,128]{3,2,1,0:T(8,128)}, f32[33,9,8,128]{3,2,1,0:T(8,128)S(1)}, u32[]{:S(2)}, u32[]{:S(2)}) collective-permute-start(f32[33,9,8,128]{3,2,1,0:T(8,128)} %get-tuple-element.28), channel_id=1, source_target_pairs={{0,4},{4,0},{1,5},{5,1},{2,6},{6,2},{3,7},{7,3},{8,12},{12,8},{9,1... | collective-permute-start | bytes 3649544 | tf_op jit(solution)/shard_map/ppermute | solution.py:353
  66.2 2.7 %collective-permute-done.8.came_ref = f32[33,9,8,128]{3,2,1,0:T(8,128)S(1)} collective-permute-done((f32[33,9,8,128]{3,2,1,0:T(8,128)}, f32[33,9,8,128]{3,2,1,0:T(8,128)S(1)}, u32[]{:S(2)}, u32[]{:S(2)}) %collective-permute-start.8) | collective-permute-done | bytes 1216544 | tf_op jit(solution)/shard_map/ppermute | solution.py:353
  69.0 1.0 copy-done.1
  70.0 2.8 %join.1 = bf16[32,15,8,128]{3,2,1,0:T(8,128)(2,1)} custom-call(f32[33,9,8,128]{3,2,1,0:T(8,128)} %get-tuple-element.27.mine_ref, f32[33,9,8,128]{3,2,1,0:T(8,128)} %copy-done.1), custom_call_target="tpu_custom_call" | custom-call | flops 1048576 | bytes 4194304 | tf_op jit(solution)/shard_map/join/pallas_call | solution.py:256
  72.9 6.9 %all-to-all-start.1 = ((bf16[32,15,8,128]{3,2,1,0:T(8,128)(2,1)}), bf16[32,15,8,128]{3,2,1,0:T(8,128)(2,1)S(1)}, u32[]{:S(2)}, u32[]{:S(2)}) async-start(bf16[32,15,8,128]{3,2,1,0:T(8,128)(2,1)} %join.1), calls=%async_computation.1 | async-start | bytes 1966080 | tf_op jit(solution)/shard_map/all_to_all | solution.py:354
  79.8 1.6 %collective-permute-start = (bf16[128,1024]{1,0:T(8,128)(2,1)S(1)}, bf16[128,1024]{1,0:T(8,128)(2,1)S(1)}, u32[]{:S(2)}, u32[]{:S(2)}) collective-permute-start(bf16[128,1024]{1,0:T(8,128)(2,1)S(1)} %copy-done.10), channel_id=1, source_target_pairs={{0,1},{1,2},{2,3},{3,0},{8,9},{9,10},{10,11},{11,8},{16,17},{17,18... | collective-permute-start | bytes 786440 | tf_op jit(solution)/shard_map/ppermute | solution.py:332
  81.4 3.5 %collective-permute-start.1 = (bf16[128,1024]{1,0:T(8,128)(2,1)S(1)}, bf16[128,1024]{1,0:T(8,128)(2,1)S(1)}, u32[]{:S(2)}, u32[]{:S(2)}) collective-permute-start(bf16[128,1024]{1,0:T(8,128)(2,1)S(1)} %copy-done.9), channel_id=1, source_target_pairs={{0,25},{1,26},{2,27},{3,24},{8,1},{9,2},{10,3},{11,0},{16,9},{17,1... | collective-permute-start | bytes 786440 | tf_op jit(solution)/shard_map/ppermute | solution.py:332
  84.8 1.5 %dynamic-slice_bitcast_fusion.4.table_ref = bf16[8,4096]{1,0:T(8,128)(2,1)} fusion(bf16[1,512,4096]{2,1,0:T(8,128)(2,1)} %param.11, s32[]{:T(128)S(6)} %select_n.27), kind=kLoop, calls=%fused_computation.8 | loop fusion | bytes 131076 | tf_op jit(solution)/shard_map/dynamic_slice | solution.py:355
  86.3 1.3 %collective-permute-start.2 = (bf16[128,1024]{1,0:T(8,128)(2,1)S(1)}, bf16[128,1024]{1,0:T(8,128)(2,1)S(1)}, u32[]{:S(2)}, u32[]{:S(2)}) collective-permute-start(bf16[128,1024]{1,0:T(8,128)(2,1)S(1)} %copy-done.8), channel_id=1, source_target_pairs={{0,17},{1,18},{2,19},{3,16},{8,25},{9,26},{10,27},{11,24},{16,1},{... | collective-permute-start | bytes 786440 | tf_op jit(solution)/shard_map/ppermute | solution.py:332
  87.6 0.4 collective-permute-start.3
  88.0 2.1 %collective-permute-done = bf16[128,1024]{1,0:T(8,128)(2,1)S(1)} collective-permute-done((bf16[128,1024]{1,0:T(8,128)(2,1)S(1)}, bf16[128,1024]{1,0:T(8,128)(2,1)S(1)}, u32[]{:S(2)}, u32[]{:S(2)}) %collective-permute-start) | collective-permute-done | bytes 262176 | tf_op jit(solution)/shard_map/ppermute | solution.py:332
  90.2 9.3 %collective-permute-done.1 = bf16[128,1024]{1,0:T(8,128)(2,1)S(1)} collective-permute-done((bf16[128,1024]{1,0:T(8,128)(2,1)S(1)}, bf16[128,1024]{1,0:T(8,128)(2,1)S(1)}, u32[]{:S(2)}, u32[]{:S(2)}) %collective-permute-start.1) | collective-permute-done | bytes 262176 | tf_op jit(solution)/shard_map/ppermute | solution.py:332
  99.5 3.1 %collective-permute-done.2 = bf16[128,1024]{1,0:T(8,128)(2,1)S(1)} collective-permute-done((bf16[128,1024]{1,0:T(8,128)(2,1)S(1)}, bf16[128,1024]{1,0:T(8,128)(2,1)S(1)}, u32[]{:S(2)}, u32[]{:S(2)}) %collective-permute-start.2) | collective-permute-done | bytes 262176 | tf_op jit(solution)/shard_map/ppermute | solution.py:332
  102.6 8.9 %collective-permute-done.3 = bf16[128,1024]{1,0:T(8,128)(2,1)S(1)} collective-permute-done((bf16[128,1024]{1,0:T(8,128)(2,1)S(1)}, bf16[128,1024]{1,0:T(8,128)(2,1)S(1)}, u32[]{:S(2)}, u32[]{:S(2)}) %collective-permute-start.3) | collective-permute-done | bytes 262176 | tf_op jit(solution)/shard_map/ppermute | solution.py:332
  111.6 1.0 copy-done
  112.6 2.1 %finish.1 = (f32[1,8,4096]{2,1,0:T(8,128)}, f32[1,4096]{1,0:T(1,128)}, f32[1,32,64]{2,1,0:T(8,128)}) custom-call(s32[7]{0:T(128)} %stack.31.where_ref, bf16[32,15,8,128]{3,2,1,0:T(8,128)(2,1)} %copy-done, bf16[8,4096]{1,0:T(8,128)(2,1)} %dynamic-slice_bitcast_fusion.4.table_ref, f32[512,128]{1,0:T(8,128)} %get-tuple-element.24.r_ref), custom_call_target="tpu_custom_call" | custom-call | flops 1048576 | bytes 2097152 | tf_op jit(solution)/shard_map/finish/pallas_call | solution.py:301
  (31 shorter events, 0.6 us)
Async XLA Ops:
  2.8 30.9 %all-to-all-start = ((s32[64,3,128]{2,1,0:T(4,128)}), s32[64,3,128]{2,1,0:T(4,128)S(1)}, u32[]{:S(2)}, u32[]{:S(2)}) async-start(s32[64,3,128]{2,1,0:T(4,128)} %broadcast_in_dim.30), calls=%async_computation | async-start | bytes 262144 | tf_op jit(solution)/shard_map/all_to_all | solution.py:341
  17.1 31.1 %collective-permute-start.4 = (bf16[128,1024]{1,0:T(8,128)(2,1)S(1)}, bf16[128,1024]{1,0:T(8,128)(2,1)S(1)}, u32[]{:S(2)}, u32[]{:S(2)}) collective-permute-start(bf16[128,1024]{1,0:T(8,128)(2,1)S(1)} %get-tuple-element.34), channel_id=1, source_target_pairs={{0,3},{1,0},{2,1},{3,2},{8,11},{9,8},{10,9},{11,10},{16,19},{17,16... | collective-permute-start | bytes 786440 | tf_op jit(solution)/shard_map/ppermute | solution.py:332
  19.9 28.3 %collective-permute-start.5 = (bf16[128,1024]{1,0:T(8,128)(2,1)S(1)}, bf16[128,1024]{1,0:T(8,128)(2,1)S(1)}, u32[]{:S(2)}, u32[]{:S(2)}) collective-permute-start(bf16[128,1024]{1,0:T(8,128)(2,1)S(1)} %get-tuple-element.33), channel_id=1, source_target_pairs={{0,11},{1,8},{2,9},{3,10},{8,19},{9,16},{10,17},{11,18},{16,27},{1... | collective-permute-start | bytes 786440 | tf_op jit(solution)/shard_map/ppermute | solution.py:332
  21.4 26.8 %collective-permute-start.6 = (bf16[128,1024]{1,0:T(8,128)(2,1)S(1)}, bf16[128,1024]{1,0:T(8,128)(2,1)S(1)}, u32[]{:S(2)}, u32[]{:S(2)}) collective-permute-start(bf16[128,1024]{1,0:T(8,128)(2,1)S(1)} %get-tuple-element.35), channel_id=1, source_target_pairs={{0,19},{1,16},{2,17},{3,18},{8,27},{9,24},{10,25},{11,26},{16,3},{... | collective-permute-start | bytes 786440 | tf_op jit(solution)/shard_map/ppermute | solution.py:332
  23.7 24.5 %collective-permute-start.7 = (bf16[128,1024]{1,0:T(8,128)(2,1)S(1)}, bf16[128,1024]{1,0:T(8,128)(2,1)S(1)}, u32[]{:S(2)}, u32[]{:S(2)}) collective-permute-start(bf16[128,1024]{1,0:T(8,128)(2,1)S(1)} %get-tuple-element.32), channel_id=1, source_target_pairs={{0,27},{1,24},{2,25},{3,26},{8,3},{9,0},{10,1},{11,2},{16,11},{17,... | collective-permute-start | bytes 786440 | tf_op jit(solution)/shard_map/ppermute | solution.py:332
  48.2 0.7 copy-start.3
  48.2 0.8 copy-start.4
  48.2 0.9 copy-start.5
  48.2 1.0 copy-start.6
  64.8 4.2 %collective-permute-start.8 = (f32[33,9,8,128]{3,2,1,0:T(8,128)}, f32[33,9,8,128]{3,2,1,0:T(8,128)S(1)}, u32[]{:S(2)}, u32[]{:S(2)}) collective-permute-start(f32[33,9,8,128]{3,2,1,0:T(8,128)} %get-tuple-element.28), channel_id=1, source_target_pairs={{0,4},{4,0},{1,5},{5,1},{2,6},{6,2},{3,7},{7,3},{8,12},{12,8},{9,1... | collective-permute-start | bytes 3649544 | tf_op jit(solution)/shard_map/ppermute | solution.py:353
  69.0 1.0 copy-start.1
  70.0 9.8 %copy-start.10 = (bf16[128,1024]{1,0:T(8,128)(2,1)S(1)}, bf16[128,1024]{1,0:T(8,128)(2,1)}, u32[]{:S(2)}) copy-start(bf16[128,1024]{1,0:T(8,128)(2,1)} %get-tuple-element.20) | copy-start | bytes 786436
  70.0 11.3 %copy-start.9 = (bf16[128,1024]{1,0:T(8,128)(2,1)S(1)}, bf16[128,1024]{1,0:T(8,128)(2,1)}, u32[]{:S(2)}) copy-start(bf16[128,1024]{1,0:T(8,128)(2,1)} %get-tuple-element.21) | copy-start | bytes 786436
  70.0 16.2 %copy-start.8 = (bf16[128,1024]{1,0:T(8,128)(2,1)S(1)}, bf16[128,1024]{1,0:T(8,128)(2,1)}, u32[]{:S(2)}) copy-start(bf16[128,1024]{1,0:T(8,128)(2,1)} %get-tuple-element.22) | copy-start | bytes 786436
  70.0 17.5 %copy-start.7 = (bf16[128,1024]{1,0:T(8,128)(2,1)S(1)}, bf16[128,1024]{1,0:T(8,128)(2,1)}, u32[]{:S(2)}) copy-start(bf16[128,1024]{1,0:T(8,128)(2,1)} %get-tuple-element.23) | copy-start | bytes 786436
  72.9 38.7 %all-to-all-start.1 = ((bf16[32,15,8,128]{3,2,1,0:T(8,128)(2,1)}), bf16[32,15,8,128]{3,2,1,0:T(8,128)(2,1)S(1)}, u32[]{:S(2)}, u32[]{:S(2)}) async-start(bf16[32,15,8,128]{3,2,1,0:T(8,128)(2,1)} %join.1), calls=%async_computation.1 | async-start | bytes 1966080 | tf_op jit(solution)/shard_map/all_to_all | solution.py:354
  79.8 10.3 %collective-permute-start = (bf16[128,1024]{1,0:T(8,128)(2,1)S(1)}, bf16[128,1024]{1,0:T(8,128)(2,1)S(1)}, u32[]{:S(2)}, u32[]{:S(2)}) collective-permute-start(bf16[128,1024]{1,0:T(8,128)(2,1)S(1)} %copy-done.10), channel_id=1, source_target_pairs={{0,1},{1,2},{2,3},{3,0},{8,9},{9,10},{10,11},{11,8},{16,17},{17,18... | collective-permute-start | bytes 786440 | tf_op jit(solution)/shard_map/ppermute | solution.py:332
  81.4 18.1 %collective-permute-start.1 = (bf16[128,1024]{1,0:T(8,128)(2,1)S(1)}, bf16[128,1024]{1,0:T(8,128)(2,1)S(1)}, u32[]{:S(2)}, u32[]{:S(2)}) collective-permute-start(bf16[128,1024]{1,0:T(8,128)(2,1)S(1)} %copy-done.9), channel_id=1, source_target_pairs={{0,25},{1,26},{2,27},{3,24},{8,1},{9,2},{10,3},{11,0},{16,9},{17,1... | collective-permute-start | bytes 786440 | tf_op jit(solution)/shard_map/ppermute | solution.py:332
  86.3 16.3 %collective-permute-start.2 = (bf16[128,1024]{1,0:T(8,128)(2,1)S(1)}, bf16[128,1024]{1,0:T(8,128)(2,1)S(1)}, u32[]{:S(2)}, u32[]{:S(2)}) collective-permute-start(bf16[128,1024]{1,0:T(8,128)(2,1)S(1)} %copy-done.8), channel_id=1, source_target_pairs={{0,17},{1,18},{2,19},{3,16},{8,25},{9,26},{10,27},{11,24},{16,1},{... | collective-permute-start | bytes 786440 | tf_op jit(solution)/shard_map/ppermute | solution.py:332
  87.6 24.0 %collective-permute-start.3 = (bf16[128,1024]{1,0:T(8,128)(2,1)S(1)}, bf16[128,1024]{1,0:T(8,128)(2,1)S(1)}, u32[]{:S(2)}, u32[]{:S(2)}) collective-permute-start(bf16[128,1024]{1,0:T(8,128)(2,1)S(1)} %copy-done.7), channel_id=1, source_target_pairs={{0,9},{1,10},{2,11},{3,8},{8,17},{9,18},{10,19},{11,16},{16,25},{1... | collective-permute-start | bytes 786440 | tf_op jit(solution)/shard_map/ppermute | solution.py:332
  111.6 3.2 %copy-start.2 = (bf16[1,128,4096]{2,1,0:T(8,128)(2,1)}, bf16[1,128,4096]{2,1,0:T(8,128)(2,1)S(1)}, u32[]{:S(2)}) copy-start(bf16[1,128,4096]{2,1,0:T(8,128)(2,1)S(1)} %bitcast_dynamic-update-slice_fusion) | copy-start | bytes 3145732
  111.6 1.0 copy-start

commit v2 on v1

v2 whole, which is shorter than its diff:
```python
import functools

import jax
import jax.numpy as jnp
import numpy as np
from jax import lax
from jax.experimental import pallas as pl
from jax.experimental.pallas import tpu as pltpu
from jax.sharding import Mesh, PartitionSpec as P

F32, BF16 = jnp.float32, jnp.bfloat16
LIMITS = (12, 16, 23, 32, 45, 64, 91)
LOG2E = 1.4426950408889634
L = 128
NX = 4
MIB = 1024 * 1024


def bucket_picks():
    c = np.arange(L)
    r = -np.where(c < 64, c, c - L)
    a = np.abs(r)
    b = np.minimum(a, 8) + sum((a >= t).astype(np.int64) for t in LIMITS) + 16 * (r > 0)
    return (np.arange(L)[:, None] == b[None, :]).astype(np.float32)


def dot(a, b, dims, precision=None):
    return lax.dot_general(a, b, (dims, ((), ())), precision=precision, preferred_element_type=F32)


NN, NT, TN = ((1,), (0,)), ((1,), (1,)), ((0,), (0,))


def halves(tile):
    low = lax.broadcasted_iota(jnp.int32, tile.shape, 1) < 64
    zero = jnp.zeros_like(tile)
    return jnp.concatenate([jnp.where(low, tile, zero), jnp.where(low, zero, tile)], axis=0)


def offset_sums(square):
    acc = square[:8]
    for k in range(8, L, 8):
        acc = acc + pltpu.roll(square[k : k + 8], L - k, 1)
    row = lax.broadcasted_iota(jnp.int32, acc.shape, 0)
    for bit in (1, 2, 4):
        acc = jnp.where((row & bit) != 0, pltpu.roll(acc, L - bit, 1), acc)
    return jnp.sum(acc, axis=0, keepdims=True)


def cost(us, mib):
    return pl.CostEstimate(flops=int(us * 1e9), bytes_accessed=int(mib * MIB), transcendentals=0)


def place():
    return lax.axis_index("z"), lax.axis_index("x"), lax.axis_index("c")


def pre_kernel(table_ref, gain_ref, pos_ref, picks_ref, ne_ref, r_ref, bvec_ref):
    width = table_ref.shape[1]
    part = width // NX
    wide = table_ref[...].astype(F32)
    r = lax.rsqrt(jnp.sum(wide * wide, axis=1, keepdims=True) * (1.0 / width) + 1e-06)
    r_ref[...] = jnp.broadcast_to(r, r_ref.shape)
    cols = pl.ds(pl.multiple_of(lax.axis_index("x") * part, L), part)
    own = table_ref[:, cols]
    ne_ref[:, :part] = (own.astype(F32) * r * gain_ref[:, cols]).astype(BF16)
    ne_ref[:, part:] = own

    @pl.when(pl.program_id(0) == 0)
    def _():
        bvec_ref[...] = dot(pos_ref[...], picks_ref[...], TN, lax.Precision.HIGHEST) * LOG2E


def prepare(table, gain, pos, picks):
    vocab, width = table.shape
    part = width // NX
    rows = 128
    heads = pos.shape[1]
    return pl.pallas_call(
        pre_kernel,
        grid=(vocab // rows,),
        in_specs=[
            pl.BlockSpec((rows, width), lambda i: (i, 0)),
            pl.BlockSpec((1, width), lambda i: (0, 0)),
            pl.BlockSpec(pos.shape, lambda i: (0, 0)),
            pl.BlockSpec(picks.shape, lambda i: (0, 0)),
        ],
        out_specs=[
            pl.BlockSpec((rows, 2 * part), lambda i: (i, 0)),
            pl.BlockSpec((rows, L), lambda i: (i, 0)),
            pl.BlockSpec((heads, L), lambda i: (0, 0)),
        ],
        out_shape=[
            jax.ShapeDtypeStruct((vocab, 2 * part), BF16),
            jax.ShapeDtypeStruct((vocab, L), F32),
            jax.ShapeDtypeStruct((heads, L), F32),
        ],
        compiler_params=pltpu.CompilerParams(vmem_limit_bytes=12 * MIB),
        cost_estimate=cost(5, 7),
        name="prepare",
    )(table, gain, pos, picks)


def onehot_t(ids_row, vocab):
    v = lax.broadcasted_iota(jnp.int32, (vocab, ids_row.shape[1]), 0)
    return jnp.where(v == ids_row, 1.0, 0.0).astype(BF16)


def packed(notes_ref, slot, what):
    z, x, c = place()
    chip = z * NX + lax.rem(x + NX - slot, NX)
    order = notes_ref[pl.ds(chip * 2 + c, 1), 2, :]
    values = notes_ref[:, what, :]
    found = lax.broadcasted_iota(jnp.int32, values.shape, 0) == order
    return jnp.sum(jnp.where(found, values, 0), axis=0, keepdims=True)


def fwd_kernel(notes_ref, ne_ref, bvec_ref, *rest):
    a_refs, (n_ref, p_ref), (e_ref, m_ref) = rest[:NX], rest[NX : NX + 2], rest[NX + 2 :]
    vocab, part = ne_ref.shape[0], ne_ref.shape[1] // 2
    pairs = part // L
    first = lax.axis_index("x") * (2 * pairs)
    for s in range(NX):
        both = dot(onehot_t(packed(notes_ref, s, 0), vocab), ne_ref[...], TN)
        n_ref[s] = both[:, :part].astype(BF16)
        e_ref[s] = both[:, part:].astype(BF16)
        seg = jnp.broadcast_to(packed(notes_ref, s, 1), (L, L)).astype(F32)
        m_ref[s] = jnp.where(seg == seg.T, 0.0, -1e30)

    @pl.loop(0, pairs)
    def _(p):
        cols = pl.ds(pl.multiple_of(p * L, L), L)
        biases = [
            pltpu.roll(
                jnp.broadcast_to(bvec_ref[pl.ds(first + 2 * p + k, 1), :], (L, L)),
                0,
                1,
                stride=1,
                stride_axis=0,
            )
            for k in range(2)
        ]
        for s in range(NX):
            tile = n_ref[s, :, cols]
            two = halves(tile)
            mask = m_ref[s]
            raw = dot(two, tile, NT)
            for k in range(2):
                scores = raw[k * L : (k + 1) * L] * (LOG2E / 64.0) + (biases[k] + mask)
                expo = jnp.exp2(scores - jnp.max(scores, axis=0, keepdims=True))
                probs = expo * (1.0 / jnp.sum(expo, axis=0, keepdims=True))
                p_ref[p, s, k * L : (k + 1) * L] = probs.astype(BF16)
            mixed = dot(p_ref[p, s], two, TN)
            a_refs[s][:, cols] = (e_ref[s, :, cols].astype(F32) + mixed).astype(BF16)


def forward(notes, ne, bvec):
    part = ne.shape[1] // 2
    pairs = part // L
    vmem = pl.BlockSpec(memory_space=pltpu.VMEM)
    return pl.pallas_call(
        fwd_kernel,
        in_specs=[vmem] * 3,
        out_specs=[vmem] * (NX + 2),
        out_shape=[jax.ShapeDtypeStruct((L, part), BF16)] * NX
        + [
            jax.ShapeDtypeStruct((NX, L, part), BF16),
            jax.ShapeDtypeStruct((pairs, NX, 2 * L, L), BF16),
        ],
        scratch_shapes=[pltpu.VMEM((NX, L, part), BF16), pltpu.VMEM((NX, L, L), F32)],
        compiler_params=pltpu.CompilerParams(vmem_limit_bytes=18 * MIB),
        cost_estimate=cost(8, 7),
        name="forward",
    )(notes, ne, bvec)


def bwd_kernel(notes_ref, ne_ref, r_ref, gain_ref, picks_ref, n_ref, p_ref, *rest):
    g_refs, (mine_ref, other_ref), (d_ref, rg_ref, o_ref, diag_ref) = rest[:NX], rest[NX : NX + 2], rest[NX + 2 :]
    vocab, part = ne_ref.shape[0], ne_ref.shape[1] // 2
    pairs = part // L
    blocks = vocab // 16
    _, x, core = place()

    @pl.loop(0, pairs)
    def _(p):
        cols = pl.ds(pl.multiple_of(p * L, L), L)
        total = [jnp.zeros((L, L), F32)] * 2
        for s in range(NX):
            tile, up = n_ref[s, :, cols], g_refs[s][:, cols]
            rg_ref[pl.ds(s * L, L), cols] = up
            two, ups = halves(tile), halves(up)
            d_all = dot(two, up, NT)
            small = []
            for k in range(2):
                wide = p_ref[p, s, k * L : (k + 1) * L].astype(F32)
                d_probs = d_all[k * L : (k + 1) * L].astype(BF16).astype(F32)
                d_scores = wide * (d_probs - jnp.sum(wide * d_probs, axis=0, keepdims=True))
                total[k] = total[k] + d_scores
                small.append(d_scores.astype(BF16))
            part64 = two * BF16(1.0 / 64.0)
            left = jnp.concatenate([p_ref[p, s, :L], p_ref[p, s, L:]] + small, axis=1)
            d_norm = dot(left, jnp.concatenate([ups, part64], axis=0), NN)
            d_norm = d_norm + dot(jnp.concatenate(small, axis=0), part64, TN)
            d_ref[pl.ds(s * L, L), cols] = d_norm.astype(BF16)
        for k in range(2):
            diag_ref[pl.ds(2 * p + k, 1), :] = offset_sums(total[k])

    for s in range(NX):
        o_ref[:, s * L : (s + 1) * L] = onehot_t(packed(notes_ref, s, 0), vocab)

    def put(tile, value):
        value = value.reshape(blocks, 2, 8, L)
        first, second = value[:, 0], value[:, 1]
        mine_ref[0:blocks, tile] = jnp.where(core == 0, first, second)
        other_ref[0:blocks, tile] = jnp.where(core == 0, second, first)

    r = r_ref[...]
    along = jnp.zeros((vocab, L), F32)
    for f in range(pairs):
        cols = slice(f * L, (f + 1) * L)
        d_act = dot(o_ref[...], rg_ref[:, cols], NN)
        d_norm = dot(o_ref[...], d_ref[:, cols], NN)
        gain = gain_ref[:, pl.ds(pl.multiple_of(x * part + f * L, L), L)]
        own = ne_ref[:, part + f * L : part + (f + 1) * L].astype(F32)
        scaled = d_norm * r
        put(f, d_act + scaled * gain)
        along = along + own * (d_norm * gain)
        g_row = jnp.sum(own * scaled, axis=0, keepdims=True)
        mine_ref[blocks, 0, pl.ds(f, 1), :] = g_row
        other_ref[blocks, 0, pl.ds(f, 1), :] = g_row
    put(pairs, along)
    sums = dot(diag_ref[...], picks_ref[...], NT, lax.Precision.HIGHEST)
    for ref in (mine_ref, other_ref):
        ref[blocks, 1] = sums[:8]
        ref[blocks, 2] = sums[8:]
        for tile in range(3, pairs + 1):
            ref[blocks, tile] = jnp.zeros((8, L), F32)


def backward(notes, ne, r, gain, picks, n, probs, grads):
    vocab, part = ne.shape[0], ne.shape[1] // 2
    pairs = part // L
    vmem = pl.BlockSpec(memory_space=pltpu.VMEM)
    out = jax.ShapeDtypeStruct((vocab // 16 + 1, pairs + 1, 8, L), F32)
    return pl.pallas_call(
        bwd_kernel,
        in_specs=[vmem] * (7 + NX),
        out_specs=[vmem, vmem],
        out_shape=[out, out],
        scratch_shapes=[
            pltpu.VMEM((NX * L, part), BF16),
            pltpu.VMEM((NX * L, part), BF16),
            pltpu.VMEM((vocab, NX * L), BF16),
            pltpu.VMEM((2 * pairs, L), F32),
        ],
        compiler_params=pltpu.CompilerParams(vmem_limit_bytes=24 * MIB),
        cost_estimate=cost(10, 10),
        name="backward",
    )(notes, ne, r, gain, picks, n, probs, *grads)


def join_kernel(mine_ref, came_ref, out_ref):
    blocks, tiles = mine_ref.shape[0] - 1, mine_ref.shape[1] - 1
    for t in range(tiles):
        out_ref[:, t] = (mine_ref[0:blocks, t] + came_ref[0:blocks, t]).astype(BF16)
    sums = [mine_ref[blocks, t] + came_ref[blocks, t] for t in range(3)]
    out_ref[:, tiles] = jnp.broadcast_to(sums[0].astype(BF16)[None], (blocks, 8, L))
    bias = sums[1] + pltpu.roll(sums[2], 32, 1)
    lane = lax.broadcasted_iota(jnp.int32, (8, L), 1)
    for d in range(blocks):
        along = jnp.sum(mine_ref[d, tiles] + came_ref[d, tiles], axis=1, keepdims=True)
        value = jnp.where(lane == 16, along, bias)
        high = value.astype(BF16).astype(F32)
        out_ref[d, tiles + 1] = (high + pltpu.roll(value - high, 64, 1)).astype(BF16)


def join(mine, came):
    blocks, tiles = mine.shape[0] - 1, mine.shape[1]
    vmem = pl.BlockSpec(memory_space=pltpu.VMEM)
    return pl.pallas_call(
        join_kernel,
        in_specs=[vmem, vmem],
        out_specs=vmem,
        out_shape=jax.ShapeDtypeStruct((blocks, tiles + 1, 8, L), BF16),
        compiler_params=pltpu.CompilerParams(vmem_limit_bytes=8 * MIB),
        cost_estimate=cost(2, 4),
        name="join",
    )(mine, came)


def last_kernel(parts_ref, table_ref, r_ref, t_ref, g_ref, b_ref, h_ref):
    sources, feats = parts_ref.shape[0], parts_ref.shape[1] - 2
    width = table_ref.shape[1]
    z, x_own, c = place()
    lane = lax.broadcasted_iota(jnp.int32, (8, L), 1)

    def total(x, tile):
        value = parts_ref[x, tile].astype(F32)
        for k in range(1, sources // NX):
            value = value + parts_ref[k * NX + x, tile].astype(F32)
        return value

    along = jnp.zeros((8, 1), F32)
    for x in range(NX):
        value = total(x, feats + 1)
        value = value + pltpu.roll(value, 64, 1)
        along = along + jnp.sum(jnp.where(lane == 16, value, 0.0), axis=1, keepdims=True)
        value = jnp.where(lane == 16, 0.0, value)
        h_ref[x * 16 : x * 16 + 8, :] = value
        h_ref[x * 16 + 8 : x * 16 + 16, :] = pltpu.roll(value, L - 32, 1)
    b_ref[0] = h_ref[...].T[:32]
    at = pl.multiple_of(((z * NX + x_own) * 2 + c) * 8, 8)
    r = r_ref[pl.ds(at, 8), :][:, :1]
    factor = along * (r * r * r) * (1.0 / width)
    for x in range(NX):
        gains = total(x, feats)
        for f in range(feats):
            k = (x * feats + f) * L
            t_ref[0, :, k : k + L] = total(x, f) - table_ref[:, k : k + L].astype(F32) * factor
            g_ref[0:1, k : k + L] = gains[f : f + 1]


def finish(parts, table, r):
    width = table.shape[1]
    vmem = pl.BlockSpec(memory_space=pltpu.VMEM)
    return pl.pallas_call(
        last_kernel,
        in_specs=[vmem, vmem, vmem],
        out_specs=[vmem] * 3,
        out_shape=[
            jax.ShapeDtypeStruct((1, 8, width), F32),
            jax.ShapeDtypeStruct((1, width), F32),
            jax.ShapeDtypeStruct((1, 32, 64), F32),
        ],
        scratch_shapes=[pltpu.VMEM((64, L), F32)],
        compiler_params=pltpu.CompilerParams(vmem_limit_bytes=8 * MIB),
        cost_estimate=cost(2, 2),
        name="finish",
    )(parts, table, r)


def local(picks, token_ids, segment_ids, row_order, embed_table, norm_gain, position_bias, returned_grad):
    x, z, c = lax.axis_index("x"), lax.axis_index("z"), lax.axis_index("c")
    table, gain, pos, grad = embed_table[0], norm_gain, position_bias[0], returned_grad[0]
    part = table.shape[1] // NX
    sections = lax.axis_size("section")

    def send(value, steps, along):
        pairs = [
            (i * sections + j, (i + steps) % NX * sections + (j + along) % sections)
            for i in range(NX)
            for j in range(sections)
        ]
        return lax.ppermute(value, ("x", "section"), pairs)

    grads = [
        send(lax.dynamic_slice(grad, (0, lax.rem(x + s, NX) * part), (L, part)), s, -1) for s in range(NX)
    ]

    ne, r, bvec = prepare(table, gain, pos, picks[:32])
    count = 64
    note = jnp.concatenate([token_ids[0], segment_ids[0], jnp.broadcast_to(row_order, (1, L))], axis=0)
    notes = lax.all_to_all(jnp.broadcast_to(note[None], (count, 3, L)), ("z", "x", "c"), 0, 0)

    *acts, normed, probs = forward(notes, ne, bvec)
    pieces = [send(acts[s], -s, 1) for s in range(NX)]
    handed = jnp.zeros((L, NX * part), BF16)
    for s in range(NX):
        handed = lax.dynamic_update_slice(handed, pieces[s], (0, lax.rem(x + s, NX) * part))

    mine, other = backward(notes, ne, r, gain, picks, normed, probs, grads)
    came = lax.ppermute(other, "c", [(0, 1), (1, 0)])
    parts = lax.all_to_all(join(mine, came), ("z", "x"), 0, 0)
    rows = lax.dynamic_slice(table, (((z * NX + x) * 2 + c) * 8, 0), (8, table.shape[1]))
    return (handed[None],) + tuple(finish(parts, rows, r))


def solution(mesh):
    fine = Mesh(mesh.devices.reshape(8, NX, 2, 4), ("z", "x", "c", "section"))
    dp = ("z", "x", "c")
    placed = (
        P(),
        P("section", dp, None),
        P("section", dp, None),
        P("section", dp),
        P("section", None, None),
        P("section", None),
        P("section", None, None),
        P("section", dp, None),
    )
    mapped = jax.shard_map(
        local,
        mesh=fine,
        in_specs=placed,
        out_specs=(
            P("section", dp, None),
            P("section", dp, None),
            P("section", None),
            P("section", None, None),
        ),
        check_vma=False,
    )
    return lambda *args: mapped(jnp.asarray(bucket_picks()), *args)
```

time: 115 us -> 97.3 us (0.85)
  Pallas kernels: 39.5 us -> 22.2 us
  waiting for transfers between devices: 26.1 us -> 20.7 us
  starting transfers between devices: 35.8 us -> 38.5 us
  local copies, waits for them, and re-layouts: 11.1 us -> 13.2 us
    pallas_call x4, Pallas kernels: 36.7 us -> 20.9 us  [the longest x1 10.5 us: backward(): pl.pallas_call(bwd_kernel, in_specs=[vmem] * (7 + NX), out_specs=[vmem, v...]
    unnamed x22 -> x28, local copies, waits for them, and re-layouts: 3.05 us -> 8.26 us
    ppermute x1, waiting for transfers between devices: 2.74 us -> 0.01 us  [local(): came = lax.ppermute(other, 'c', [(0, 1), (1, 0)])]
    ppermute x8, waiting for transfers between devices: 23.4 us -> 20.7 us  [send(): return lax.ppermute(value, ('x', 'section'), pairs)]
    slice x2 -> x0, local copies, waits for them, and re-layouts: 2.42 us -> none  [local(): ids, segs, order = (notes[:, 0], notes[:, 1], notes[:, 2, 0])]
    dynamic_update_slice x4, local copies, waits for them, and re-layouts: 0.09 us -> 1.99 us  [local(): lax.dynamic_update_slice(handed, pieces[s], (0, lax.rem(x + s, NX) * part))]
    dynamic_slice x2 -> x1, local copies, waits for them, and re-layouts: 2.74 us -> 0.85 us  [local(): lax.dynamic_slice(table, (((z * NX + x) * 2 + c) * 8, 0), (8, table.shape...]
    all_to_all x1, starting transfers between devices: 6.89 us -> 8.77 us  [local(): parts = lax.all_to_all(join(mine, came), ('z', 'x'), 0, 0)]
  transfers between devices with their start and end apart: 11 -> 11, of which waited for: 5 -> 4; matrix products, arithmetic and copies ran while one was open for 6% -> 4% of each run, Pallas kernels for 17% -> 11%
where the time goes in v2:
time: 97.3 us; the launch traced here: 96.8 us
  starting transfers between devices  38.5 us (40%)
  Pallas kernels  22.2 us (23%)
  waiting for transfers between devices  20.7 us (21%)
  local copies, waits for them, and re-layouts  13.2 us (14%)
  between operations  1.51 us (2%)
    ppermute x8, waiting for transfers between devices, send(): return lax.ppermute(value, ('x', 'section'), pairs)  20.7 us
    ppermute x8, starting transfers between devices, send(): return lax.ppermute(value, ('x', 'section'), pairs)  15 us
    all_to_all x1, starting transfers between devices, local(): lax.all_to_all(jnp.broadcast_to(note[None], (count, 3, L)), ('z', 'x', 'c...  13 us
    pallas_call x1, Pallas kernels, backward(): pl.pallas_call(bwd_kernel, in_specs=[vmem] * (7 + NX), out_specs=[vmem, v...  10.5 us
    all_to_all x1, starting transfers between devices, local(): parts = lax.all_to_all(join(mine, came), ('z', 'x'), 0, 0)  8.77 us
    unnamed x28, local copies, waits for them, and re-layouts  8.26 us
    pallas_call x1, Pallas kernels, forward(): pl.pallas_call(fwd_kernel, in_specs=[vmem] * 3, out_specs=[vmem] * (NX +...  7.93 us
    dynamic_update_slice x4, local copies, waits for them, and re-layouts, local(): lax.dynamic_update_slice(handed, pieces[s], (0, lax.rem(x + s, NX) * part))  1.99 us
  transfers between devices with their start and end apart: 11, of which 4 were waited for; matrix products, arithmetic and copies ran while one was open for 4% of the time, Pallas kernels for 11%

profile of v2, /device:TPU:1, one launch (start us, length us, event | category | flops | bytes accessed | tf_op | source)
XLA Modules:
  0.0 96.8 jit_solution(7543779029247675164)
XLA Ops:
  1.4 0.7 add_add_fusion
  2.1 0.7 broadcast_in_dim.28
  2.8 13.0 %all-to-all-start = ((s32[64,3,128]{2,1,0:T(4,128)}), s32[64,3,128]{2,1,0:T(4,128)S(1)}, u32[]{:S(2)}, u32[]{:S(2)}) async-start(s32[64,3,128]{2,1,0:T(4,128)} %broadcast_in_dim.28), calls=%async_computation | async-start | bytes 262144 | tf_op jit(solution)/shard_map/all_to_all | solution.py:363
  15.8 1.3 %dynamic-slice_bitcast_fusion = (bf16[128,1024]{1,0:T(8,128)(2,1)S(1)}, bf16[128,1024]{1,0:T(8,128)(2,1)S(1)}, bf16[128,1024]{1,0:T(8,128)(2,1)S(1)}, bf16[128,1024]{1,0:T(8,128)(2,1)S(1)}) fusion(bf16[1,128,4096]{2,1,0:T(8,128)(2,1)} %param.14, s32[]{:T(128)S(6)} %select_n.22, s32[]{:T(128)S(6)} %select_n.20, s32[]{:T(128)S(6)} %select_n.19, s32[]{:T(128)S(6)} %select_n.21), kind=kLoop, calls=%fused_computation.4 | loop fusion | bytes 2097168 | tf_op jit(solution)/shard_map/dynamic_slice | solution.py:357
  17.1 2.8 %collective-permute-start.4 = (bf16[128,1024]{1,0:T(8,128)(2,1)S(1)}, bf16[128,1024]{1,0:T(8,128)(2,1)S(1)}, u32[]{:S(2)}, u32[]{:S(2)}) collective-permute-start(bf16[128,1024]{1,0:T(8,128)(2,1)S(1)} %get-tuple-element.34), channel_id=1, source_target_pairs={{0,3},{1,0},{2,1},{3,2},{8,11},{9,8},{10,9},{11,10},{16,19},{17,16... | collective-permute-start | bytes 786440 | tf_op jit(solution)/shard_map/ppermute | solution.py:354
  19.9 1.6 %collective-permute-start.5 = (bf16[128,1024]{1,0:T(8,128)(2,1)S(1)}, bf16[128,1024]{1,0:T(8,128)(2,1)S(1)}, u32[]{:S(2)}, u32[]{:S(2)}) collective-permute-start(bf16[128,1024]{1,0:T(8,128)(2,1)S(1)} %get-tuple-element.33), channel_id=1, source_target_pairs={{0,11},{1,8},{2,9},{3,10},{8,19},{9,16},{10,17},{11,18},{16,27},{1... | collective-permute-start | bytes 786440 | tf_op jit(solution)/shard_map/ppermute | solution.py:354
  21.5 2.3 %collective-permute-start.6 = (bf16[128,1024]{1,0:T(8,128)(2,1)S(1)}, bf16[128,1024]{1,0:T(8,128)(2,1)S(1)}, u32[]{:S(2)}, u32[]{:S(2)}) collective-permute-start(bf16[128,1024]{1,0:T(8,128)(2,1)S(1)} %get-tuple-element.35), channel_id=1, source_target_pairs={{0,19},{1,16},{2,17},{3,18},{8,27},{9,24},{10,25},{11,26},{16,3},{... | collective-permute-start | bytes 786440 | tf_op jit(solution)/shard_map/ppermute | solution.py:354
  23.8 1.1 %collective-permute-start.7 = (bf16[128,1024]{1,0:T(8,128)(2,1)S(1)}, bf16[128,1024]{1,0:T(8,128)(2,1)S(1)}, u32[]{:S(2)}, u32[]{:S(2)}) collective-permute-start(bf16[128,1024]{1,0:T(8,128)(2,1)S(1)} %get-tuple-element.32), channel_id=1, source_target_pairs={{0,27},{1,24},{2,25},{3,26},{8,3},{9,0},{10,1},{11,2},{16,11},{17,... | collective-permute-start | bytes 786440 | tf_op jit(solution)/shard_map/ppermute | solution.py:354
  24.9 2.2 %copy-done = bf16[1,512,4096]{2,1,0:T(8,128)(2,1)S(1)} copy-done((bf16[1,512,4096]{2,1,0:T(8,128)(2,1)S(1)}, bf16[1,512,4096]{2,1,0:T(8,128)(2,1)}, u32[]{:S(2)}) %copy-start) | copy-done | bytes 4194328
  27.0 1.5 %prepare.1 = (bf16[512,2048]{1,0:T(8,128)(2,1)S(1)}, f32[512,128]{1,0:T(8,128)S(1)}, f32[64,128]{1,0:T(8,128)S(1)}) custom-call(bf16[512,4096]{1,0:T(8,128)(2,1)S(1)} %bitcast.26, f32[1,4096]{1,0:T(1,128)S(1)} %copy-done.3, f32[32,64]{1,0:T(8,128)S(1)} %bitcast.27, f32[32,128]{1,0:T(8,128)S(1)} %copy-done.5), custom_call_target="tpu_custom_call" | custom-call | flops 5000000000 | bytes 7340032 | tf_op jit(solution)/shard_map/prepare/pallas_call | solution.py:79
  28.5 1.3 %copy-done.8 = bf16[512,2048]{1,0:T(8,128)(2,1)} copy-done((bf16[512,2048]{1,0:T(8,128)(2,1)}, bf16[512,2048]{1,0:T(8,128)(2,1)S(1)}, u32[]{:S(2)}) %copy-start.8) | copy-done | bytes 2097176
  29.9 1.7 %copy-done.9 = bf16[512,2048]{1,0:T(8,128)(2,1)S(1)} copy-done((bf16[512,2048]{1,0:T(8,128)(2,1)S(1)}, bf16[512,2048]{1,0:T(8,128)(2,1)}, u32[]{:S(2)}) %copy-start.9) | copy-done | bytes 2097176
  31.6 7.9 %forward.1 = (bf16[128,1024]{1,0:T(8,128)(2,1)S(1)}, bf16[128,1024]{1,0:T(8,128)(2,1)S(1)}, bf16[128,1024]{1,0:T(8,128)(2,1)S(1)}, bf16[128,1024]{1,0:T(8,128)(2...) custom-call(s32[64,3,128]{2,1,0:T(4,128)S(1)} %all-to-all-done.notes_ref, ...), custom_call_target="tpu_custom_call" | custom-call | flops 8000000000 | bytes 7340032 | tf_op jit(solution)/shard_map/forward/pallas_call | solution.py:161
  39.5 0.7 copy-done.1
  40.2 1.6 %collective-permute-done.4.rest_0_ = bf16[128,1024]{1,0:T(8,128)(2,1)S(1)} collective-permute-done((bf16[128,1024]{1,0:T(8,128)(2,1)S(1)}, bf16[128,1024]{1,0:T(8,128)(2,1)S(1)}, u32[]{:S(2)}, u32[]{:S(2)}) %collective-permute-start.4) | collective-permute-done | bytes 262176 | tf_op jit(solution)/shard_map/ppermute | solution.py:354
  41.9 0.4 collective-permute-done.6.rest_2_
  42.3 10.5 %backward.1 = (f32[33,9,8,128]{3,2,1,0:T(8,128)S(1)}, f32[33,9,8,128]{3,2,1,0:T(8,128)S(1)}) custom-call(s32[64,3,128]{2,1,0:T(4,128)S(1)} %all-to-all-done.notes_ref, bf16[512,2048]{1,0:T(8,128)(2,1)S(1)} %copy-done.10, f32[512,128]{1,0:T(8,128)S(1)} %get-tuple-element.24.r_ref, f32[1,4096]{1,0:T(1,128)S(1)} %copy-done.3, f32[128,128]{1,0:T(8,128)S(1)} %copy-done.4, ...), custom_call_target="tpu_custom_call" | custom-call | flops 10000000000 | bytes 10485760 | tf_op jit(solution)/shard_map/backward/pallas_call | solution.py:245
  52.8 1.0 %copy-done.6 = f32[33,9,8,128]{3,2,1,0:T(8,128)} copy-done((f32[33,9,8,128]{3,2,1,0:T(8,128)}, f32[33,9,8,128]{3,2,1,0:T(8,128)S(1)}, u32[]{:S(2)}) %copy-start.6) | copy-done | bytes 1216536
  53.8 1.7 %collective-permute-start.8 = (f32[33,9,8,128]{3,2,1,0:T(8,128)S(1)}, f32[33,9,8,128]{3,2,1,0:T(8,128)S(1)}, u32[]{:S(2)}, u32[]{:S(2)}) collective-permute-start(f32[33,9,8,128]{3,2,1,0:T(8,128)S(1)} %get-tuple-element.28), channel_id=1, source_target_pairs={{0,4},{4,0},{1,5},{5,1},{2,6},{6,2},{3,7},{7,3},{8,12},{12,8},{9,1... | collective-permute-start | bytes 3649544 | tf_op jit(solution)/shard_map/ppermute | solution.py:372
  55.4 0.2 collective-permute-start
  55.6 3.6 %collective-permute-start.1 = (bf16[128,1024]{1,0:T(8,128)(2,1)S(1)}, bf16[128,1024]{1,0:T(8,128)(2,1)}, u32[]{:S(2)}, u32[]{:S(2)}) collective-permute-start(bf16[128,1024]{1,0:T(8,128)(2,1)S(1)} %get-tuple-element.21), channel_id=1, source_target_pairs={{0,25},{1,26},{2,27},{3,24},{8,1},{9,2},{10,3},{11,0},{16,9},{17,1... | collective-permute-start | bytes 786440 | tf_op jit(solution)/shard_map/ppermute | solution.py:354
  59.3 1.3 %copy-done.7 = f32[33,9,8,128]{3,2,1,0:T(8,128)S(1)} copy-done((f32[33,9,8,128]{3,2,1,0:T(8,128)S(1)}, f32[33,9,8,128]{3,2,1,0:T(8,128)}, u32[]{:S(2)}) %copy-start.7) | copy-done | bytes 1216536
  60.5 1.3 %join.1 = bf16[32,10,8,128]{3,2,1,0:T(8,128)(2,1)} custom-call(f32[33,9,8,128]{3,2,1,0:T(8,128)S(1)} %copy-done.7, f32[33,9,8,128]{3,2,1,0:T(8,128)S(1)} %collective-permute-done.8.came_ref), custom_call_target="tpu_custom_call" | custom-call | flops 2000000000 | bytes 4194304 | tf_op jit(solution)/shard_map/join/pallas_call | solution.py:280
  61.8 8.8 %all-to-all-start.1 = ((bf16[32,10,8,128]{3,2,1,0:T(8,128)(2,1)}), bf16[32,10,8,128]{3,2,1,0:T(8,128)(2,1)S(1)}, u32[]{:S(2)}, u32[]{:S(2)}) async-start(bf16[32,10,8,128]{3,2,1,0:T(8,128)(2,1)} %join.1), calls=%async_computation.1 | async-start | bytes 1310720 | tf_op jit(solution)/shard_map/all_to_all | solution.py:373
  70.6 0.9 dynamic-slice_bitcast_fusion.4.table_ref
  71.5 3.2 %collective-permute-start.2 = (bf16[128,1024]{1,0:T(8,128)(2,1)S(1)}, bf16[128,1024]{1,0:T(8,128)(2,1)S(1)}, u32[]{:S(2)}, u32[]{:S(2)}) collective-permute-start(bf16[128,1024]{1,0:T(8,128)(2,1)S(1)} %get-tuple-element.22), channel_id=1, source_target_pairs={{0,17},{1,18},{2,19},{3,16},{8,25},{9,26},{10,27},{11,24},{16,1},{... | collective-permute-start | bytes 786440 | tf_op jit(solution)/shard_map/ppermute | solution.py:354
  74.7 0.3 collective-permute-start.3
  75.1 1.0 %bitcast_dynamic-update-slice_fusion.3 = bf16[1,128,4096]{2,1,0:T(8,128)(2,1)S(1)} fusion(bf16[1,128,4096]{2,1,0:T(8,128)(2,1)S(1)} %broadcast_in_dim.25, s32[]{:T(128)S(6)} %select_n.19, bf16[128,1024]{1,0:T(8,128)(2,1)} %collective-permute-done), kind=kLoop, calls=%fused_computation.3 | loop fusion | bytes 524292 | tf_op jit(solution)/shard_map/dynamic_update_slice | solution.py:369
  76.1 1.0 %bitcast_dynamic-update-slice_fusion.2 = bf16[1,128,4096]{2,1,0:T(8,128)(2,1)S(1)} fusion(bf16[1,128,4096]{2,1,0:T(8,128)(2,1)S(1)} %bitcast_dynamic-update-slice_fusion.3, s32[]{:T(128)S(6)} %select_n.20, bf16[128,1024]{1,0:T(8,128)(2,1)} %collective-permute-done.1), kind=kLoop, calls=%fused_computation.2 | loop fusion | bytes 524292 | tf_op jit(solution)/shard_map/dynamic_update_slice | solution.py:369
  77.1 11.2 %collective-permute-done.2 = bf16[128,1024]{1,0:T(8,128)(2,1)S(1)} collective-permute-done((bf16[128,1024]{1,0:T(8,128)(2,1)S(1)}, bf16[128,1024]{1,0:T(8,128)(2,1)S(1)}, u32[]{:S(2)}, u32[]{:S(2)}) %collective-permute-start.2) | collective-permute-done | bytes 262176 | tf_op jit(solution)/shard_map/ppermute | solution.py:354
  88.3 7.4 %collective-permute-done.3 = bf16[128,1024]{1,0:T(8,128)(2,1)S(1)} collective-permute-done((bf16[128,1024]{1,0:T(8,128)(2,1)S(1)}, bf16[128,1024]{1,0:T(8,128)(2,1)S(1)}, u32[]{:S(2)}, u32[]{:S(2)}) %collective-permute-start.3) | collective-permute-done | bytes 262176 | tf_op jit(solution)/shard_map/ppermute | solution.py:354
  95.8 1.0 %finish.1 = (f32[1,8,4096]{2,1,0:T(8,128)}, f32[1,4096]{1,0:T(1,128)}, f32[1,32,64]{2,1,0:T(8,128)}) custom-call(bf16[32,10,8,128]{3,2,1,0:T(8,128)(2,1)S(1)} %all-to-all-done.1.parts_ref, bf16[8,4096]{1,0:T(8,128)(2,1)S(1)} %dynamic-slice_bitcast_fusion.4.table_ref, f32[512,128]{1,0:T(8,128)S(1)} %copy-done.12), custom_call_target="tpu_custom_call" | custom-call | flops 2000000000 | bytes 2097152 | tf_op jit(solution)/shard_map/finish/pallas_call | solution.py:326
  (33 shorter events, 0.3 us)
Async XLA Ops:
  0.6 24.2 %copy-start.5 = (f32[32,128]{1,0:T(8,128)S(1)}, f32[32,128]{1,0:T(8,128)}, u32[]{:S(2)}) copy-start(f32[32,128]{1,0:T(8,128)} %constant.62.picks_ref) | copy-start | bytes 49156
  0.6 24.2 %copy-start.3 = (f32[1,4096]{1,0:T(1,128)S(1)}, f32[1,4096]{1,0:T(1,128)}, u32[]{:S(2)}) copy-start(f32[1,4096]{1,0:T(1,128)} %gain_ref.3) | copy-start | bytes 49156
  0.7 24.2 %copy-start.2 = (f32[1,32,64]{2,1,0:T(8,128)S(1)}, f32[1,32,64]{2,1,0:T(8,128)}, u32[]{:S(2)}) copy-start(f32[1,32,64]{2,1,0:T(8,128)} %param.13) | copy-start | bytes 24580
  2.8 27.1 %all-to-all-start = ((s32[64,3,128]{2,1,0:T(4,128)}), s32[64,3,128]{2,1,0:T(4,128)S(1)}, u32[]{:S(2)}, u32[]{:S(2)}) async-start(s32[64,3,128]{2,1,0:T(4,128)} %broadcast_in_dim.28), calls=%async_computation | async-start | bytes 262144 | tf_op jit(solution)/shard_map/all_to_all | solution.py:363
  17.1 24.7 %collective-permute-start.4 = (bf16[128,1024]{1,0:T(8,128)(2,1)S(1)}, bf16[128,1024]{1,0:T(8,128)(2,1)S(1)}, u32[]{:S(2)}, u32[]{:S(2)}) collective-permute-start(bf16[128,1024]{1,0:T(8,128)(2,1)S(1)} %get-tuple-element.34), channel_id=1, source_target_pairs={{0,3},{1,0},{2,1},{3,2},{8,11},{9,8},{10,9},{11,10},{16,19},{17,16... | collective-permute-start | bytes 786440 | tf_op jit(solution)/shard_map/ppermute | solution.py:354
  19.9 21.9 %collective-permute-start.5 = (bf16[128,1024]{1,0:T(8,128)(2,1)S(1)}, bf16[128,1024]{1,0:T(8,128)(2,1)S(1)}, u32[]{:S(2)}, u32[]{:S(2)}) collective-permute-start(bf16[128,1024]{1,0:T(8,128)(2,1)S(1)} %get-tuple-element.33), channel_id=1, source_target_pairs={{0,11},{1,8},{2,9},{3,10},{8,19},{9,16},{10,17},{11,18},{16,27},{1... | collective-permute-start | bytes 786440 | tf_op jit(solution)/shard_map/ppermute | solution.py:354
  21.5 20.7 %collective-permute-start.6 = (bf16[128,1024]{1,0:T(8,128)(2,1)S(1)}, bf16[128,1024]{1,0:T(8,128)(2,1)S(1)}, u32[]{:S(2)}, u32[]{:S(2)}) collective-permute-start(bf16[128,1024]{1,0:T(8,128)(2,1)S(1)} %get-tuple-element.35), channel_id=1, source_target_pairs={{0,19},{1,16},{2,17},{3,18},{8,27},{9,24},{10,25},{11,26},{16,3},{... | collective-permute-start | bytes 786440 | tf_op jit(solution)/shard_map/ppermute | solution.py:354
  23.8 18.5 %collective-permute-start.7 = (bf16[128,1024]{1,0:T(8,128)(2,1)S(1)}, bf16[128,1024]{1,0:T(8,128)(2,1)S(1)}, u32[]{:S(2)}, u32[]{:S(2)}) collective-permute-start(bf16[128,1024]{1,0:T(8,128)(2,1)S(1)} %get-tuple-element.32), channel_id=1, source_target_pairs={{0,27},{1,24},{2,25},{3,26},{8,3},{9,0},{10,1},{11,2},{16,11},{17,... | collective-permute-start | bytes 786440 | tf_op jit(solution)/shard_map/ppermute | solution.py:354
  24.9 2.2 %copy-start = (bf16[1,512,4096]{2,1,0:T(8,128)(2,1)S(1)}, bf16[1,512,4096]{2,1,0:T(8,128)(2,1)}, u32[]{:S(2)}) copy-start(bf16[1,512,4096]{2,1,0:T(8,128)(2,1)} %param.11) | copy-start | bytes 12582916
  28.5 1.3 %copy-start.8 = (bf16[512,2048]{1,0:T(8,128)(2,1)}, bf16[512,2048]{1,0:T(8,128)(2,1)S(1)}, u32[]{:S(2)}) copy-start(bf16[512,2048]{1,0:T(8,128)(2,1)S(1)} %get-tuple-element.18.ne_ref) | copy-start | bytes 6291460
  29.9 12.4 %copy-start.11 = (f32[512,128]{1,0:T(8,128)}, f32[512,128]{1,0:T(8,128)S(1)}, u32[]{:S(2)}) copy-start(f32[512,128]{1,0:T(8,128)S(1)} %get-tuple-element.24.r_ref) | copy-start | bytes 786436
  29.9 1.7 %copy-start.9 = (bf16[512,2048]{1,0:T(8,128)(2,1)S(1)}, bf16[512,2048]{1,0:T(8,128)(2,1)}, u32[]{:S(2)}) copy-start(bf16[512,2048]{1,0:T(8,128)(2,1)} %copy-done.8) | copy-start | bytes 6291460
  31.6 10.7 %copy-start.4 = (f32[128,128]{1,0:T(8,128)S(1)}, f32[128,128]{1,0:T(8,128)}, u32[]{:S(2)}) copy-start(f32[128,128]{1,0:T(8,128)} %constant.54.clone.picks_ref) | copy-start | bytes 196612
  31.6 10.7 %copy-start.10 = (bf16[512,2048]{1,0:T(8,128)(2,1)S(1)}, bf16[512,2048]{1,0:T(8,128)(2,1)}, u32[]{:S(2)}) copy-start(bf16[512,2048]{1,0:T(8,128)(2,1)} %copy-done.8) | copy-start | bytes 6291460
  39.5 0.7 copy-start.1
  52.8 1.0 %copy-start.6 = (f32[33,9,8,128]{3,2,1,0:T(8,128)}, f32[33,9,8,128]{3,2,1,0:T(8,128)S(1)}, u32[]{:S(2)}) copy-start(f32[33,9,8,128]{3,2,1,0:T(8,128)S(1)} %get-tuple-element.27.mine_ref) | copy-start | bytes 3649540
  53.8 5.5 %collective-permute-start.8 = (f32[33,9,8,128]{3,2,1,0:T(8,128)S(1)}, f32[33,9,8,128]{3,2,1,0:T(8,128)S(1)}, u32[]{:S(2)}, u32[]{:S(2)}) collective-permute-start(f32[33,9,8,128]{3,2,1,0:T(8,128)S(1)} %get-tuple-element.28), channel_id=1, source_target_pairs={{0,4},{4,0},{1,5},{5,1},{2,6},{6,2},{3,7},{7,3},{8,12},{12,8},{9,1... | collective-permute-start | bytes 3649544 | tf_op jit(solution)/shard_map/ppermute | solution.py:372
  55.4 19.5 %collective-permute-start = (bf16[128,1024]{1,0:T(8,128)(2,1)}, bf16[128,1024]{1,0:T(8,128)(2,1)}, u32[]{:S(2)}, u32[]{:S(2)}) collective-permute-start(bf16[128,1024]{1,0:T(8,128)(2,1)} %copy-done.1), channel_id=1, source_target_pairs={{0,1},{1,2},{2,3},{3,0},{8,9},{9,10},{10,11},{11,8},{16,17},{17,18... | collective-permute-start | bytes 786440 | tf_op jit(solution)/shard_map/ppermute | solution.py:354
  55.6 20.4 %collective-permute-start.1 = (bf16[128,1024]{1,0:T(8,128)(2,1)S(1)}, bf16[128,1024]{1,0:T(8,128)(2,1)}, u32[]{:S(2)}, u32[]{:S(2)}) collective-permute-start(bf16[128,1024]{1,0:T(8,128)(2,1)S(1)} %get-tuple-element.21), channel_id=1, source_target_pairs={{0,25},{1,26},{2,27},{3,24},{8,1},{9,2},{10,3},{11,0},{16,9},{17,1... | collective-permute-start | bytes 786440 | tf_op jit(solution)/shard_map/ppermute | solution.py:354
  59.3 1.3 %copy-start.7 = (f32[33,9,8,128]{3,2,1,0:T(8,128)S(1)}, f32[33,9,8,128]{3,2,1,0:T(8,128)}, u32[]{:S(2)}) copy-start(f32[33,9,8,128]{3,2,1,0:T(8,128)} %copy-done.6) | copy-start | bytes 3649540
  61.8 34.0 %copy-start.12 = (f32[512,128]{1,0:T(8,128)S(1)}, f32[512,128]{1,0:T(8,128)}, u32[]{:S(2)}) copy-start(f32[512,128]{1,0:T(8,128)} %copy-done.11) | copy-start | bytes 786436
  61.8 33.9 %all-to-all-start.1 = ((bf16[32,10,8,128]{3,2,1,0:T(8,128)(2,1)}), bf16[32,10,8,128]{3,2,1,0:T(8,128)(2,1)S(1)}, u32[]{:S(2)}, u32[]{:S(2)}) async-start(bf16[32,10,8,128]{3,2,1,0:T(8,128)(2,1)} %join.1), calls=%async_computation.1 | async-start | bytes 1310720 | tf_op jit(solution)/shard_map/all_to_all | solution.py:373
  71.5 16.8 %collective-permute-start.2 = (bf16[128,1024]{1,0:T(8,128)(2,1)S(1)}, bf16[128,1024]{1,0:T(8,128)(2,1)S(1)}, u32[]{:S(2)}, u32[]{:S(2)}) collective-permute-start(bf16[128,1024]{1,0:T(8,128)(2,1)S(1)} %get-tuple-element.22), channel_id=1, source_target_pairs={{0,17},{1,18},{2,19},{3,16},{8,25},{9,26},{10,27},{11,24},{16,1},{... | collective-permute-start | bytes 786440 | tf_op jit(solution)/shard_map/ppermute | solution.py:354
  74.7 21.1 %collective-permute-start.3 = (bf16[128,1024]{1,0:T(8,128)(2,1)S(1)}, bf16[128,1024]{1,0:T(8,128)(2,1)S(1)}, u32[]{:S(2)}, u32[]{:S(2)}) collective-permute-start(bf16[128,1024]{1,0:T(8,128)(2,1)S(1)} %get-tuple-element.23), channel_id=1, source_target_pairs={{0,9},{1,10},{2,11},{3,8},{8,17},{9,18},{10,19},{11,16},{16,25},{1... | collective-permute-start | bytes 786440 | tf_op jit(solution)/shard_map/ppermute | solution.py:354
  95.8 1.0 %copy-start.13 = (bf16[1,128,4096]{2,1,0:T(8,128)(2,1)}, bf16[1,128,4096]{2,1,0:T(8,128)(2,1)S(1)}, u32[]{:S(2)}) copy-start(bf16[1,128,4096]{2,1,0:T(8,128)(2,1)S(1)} %bitcast_dynamic-update-slice_fusion) | copy-start | bytes 3145732

commit v3 on v2

--- a/solution.py
+++ b/solution.py
@@ -115,17 +115,29 @@
     return jnp.sum(jnp.where(found, values, 0), axis=0, keepdims=True)
 
 
-def fwd_kernel(notes_ref, ne_ref, bvec_ref, *rest):
-    a_refs, (n_ref, p_ref), (e_ref, m_ref) = rest[:NX], rest[NX : NX + 2], rest[NX + 2 :]
+def fwd_kernel(notes_ref, ne_hbm, bvec_hbm, *rest):
+    a_refs, (n_ref, p_ref), (e_ref, m_ref, ne_ref, bvec_ref, sems) = rest[:NX], rest[NX : NX + 2], rest[NX + 2 :]
+    eighth = ne_ref.shape[0] // 8
+    copies = [
+        pltpu.make_async_copy(ne_hbm.at[pl.ds(k * eighth, eighth)], ne_ref.at[pl.ds(k * eighth, eighth)], sems.at[k])
+        for k in range(8)
+    ]
+    copies.append(pltpu.make_async_copy(bvec_hbm, bvec_ref, sems.at[8]))
+    for copy in copies:
+        copy.start()
     vocab, part = ne_ref.shape[0], ne_ref.shape[1] // 2
     pairs = part // L
     first = lax.axis_index("x") * (2 * pairs)
     for s in range(NX):
-        both = dot(onehot_t(packed(notes_ref, s, 0), vocab), ne_ref[...], TN)
+        seg = jnp.broadcast_to(packed(notes_ref, s, 1), (L, L)).astype(F32)
+        m_ref[s] = jnp.where(seg == seg.T, 0.0, -1e30)
+    picked = [onehot_t(packed(notes_ref, s, 0), vocab) for s in range(NX)]
+    for copy in copies:
+        copy.wait()
+    for s in range(NX):
+        both = dot(picked[s], ne_ref[...], TN)
         n_ref[s] = both[:, :part].astype(BF16)
         e_ref[s] = both[:, part:].astype(BF16)
-        seg = jnp.broadcast_to(packed(notes_ref, s, 1), (L, L)).astype(F32)
-        m_ref[s] = jnp.where(seg == seg.T, 0.0, -1e30)
 
     @pl.loop(0, pairs)
     def _(p):
@@ -157,17 +169,23 @@
 def forward(notes, ne, bvec):
     part = ne.shape[1] // 2
     pairs = part // L
-    vmem = pl.BlockSpec(memory_space=pltpu.VMEM)
+    vmem, hbm = pl.BlockSpec(memory_space=pltpu.VMEM), pl.BlockSpec(memory_space=pltpu.HBM)
     return pl.pallas_call(
         fwd_kernel,
-        in_specs=[vmem] * 3,
+        in_specs=[vmem, hbm, hbm],
         out_specs=[vmem] * (NX + 2),
         out_shape=[jax.ShapeDtypeStruct((L, part), BF16)] * NX
         + [
             jax.ShapeDtypeStruct((NX, L, part), BF16),
             jax.ShapeDtypeStruct((pairs, NX, 2 * L, L), BF16),
         ],
-        scratch_shapes=[pltpu.VMEM((NX, L, part), BF16), pltpu.VMEM((NX, L, L), F32)],
+        scratch_shapes=[
+            pltpu.VMEM((NX, L, part), BF16),
+            pltpu.VMEM((NX, L, L), F32),
+            pltpu.VMEM(ne.shape, BF16),
+            pltpu.VMEM(bvec.shape, F32),
+            pltpu.SemaphoreType.DMA((9,)),
+        ],
         compiler_params=pltpu.CompilerParams(vmem_limit_bytes=18 * MIB),
         cost_estimate=cost(8, 7),
         name="forward",
@@ -175,7 +193,8 @@
 
 
 def bwd_kernel(notes_ref, ne_ref, r_ref, gain_ref, picks_ref, n_ref, p_ref, *rest):
-    g_refs, (mine_ref, other_ref), (d_ref, rg_ref, o_ref, diag_ref) = rest[:NX], rest[NX : NX + 2], rest[NX + 2 :]
+    g_refs, (mine_ref, other_ref), rest = rest[:NX], rest[NX : NX + 2], rest[NX + 2 :]
+    d_ref, rg_ref, o_ref, diag_ref = rest
     vocab, part = ne_ref.shape[0], ne_ref.shape[1] // 2
     pairs = part // L
     blocks = vocab // 16
@@ -211,8 +230,8 @@
     def put(tile, value):
         value = value.reshape(blocks, 2, 8, L)
         first, second = value[:, 0], value[:, 1]
-        mine_ref[0:blocks, tile] = jnp.where(core == 0, first, second)
-        other_ref[0:blocks, tile] = jnp.where(core == 0, second, first)
+        mine_ref[tile] = jnp.where(core == 0, first, second)
+        other_ref[tile] = jnp.where(core == 0, second, first)
 
     r = r_ref[...]
     along = jnp.zeros((vocab, L), F32)
@@ -226,22 +245,22 @@
         put(f, d_act + scaled * gain)
         along = along + own * (d_norm * gain)
         g_row = jnp.sum(own * scaled, axis=0, keepdims=True)
-        mine_ref[blocks, 0, pl.ds(f, 1), :] = g_row
-        other_ref[blocks, 0, pl.ds(f, 1), :] = g_row
+        for ref in (mine_ref, other_ref):
+            ref[pairs + 1, 0, pl.ds(f, 1), :] = g_row
     put(pairs, along)
     sums = dot(diag_ref[...], picks_ref[...], NT, lax.Precision.HIGHEST)
     for ref in (mine_ref, other_ref):
-        ref[blocks, 1] = sums[:8]
-        ref[blocks, 2] = sums[8:]
-        for tile in range(3, pairs + 1):
-            ref[blocks, tile] = jnp.zeros((8, L), F32)
+        ref[pairs + 1, 1] = sums[:8]
+        ref[pairs + 1, 2] = sums[8:]
+        ref[pairs + 1, 3:] = jnp.zeros((blocks - 3, 8, L), F32)
 
 
 def backward(notes, ne, r, gain, picks, n, probs, grads):
     vocab, part = ne.shape[0], ne.shape[1] // 2
     pairs = part // L
     vmem = pl.BlockSpec(memory_space=pltpu.VMEM)
-    out = jax.ShapeDtypeStruct((vocab // 16 + 1, pairs + 1, 8, L), F32)
+    stacked = (pairs + 2, vocab // 16, 8, L)
+    out = jax.ShapeDtypeStruct(stacked, F32)
     return pl.pallas_call(
         bwd_kernel,
         in_specs=[vmem] * (7 + NX),
@@ -260,28 +279,28 @@
 
 
 def join_kernel(mine_ref, came_ref, out_ref):
-    blocks, tiles = mine_ref.shape[0] - 1, mine_ref.shape[1] - 1
+    tiles, blocks = mine_ref.shape[0] - 2, mine_ref.shape[1]
     for t in range(tiles):
-        out_ref[:, t] = (mine_ref[0:blocks, t] + came_ref[0:blocks, t]).astype(BF16)
-    sums = [mine_ref[blocks, t] + came_ref[blocks, t] for t in range(3)]
+        out_ref[:, t] = (mine_ref[t] + came_ref[t]).astype(BF16)
+    sums = [mine_ref[tiles + 1, t] + came_ref[tiles + 1, t] for t in range(3)]
     out_ref[:, tiles] = jnp.broadcast_to(sums[0].astype(BF16)[None], (blocks, 8, L))
     bias = sums[1] + pltpu.roll(sums[2], 32, 1)
     lane = lax.broadcasted_iota(jnp.int32, (8, L), 1)
     for d in range(blocks):
-        along = jnp.sum(mine_ref[d, tiles] + came_ref[d, tiles], axis=1, keepdims=True)
+        along = jnp.sum(mine_ref[tiles, d] + came_ref[tiles, d], axis=1, keepdims=True)
         value = jnp.where(lane == 16, along, bias)
         high = value.astype(BF16).astype(F32)
         out_ref[d, tiles + 1] = (high + pltpu.roll(value - high, 64, 1)).astype(BF16)
 
 
 def join(mine, came):
-    blocks, tiles = mine.shape[0] - 1, mine.shape[1]
+    tiles, blocks = mine.shape[:2]
     vmem = pl.BlockSpec(memory_space=pltpu.VMEM)
     return pl.pallas_call(
         join_kernel,
         in_specs=[vmem, vmem],
         out_specs=vmem,
-        out_shape=jax.ShapeDtypeStruct((blocks, tiles + 1, 8, L), BF16),
+        out_shape=jax.ShapeDtypeStruct((blocks, tiles, 8, L), BF16),
         compiler_params=pltpu.CompilerParams(vmem_limit_bytes=8 * MIB),
         cost_estimate=cost(2, 4),
         name="join",
@@ -357,19 +376,20 @@
         send(lax.dynamic_slice(grad, (0, lax.rem(x + s, NX) * part), (L, part)), s, -1) for s in range(NX)
     ]
 
-    ne, r, bvec = prepare(table, gain, pos, picks[:32])
+    table_then, grads[2] = lax.optimization_barrier((table, grads[2]))
+    ne, r, bvec = prepare(table_then, gain, pos, picks[:32])
     count = 64
-    note = jnp.concatenate([token_ids[0], segment_ids[0], jnp.broadcast_to(row_order, (1, L))], axis=0)
-    notes = lax.all_to_all(jnp.broadcast_to(note[None], (count, 3, L)), ("z", "x", "c"), 0, 0)
+    note = [jnp.broadcast_to(v.reshape(1, 1, -1), (count, 1, L)) for v in (token_ids, segment_ids, row_order)]
+    notes = lax.all_to_all(jnp.concatenate(note, axis=1), ("z", "x", "c"), 0, 0)
 
     *acts, normed, probs = forward(notes, ne, bvec)
-    pieces = [send(acts[s], -s, 1) for s in range(NX)]
-    handed = jnp.zeros((L, NX * part), BF16)
-    for s in range(NX):
-        handed = lax.dynamic_update_slice(handed, pieces[s], (0, lax.rem(x + s, NX) * part))
-
+    pieces = {s: send(acts[s], -s, 1) for s in (2, 1, 3, 0)}
     mine, other = backward(notes, ne, r, gain, picks, normed, probs, grads)
     came = lax.ppermute(other, "c", [(0, 1), (1, 0)])
+    handed = jnp.zeros((L, NX * part), BF16)
+    for s in (2, 1, 3, 0):
+        handed = lax.dynamic_update_slice(handed, pieces[s], (0, lax.rem(x + s, NX) * part))
+
     parts = lax.all_to_all(join(mine, came), ("z", "x"), 0, 0)
     rows = lax.dynamic_slice(table, (((z * NX + x) * 2 + c) * 8, 0), (8, table.shape[1]))
     return (handed[None],) + tuple(finish(parts, rows, r))

time: 97.3 us -> 87.9 us (0.903)
  starting transfers between devices: 38.5 us -> 33.2 us
  waiting for transfers between devices: 20.7 us -> 15.9 us
    ppermute x8, waiting for transfers between devices: 20.7 us -> 11.3 us  [send(): return lax.ppermute(value, ('x', 'section'), pairs)]
    all_to_all x1, waiting for transfers between devices: 0.01 us -> 3.01 us  [local(): notes = lax.all_to_all(jnp.concatenate(note, axis=1), ('z', 'x', 'c'), 0, 0)]
    all_to_all x1, starting transfers between devices: 13 us -> 10.6 us  [local(): notes = lax.all_to_all(jnp.concatenate(note, axis=1), ('z', 'x', 'c'), 0, 0)]
    all_to_all x1, waiting for transfers between devices: 0.01 us -> 1.29 us  [local(): parts = lax.all_to_all(join(mine, came), ('z', 'x'), 0, 0)]
    ppermute x1, starting transfers between devices: 1.65 us -> 0.41 us  [local(): came = lax.ppermute(other, 'c', [(0, 1), (1, 0)])]
    all_to_all x1, starting transfers between devices: 8.77 us -> 7.7 us  [local(): parts = lax.all_to_all(join(mine, came), ('z', 'x'), 0, 0)]
    unnamed x28 -> x32, local copies, waits for them, and re-layouts: 8.26 us -> 8.25 us
  transfers between devices with their start and end apart: 11 -> 11, of which waited for: 4 -> 5; matrix products, arithmetic and copies ran while one was open for 4% -> 4% of each run, Pallas kernels for 11% -> 13%
where the time goes in v3:
time: 87.9 us; the launch traced here: 86.5 us
  starting transfers between devices  33.2 us (38%)
  Pallas kernels  22.6 us (26%)
  waiting for transfers between devices  15.9 us (18%)
  local copies, waits for them, and re-layouts  12.6 us (14%)
  between operations  1.55 us (2%)
    ppermute x8, starting transfers between devices, send(): return lax.ppermute(value, ('x', 'section'), pairs)  14.5 us
    ppermute x8, waiting for transfers between devices, send(): return lax.ppermute(value, ('x', 'section'), pairs)  11.3 us
    all_to_all x1, starting transfers between devices, local(): notes = lax.all_to_all(jnp.concatenate(note, axis=1), ('z', 'x', 'c'), 0, 0)  10.6 us
    pallas_call x1, Pallas kernels, backward(): pl.pallas_call(bwd_kernel, in_specs=[vmem] * (7 + NX), out_specs=[vmem, v...  10.4 us
    pallas_call x1, Pallas kernels, forward(): pl.pallas_call(fwd_kernel, in_specs=[vmem, hbm, hbm], out_specs=[vmem] *...  8.49 us
    unnamed x32, local copies, waits for them, and re-layouts  8.25 us
    all_to_all x1, starting transfers between devices, local(): parts = lax.all_to_all(join(mine, came), ('z', 'x'), 0, 0)  7.7 us
    all_to_all x1, waiting for transfers between devices, local(): notes = lax.all_to_all(jnp.concatenate(note, axis=1), ('z', 'x', 'c'), 0, 0)  3.01 us
  transfers between devices with their start and end apart: 11, of which 5 were waited for; matrix products, arithmetic and copies ran while one was open for 4% of the time, Pallas kernels for 13%

profile of v3, /device:TPU:1, one launch (start us, length us, event | category | flops | bytes accessed | tf_op | source)
XLA Modules:
  0.0 86.5 jit_solution(873881117891626977)
XLA Ops:
  0.7 1.3 %dynamic-slice_bitcast_fusion = (bf16[128,1024]{1,0:T(8,128)(2,1)S(1)}, bf16[128,1024]{1,0:T(8,128)(2,1)S(1)}, bf16[128,1024]{1,0:T(8,128)(2,1)S(1)}, bf16[128,1024]{1,0:T(8,128)(2,1)S(1)}) fusion(bf16[1,128,4096]{2,1,0:T(8,128)(2,1)} %param.14, s32[]{:T(128)S(6)} %select_n.21, s32[]{:T(128)S(6)} %select_n.22, s32[]{:T(128)S(6)} %select_n.19, s32[]{:T(128)S(6)} %select_n.20), kind=kLoop, calls=%fused_computation.4 | loop fusion | bytes 2097168 | tf_op jit(solution)/shard_map/dynamic_slice | solution.py:376
  2.0 6.1 %collective-permute-start = (bf16[128,1024]{1,0:T(8,128)(2,1)S(1)}, bf16[128,1024]{1,0:T(8,128)(2,1)S(1)}, u32[]{:S(2)}, u32[]{:S(2)}) collective-permute-start(bf16[128,1024]{1,0:T(8,128)(2,1)S(1)} %get-tuple-element.38), channel_id=1, source_target_pairs={{0,19},{1,16},{2,17},{3,18},{8,27},{9,24},{10,25},{11,26},{16,3},{... | collective-permute-start | bytes 786440 | tf_op jit(solution)/shard_map/ppermute | solution.py:373
  8.9 0.7 add_add_fusion
  9.6 10.6 %all-to-all-start = ((s32[64,3,128]{2,1,0:T(4,128)}), s32[64,3,128]{2,1,0:T(4,128)S(1)}, u32[]{:S(2)}, u32[]{:S(2)}) async-start(s32[64,3,128]{2,1,0:T(4,128)} %add_add_fusion), calls=%async_computation | async-start | bytes 262144 | tf_op jit(solution)/shard_map/all_to_all | solution.py:383
  20.2 0.5 collective-permute-start.5
  20.7 1.3 %collective-permute-start.6 = (bf16[128,1024]{1,0:T(8,128)(2,1)S(1)}, bf16[128,1024]{1,0:T(8,128)(2,1)S(1)}, u32[]{:S(2)}, u32[]{:S(2)}) collective-permute-start(bf16[128,1024]{1,0:T(8,128)(2,1)S(1)} %get-tuple-element.39), channel_id=1, source_target_pairs={{0,11},{1,8},{2,9},{3,10},{8,19},{9,16},{10,17},{11,18},{16,27},{1... | collective-permute-start | bytes 786440 | tf_op jit(solution)/shard_map/ppermute | solution.py:373
  22.0 1.2 %collective-permute-start.7 = (bf16[128,1024]{1,0:T(8,128)(2,1)S(1)}, bf16[128,1024]{1,0:T(8,128)(2,1)S(1)}, u32[]{:S(2)}, u32[]{:S(2)}) collective-permute-start(bf16[128,1024]{1,0:T(8,128)(2,1)S(1)} %get-tuple-element.36), channel_id=1, source_target_pairs={{0,27},{1,24},{2,25},{3,26},{8,3},{9,0},{10,1},{11,2},{16,11},{17,... | collective-permute-start | bytes 786440 | tf_op jit(solution)/shard_map/ppermute | solution.py:373
  23.2 2.2 %copy-done = bf16[1,512,4096]{2,1,0:T(8,128)(2,1)S(1)} copy-done((bf16[1,512,4096]{2,1,0:T(8,128)(2,1)S(1)}, bf16[1,512,4096]{2,1,0:T(8,128)(2,1)}, u32[]{:S(2)}) %copy-start) | copy-done | bytes 4194328
  25.4 1.5 %prepare.1 = (bf16[512,2048]{1,0:T(8,128)(2,1)S(1)}, f32[512,128]{1,0:T(8,128)S(1)}, f32[64,128]{1,0:T(8,128)S(1)}) custom-call(bf16[512,4096]{1,0:T(8,128)(2,1)S(1)} %bitcast.26, f32[1,4096]{1,0:T(1,128)S(1)} %copy-done.3, f32[32,64]{1,0:T(8,128)S(1)} %bitcast.27, f32[32,128]{1,0:T(8,128)S(1)} %copy-done.5), custom_call_target="tpu_custom_call" | custom-call | flops 5000000000 | bytes 7340032 | tf_op jit(solution)/shard_map/prepare/pallas_call | solution.py:79
  26.9 1.3 %copy-done.8 = bf16[512,2048]{1,0:T(8,128)(2,1)} copy-done((bf16[512,2048]{1,0:T(8,128)(2,1)}, bf16[512,2048]{1,0:T(8,128)(2,1)S(1)}, u32[]{:S(2)}) %copy-start.8) | copy-done | bytes 2097176
  28.3 3.0 %all-to-all-done.notes_ref = s32[64,3,128]{2,1,0:T(4,128)S(1)} async-done(((s32[64,3,128]{2,1,0:T(4,128)}), s32[64,3,128]{2,1,0:T(4,128)S(1)}, u32[]{:S(2)}, u32[]{:S(2)}) %all-to-all-start) | async-done | bytes 98336 | tf_op jit(solution)/shard_map/all_to_all | solution.py:383
  31.3 1.6 %copy-done.9 = bf16[512,2048]{1,0:T(8,128)(2,1)S(1)} copy-done((bf16[512,2048]{1,0:T(8,128)(2,1)S(1)}, bf16[512,2048]{1,0:T(8,128)(2,1)}, u32[]{:S(2)}) %copy-start.9) | copy-done | bytes 2097176
  32.9 8.5 %forward.1 = (bf16[128,1024]{1,0:T(8,128)(2,1)S(1)}, bf16[128,1024]{1,0:T(8,128)(2,1)S(1)}, bf16[128,1024]{1,0:T(8,128)(2,1)S(1)}, bf16[128,1024]{1,0:T(8,128)(2...) custom-call(s32[64,3,128]{2,1,0:T(4,128)S(1)} %all-to-all-done.notes_ref, ...), custom_call_target="tpu_custom_call" | custom-call | flops 8000000000 | bytes 7340032 | tf_op jit(solution)/shard_map/forward/pallas_call | solution.py:173
  41.4 0.7 copy-done.1
  42.1 10.4 %backward.1 = (f32[10,32,8,128]{3,2,1,0:T(8,128)S(1)}, f32[10,32,8,128]{3,2,1,0:T(8,128)S(1)}) custom-call(s32[64,3,128]{2,1,0:T(4,128)S(1)} %all-to-all-done.notes_ref, bf16[512,2048]{1,0:T(8,128)(2,1)S(1)} %copy-done.10, f32[512,128]{1,0:T(8,128)S(1)} %get-tuple-element.27.r_ref, f32[1,4096]{1,0:T(1,128)S(1)} %copy-done.3, f32[128,128]{1,0:T(8,128)S(1)} %copy-done.4, ...), custom_call_target="tpu_custom_call" | custom-call | flops 10000000000 | bytes 10485760 | tf_op jit(solution)/shard_map/backward/pallas_call | solution.py:264
  52.6 1.1 %copy-done.6 = f32[10,32,8,128]{3,2,1,0:T(8,128)} copy-done((f32[10,32,8,128]{3,2,1,0:T(8,128)}, f32[10,32,8,128]{3,2,1,0:T(8,128)S(1)}, u32[]{:S(2)}) %copy-start.6) | copy-done | bytes 1310744
  53.6 0.4 collective-permute-start.8
  54.0 0.5 collective-permute-start.1
  54.6 1.9 %collective-permute-start.2 = (bf16[128,1024]{1,0:T(8,128)(2,1)S(1)}, bf16[128,1024]{1,0:T(8,128)(2,1)}, u32[]{:S(2)}, u32[]{:S(2)}) collective-permute-start(bf16[128,1024]{1,0:T(8,128)(2,1)S(1)} %get-tuple-element.24), channel_id=1, source_target_pairs={{0,25},{1,26},{2,27},{3,24},{8,1},{9,2},{10,3},{11,0},{16,9},{17,1... | collective-permute-start | bytes 786440 | tf_op jit(solution)/shard_map/ppermute | solution.py:373
  56.5 0.2 collective-permute-done.8.came_ref
  56.7 1.3 %copy-done.7 = f32[10,32,8,128]{3,2,1,0:T(8,128)S(1)} copy-done((f32[10,32,8,128]{3,2,1,0:T(8,128)S(1)}, f32[10,32,8,128]{3,2,1,0:T(8,128)}, u32[]{:S(2)}) %copy-start.7) | copy-done | bytes 1310744
  58.0 1.3 %join.1 = bf16[32,10,8,128]{3,2,1,0:T(8,128)(2,1)} custom-call(f32[10,32,8,128]{3,2,1,0:T(8,128)S(1)} %copy-done.7, f32[10,32,8,128]{3,2,1,0:T(8,128)S(1)} %collective-permute-done.8.came_ref), custom_call_target="tpu_custom_call" | custom-call | flops 2000000000 | bytes 4194304 | tf_op jit(solution)/shard_map/join/pallas_call | solution.py:299
  59.3 7.7 %all-to-all-start.1 = ((bf16[32,10,8,128]{3,2,1,0:T(8,128)(2,1)}), bf16[32,10,8,128]{3,2,1,0:T(8,128)(2,1)S(1)}, u32[]{:S(2)}, u32[]{:S(2)}) async-start(bf16[32,10,8,128]{3,2,1,0:T(8,128)(2,1)} %join.1), calls=%async_computation.1 | async-start | bytes 1310720 | tf_op jit(solution)/shard_map/all_to_all | solution.py:393
  67.0 0.9 dynamic-slice_bitcast_fusion.4.table_ref
  67.8 2.0 %collective-permute-start.3 = (bf16[128,1024]{1,0:T(8,128)(2,1)S(1)}, bf16[128,1024]{1,0:T(8,128)(2,1)S(1)}, u32[]{:S(2)}, u32[]{:S(2)}) collective-permute-start(bf16[128,1024]{1,0:T(8,128)(2,1)S(1)} %get-tuple-element.25), channel_id=1, source_target_pairs={{0,9},{1,10},{2,11},{3,8},{8,17},{9,18},{10,19},{11,16},{16,25},{1... | collective-permute-start | bytes 786440 | tf_op jit(solution)/shard_map/ppermute | solution.py:373
  69.8 1.0 %collective-permute-start.4 = (bf16[128,1024]{1,0:T(8,128)(2,1)S(1)}, bf16[128,1024]{1,0:T(8,128)(2,1)S(1)}, u32[]{:S(2)}, u32[]{:S(2)}) collective-permute-start(bf16[128,1024]{1,0:T(8,128)(2,1)S(1)} %get-tuple-element.26), channel_id=1, source_target_pairs={{0,1},{1,2},{2,3},{3,0},{8,9},{9,10},{10,11},{11,8},{16,17},{17,18... | collective-permute-start | bytes 786440 | tf_op jit(solution)/shard_map/ppermute | solution.py:373
  70.9 1.0 %bitcast_dynamic-update-slice_fusion.3 = bf16[1,128,4096]{2,1,0:T(8,128)(2,1)S(1)} fusion(bf16[1,128,4096]{2,1,0:T(8,128)(2,1)S(1)} %broadcast_in_dim.33, s32[]{:T(128)S(6)} %select_n.19, bf16[128,1024]{1,0:T(8,128)(2,1)} %collective-permute-done.1), kind=kLoop, calls=%fused_computation.3 | loop fusion | bytes 524292 | tf_op jit(solution)/shard_map/dynamic_update_slice | solution.py:391
  71.9 1.0 %bitcast_dynamic-update-slice_fusion.2 = bf16[1,128,4096]{2,1,0:T(8,128)(2,1)S(1)} fusion(bf16[1,128,4096]{2,1,0:T(8,128)(2,1)S(1)} %bitcast_dynamic-update-slice_fusion.3, s32[]{:T(128)S(6)} %select_n.20, bf16[128,1024]{1,0:T(8,128)(2,1)} %collective-permute-done.2), kind=kLoop, calls=%fused_computation.2 | loop fusion | bytes 524292 | tf_op jit(solution)/shard_map/dynamic_update_slice | solution.py:391
  72.9 10.0 %collective-permute-done.3 = bf16[128,1024]{1,0:T(8,128)(2,1)S(1)} collective-permute-done((bf16[128,1024]{1,0:T(8,128)(2,1)S(1)}, bf16[128,1024]{1,0:T(8,128)(2,1)S(1)}, u32[]{:S(2)}, u32[]{:S(2)}) %collective-permute-start.3) | collective-permute-done | bytes 262176 | tf_op jit(solution)/shard_map/ppermute | solution.py:373
  82.9 1.3 %collective-permute-done.4 = bf16[128,1024]{1,0:T(8,128)(2,1)S(1)} collective-permute-done((bf16[128,1024]{1,0:T(8,128)(2,1)S(1)}, bf16[128,1024]{1,0:T(8,128)(2,1)S(1)}, u32[]{:S(2)}, u32[]{:S(2)}) %collective-permute-start.4) | collective-permute-done | bytes 262176 | tf_op jit(solution)/shard_map/ppermute | solution.py:373
  84.3 1.3 %all-to-all-done.1.parts_ref = bf16[32,10,8,128]{3,2,1,0:T(8,128)(2,1)S(1)} async-done(((bf16[32,10,8,128]{3,2,1,0:T(8,128)(2,1)}), bf16[32,10,8,128]{3,2,1,0:T(8,128)(2,1)S(1)}, u32[]{:S(2)}, u32[]{:S(2)}) %all-to-all-start.1) | async-done | bytes 655392 | tf_op jit(solution)/shard_map/all_to_all | solution.py:393
  85.6 0.9 %finish.1 = (f32[1,8,4096]{2,1,0:T(8,128)}, f32[1,4096]{1,0:T(1,128)}, f32[1,32,64]{2,1,0:T(8,128)}) custom-call(bf16[32,10,8,128]{3,2,1,0:T(8,128)(2,1)S(1)} %all-to-all-done.1.parts_ref, bf16[8,4096]{1,0:T(8,128)(2,1)S(1)} %dynamic-slice_bitcast_fusion.4.table_ref, f32[512,128]{1,0:T(8,128)S(1)} %copy-done.12), custom_call_target="tpu_custom_call" | custom-call | flops 2000000000 | bytes 2097152 | tf_op jit(solution)/shard_map/finish/pallas_call | solution.py:345
  (38 shorter events, 0.3 us)
Async XLA Ops:
  0.6 22.6 %copy-start.5 = (f32[32,128]{1,0:T(8,128)S(1)}, f32[32,128]{1,0:T(8,128)}, u32[]{:S(2)}) copy-start(f32[32,128]{1,0:T(8,128)} %constant.62.picks_ref) | copy-start | bytes 49156
  0.6 8.2 %copy-start.14 = (s32[1,1,128]{2,1,0:T(1,128)S(1)}, s32[1,1,128]{2,1,0:T(1,128)}, u32[]{:S(2)}) copy-start(s32[1,1,128]{2,1,0:T(1,128)} %param.9) | copy-start | bytes 1540
  0.7 8.2 %copy-start.15 = (s32[1,1,128]{2,1,0:T(1,128)S(1)}, s32[1,1,128]{2,1,0:T(1,128)}, u32[]{:S(2)}) copy-start(s32[1,1,128]{2,1,0:T(1,128)} %param.8) | copy-start | bytes 1540
  0.7 22.6 %copy-start.3 = (f32[1,4096]{1,0:T(1,128)S(1)}, f32[1,4096]{1,0:T(1,128)}, u32[]{:S(2)}) copy-start(f32[1,4096]{1,0:T(1,128)} %gain_ref.3) | copy-start | bytes 49156
  0.7 22.6 %copy-start.2 = (f32[1,32,64]{2,1,0:T(8,128)S(1)}, f32[1,32,64]{2,1,0:T(8,128)}, u32[]{:S(2)}) copy-start(f32[1,32,64]{2,1,0:T(8,128)} %param.13) | copy-start | bytes 24580
  2.0 21.2 %collective-permute-start = (bf16[128,1024]{1,0:T(8,128)(2,1)S(1)}, bf16[128,1024]{1,0:T(8,128)(2,1)S(1)}, u32[]{:S(2)}, u32[]{:S(2)}) collective-permute-start(bf16[128,1024]{1,0:T(8,128)(2,1)S(1)} %get-tuple-element.38), channel_id=1, source_target_pairs={{0,19},{1,16},{2,17},{3,18},{8,27},{9,24},{10,25},{11,26},{16,3},{... | collective-permute-start | bytes 786440 | tf_op jit(solution)/shard_map/ppermute | solution.py:373
  9.6 21.7 %all-to-all-start = ((s32[64,3,128]{2,1,0:T(4,128)}), s32[64,3,128]{2,1,0:T(4,128)S(1)}, u32[]{:S(2)}, u32[]{:S(2)}) async-start(s32[64,3,128]{2,1,0:T(4,128)} %add_add_fusion), calls=%async_computation | async-start | bytes 262144 | tf_op jit(solution)/shard_map/all_to_all | solution.py:383
  20.2 21.9 %collective-permute-start.5 = (bf16[128,1024]{1,0:T(8,128)(2,1)S(1)}, bf16[128,1024]{1,0:T(8,128)(2,1)S(1)}, u32[]{:S(2)}, u32[]{:S(2)}) collective-permute-start(bf16[128,1024]{1,0:T(8,128)(2,1)S(1)} %get-tuple-element.37), channel_id=1, source_target_pairs={{0,3},{1,0},{2,1},{3,2},{8,11},{9,8},{10,9},{11,10},{16,19},{17,16... | collective-permute-start | bytes 786440 | tf_op jit(solution)/shard_map/ppermute | solution.py:373
  20.7 21.4 %collective-permute-start.6 = (bf16[128,1024]{1,0:T(8,128)(2,1)S(1)}, bf16[128,1024]{1,0:T(8,128)(2,1)S(1)}, u32[]{:S(2)}, u32[]{:S(2)}) collective-permute-start(bf16[128,1024]{1,0:T(8,128)(2,1)S(1)} %get-tuple-element.39), channel_id=1, source_target_pairs={{0,11},{1,8},{2,9},{3,10},{8,19},{9,16},{10,17},{11,18},{16,27},{1... | collective-permute-start | bytes 786440 | tf_op jit(solution)/shard_map/ppermute | solution.py:373
  22.0 20.1 %collective-permute-start.7 = (bf16[128,1024]{1,0:T(8,128)(2,1)S(1)}, bf16[128,1024]{1,0:T(8,128)(2,1)S(1)}, u32[]{:S(2)}, u32[]{:S(2)}) collective-permute-start(bf16[128,1024]{1,0:T(8,128)(2,1)S(1)} %get-tuple-element.36), channel_id=1, source_target_pairs={{0,27},{1,24},{2,25},{3,26},{8,3},{9,0},{10,1},{11,2},{16,11},{17,... | collective-permute-start | bytes 786440 | tf_op jit(solution)/shard_map/ppermute | solution.py:373
  23.2 2.2 %copy-start = (bf16[1,512,4096]{2,1,0:T(8,128)(2,1)S(1)}, bf16[1,512,4096]{2,1,0:T(8,128)(2,1)}, u32[]{:S(2)}) copy-start(bf16[1,512,4096]{2,1,0:T(8,128)(2,1)} %param.11) | copy-start | bytes 12582916
  26.9 1.4 %copy-start.8 = (bf16[512,2048]{1,0:T(8,128)(2,1)}, bf16[512,2048]{1,0:T(8,128)(2,1)S(1)}, u32[]{:S(2)}) copy-start(bf16[512,2048]{1,0:T(8,128)(2,1)S(1)} %get-tuple-element.21.ne_hbm.ne_ref) | copy-start | bytes 6291460
  28.3 13.8 %copy-start.11 = (f32[512,128]{1,0:T(8,128)}, f32[512,128]{1,0:T(8,128)S(1)}, u32[]{:S(2)}) copy-start(f32[512,128]{1,0:T(8,128)S(1)} %get-tuple-element.27.r_ref) | copy-start | bytes 786436
  31.3 1.6 %copy-start.9 = (bf16[512,2048]{1,0:T(8,128)(2,1)S(1)}, bf16[512,2048]{1,0:T(8,128)(2,1)}, u32[]{:S(2)}) copy-start(bf16[512,2048]{1,0:T(8,128)(2,1)} %copy-done.8) | copy-start | bytes 6291460
  32.9 9.2 %copy-start.4 = (f32[128,128]{1,0:T(8,128)S(1)}, f32[128,128]{1,0:T(8,128)}, u32[]{:S(2)}) copy-start(f32[128,128]{1,0:T(8,128)} %constant.54.clone.picks_ref) | copy-start | bytes 196612
  32.9 9.2 %copy-start.10 = (bf16[512,2048]{1,0:T(8,128)(2,1)S(1)}, bf16[512,2048]{1,0:T(8,128)(2,1)}, u32[]{:S(2)}) copy-start(bf16[512,2048]{1,0:T(8,128)(2,1)} %copy-done.8) | copy-start | bytes 6291460
  41.4 0.7 copy-start.1
  52.6 1.1 %copy-start.6 = (f32[10,32,8,128]{3,2,1,0:T(8,128)}, f32[10,32,8,128]{3,2,1,0:T(8,128)S(1)}, u32[]{:S(2)}) copy-start(f32[10,32,8,128]{3,2,1,0:T(8,128)S(1)} %get-tuple-element.31.mine_ref) | copy-start | bytes 3932164
  53.6 3.1 %collective-permute-start.8 = (f32[10,32,8,128]{3,2,1,0:T(8,128)S(1)}, f32[10,32,8,128]{3,2,1,0:T(8,128)S(1)}, u32[]{:S(2)}, u32[]{:S(2)}) collective-permute-start(f32[10,32,8,128]{3,2,1,0:T(8,128)S(1)} %get-tuple-element.32), channel_id=1, source_target_pairs={{0,4},{4,0},{1,5},{5,1},{2,6},{6,2},{3,7},{7,3},{8,12},{12,8},{9,1... | collective-permute-start | bytes 3932168 | tf_op jit(solution)/shard_map/ppermute | solution.py:388
  54.0 16.8 %collective-permute-start.1 = (bf16[128,1024]{1,0:T(8,128)(2,1)}, bf16[128,1024]{1,0:T(8,128)(2,1)}, u32[]{:S(2)}, u32[]{:S(2)}) collective-permute-start(bf16[128,1024]{1,0:T(8,128)(2,1)} %copy-done.1), channel_id=1, source_target_pairs={{0,17},{1,18},{2,19},{3,16},{8,25},{9,26},{10,27},{11,24},{16,1},{... | collective-permute-start | bytes 786440 | tf_op jit(solution)/shard_map/ppermute | solution.py:373
  54.6 17.3 %collective-permute-start.2 = (bf16[128,1024]{1,0:T(8,128)(2,1)S(1)}, bf16[128,1024]{1,0:T(8,128)(2,1)}, u32[]{:S(2)}, u32[]{:S(2)}) collective-permute-start(bf16[128,1024]{1,0:T(8,128)(2,1)S(1)} %get-tuple-element.24), channel_id=1, source_target_pairs={{0,25},{1,26},{2,27},{3,24},{8,1},{9,2},{10,3},{11,0},{16,9},{17,1... | collective-permute-start | bytes 786440 | tf_op jit(solution)/shard_map/ppermute | solution.py:373
  56.7 1.3 %copy-start.7 = (f32[10,32,8,128]{3,2,1,0:T(8,128)S(1)}, f32[10,32,8,128]{3,2,1,0:T(8,128)}, u32[]{:S(2)}) copy-start(f32[10,32,8,128]{3,2,1,0:T(8,128)} %copy-done.6) | copy-start | bytes 3932164
  59.3 26.3 %copy-start.12 = (f32[512,128]{1,0:T(8,128)S(1)}, f32[512,128]{1,0:T(8,128)}, u32[]{:S(2)}) copy-start(f32[512,128]{1,0:T(8,128)} %copy-done.11) | copy-start | bytes 786436
  59.3 26.3 %all-to-all-start.1 = ((bf16[32,10,8,128]{3,2,1,0:T(8,128)(2,1)}), bf16[32,10,8,128]{3,2,1,0:T(8,128)(2,1)S(1)}, u32[]{:S(2)}, u32[]{:S(2)}) async-start(bf16[32,10,8,128]{3,2,1,0:T(8,128)(2,1)} %join.1), calls=%async_computation.1 | async-start | bytes 1310720 | tf_op jit(solution)/shard_map/all_to_all | solution.py:393
  67.8 15.0 %collective-permute-start.3 = (bf16[128,1024]{1,0:T(8,128)(2,1)S(1)}, bf16[128,1024]{1,0:T(8,128)(2,1)S(1)}, u32[]{:S(2)}, u32[]{:S(2)}) collective-permute-start(bf16[128,1024]{1,0:T(8,128)(2,1)S(1)} %get-tuple-element.25), channel_id=1, source_target_pairs={{0,9},{1,10},{2,11},{3,8},{8,17},{9,18},{10,19},{11,16},{16,25},{1... | collective-permute-start | bytes 786440 | tf_op jit(solution)/shard_map/ppermute | solution.py:373
  69.8 14.4 %collective-permute-start.4 = (bf16[128,1024]{1,0:T(8,128)(2,1)S(1)}, bf16[128,1024]{1,0:T(8,128)(2,1)S(1)}, u32[]{:S(2)}, u32[]{:S(2)}) collective-permute-start(bf16[128,1024]{1,0:T(8,128)(2,1)S(1)} %get-tuple-element.26), channel_id=1, source_target_pairs={{0,1},{1,2},{2,3},{3,0},{8,9},{9,10},{10,11},{11,8},{16,17},{17,18... | collective-permute-start | bytes 786440 | tf_op jit(solution)/shard_map/ppermute | solution.py:373
  84.3 2.2 %copy-start.13 = (bf16[1,128,4096]{2,1,0:T(8,128)(2,1)}, bf16[1,128,4096]{2,1,0:T(8,128)(2,1)S(1)}, u32[]{:S(2)}) copy-start(bf16[1,128,4096]{2,1,0:T(8,128)(2,1)S(1)} %bitcast_dynamic-update-slice_fusion) | copy-start | bytes 3145732

commit v4 on v3

--- a/solution.py
+++ b/solution.py
@@ -10,6 +10,7 @@
 
 F32, BF16 = jnp.float32, jnp.bfloat16
 LIMITS = (12, 16, 23, 32, 45, 64, 91)
+UF, UB = 8, 8
 LOG2E = 1.4426950408889634
 L = 128
 NX = 4
@@ -139,7 +140,7 @@
         n_ref[s] = both[:, :part].astype(BF16)
         e_ref[s] = both[:, part:].astype(BF16)
 
-    @pl.loop(0, pairs)
+    @pl.loop(0, pairs, unroll=UF)
     def _(p):
         cols = pl.ds(pl.multiple_of(p * L, L), L)
         biases = [
@@ -157,12 +158,14 @@
             two = halves(tile)
             mask = m_ref[s]
             raw = dot(two, tile, NT)
+            both_p = []
             for k in range(2):
                 scores = raw[k * L : (k + 1) * L] * (LOG2E / 64.0) + (biases[k] + mask)
                 expo = jnp.exp2(scores - jnp.max(scores, axis=0, keepdims=True))
                 probs = expo * (1.0 / jnp.sum(expo, axis=0, keepdims=True))
-                p_ref[p, s, k * L : (k + 1) * L] = probs.astype(BF16)
-            mixed = dot(p_ref[p, s], two, TN)
+                both_p.append(probs.astype(BF16))
+                p_ref[p, s, k * L : (k + 1) * L] = both_p[-1]
+            mixed = dot(jnp.concatenate(both_p, axis=0), two, TN)
             a_refs[s][:, cols] = (e_ref[s, :, cols].astype(F32) + mixed).astype(BF16)
 
 
@@ -200,7 +203,7 @@
     blocks = vocab // 16
     _, x, core = place()
 
-    @pl.loop(0, pairs)
+    @pl.loop(0, pairs, unroll=UB)
     def _(p):
         cols = pl.ds(pl.multiple_of(p * L, L), L)
         total = [jnp.zeros((L, L), F32)] * 2

time: 87.9 us -> 83 us (0.944)
  Pallas kernels: 22.6 us -> 13.4 us
  starting transfers between devices: 33.2 us -> 36.8 us
    pallas_call x1, Pallas kernels: 10.4 us -> 5.58 us  [backward(): pl.pallas_call(bwd_kernel, in_specs=[vmem] * (7 + NX), out_specs=[vmem, v...]
    pallas_call x1, Pallas kernels: 8.49 us -> 4.12 us  [forward(): pl.pallas_call(fwd_kernel, in_specs=[vmem, hbm, hbm], out_specs=[vmem] *...]
    ppermute x8, starting transfers between devices: 14.5 us -> 15.9 us  [send(): return lax.ppermute(value, ('x', 'section'), pairs)]
    all_to_all x1, starting transfers between devices: 7.7 us -> 9.04 us  [local(): parts = lax.all_to_all(join(mine, came), ('z', 'x'), 0, 0)]
    ppermute x8, waiting for transfers between devices: 11.3 us -> 12.5 us  [send(): return lax.ppermute(value, ('x', 'section'), pairs)]
    ppermute x1, starting transfers between devices: 0.41 us -> 1.3 us  [local(): came = lax.ppermute(other, 'c', [(0, 1), (1, 0)])]
  transfers between devices with their start and end apart: 11 -> 11, of which waited for: 5 -> 5; matrix products, arithmetic and copies ran while one was open for 4% -> 5% of each run, Pallas kernels for 13% -> 8%
where the time goes in v4:
time: 83 us; the launch traced here: 81.4 us
  starting transfers between devices  36.8 us (44%)
  waiting for transfers between devices  16.4 us (20%)
  Pallas kernels  13.4 us (16%)
  local copies, waits for them, and re-layouts  12.6 us (15%)
  between operations  1.54 us (2%)
    ppermute x8, starting transfers between devices, send(): return lax.ppermute(value, ('x', 'section'), pairs)  15.9 us
    ppermute x8, waiting for transfers between devices, send(): return lax.ppermute(value, ('x', 'section'), pairs)  12.5 us
    all_to_all x1, starting transfers between devices, local(): notes = lax.all_to_all(jnp.concatenate(note, axis=1), ('z', 'x', 'c'), 0, 0)  10.6 us
    all_to_all x1, starting transfers between devices, local(): parts = lax.all_to_all(join(mine, came), ('z', 'x'), 0, 0)  9.04 us
    unnamed x32, local copies, waits for them, and re-layouts  8.25 us
    pallas_call x1, Pallas kernels, backward(): pl.pallas_call(bwd_kernel, in_specs=[vmem] * (7 + NX), out_specs=[vmem, v...  5.58 us
    pallas_call x1, Pallas kernels, forward(): pl.pallas_call(fwd_kernel, in_specs=[vmem, hbm, hbm], out_specs=[vmem] *...  4.12 us
    all_to_all x1, waiting for transfers between devices, local(): notes = lax.all_to_all(jnp.concatenate(note, axis=1), ('z', 'x', 'c'), 0, 0)  2.83 us
  transfers between devices with their start and end apart: 11, of which 5 were waited for; matrix products, arithmetic and copies ran while one was open for 5% of the time, Pallas kernels for 8%

profile of v4, /device:TPU:1, one launch (start us, length us, event | category | flops | bytes accessed | tf_op | source)
XLA Modules:
  0.0 81.4 jit_solution(6935445219576379783)
XLA Ops:
  0.7 1.3 %dynamic-slice_bitcast_fusion = (bf16[128,1024]{1,0:T(8,128)(2,1)S(1)}, bf16[128,1024]{1,0:T(8,128)(2,1)S(1)}, bf16[128,1024]{1,0:T(8,128)(2,1)S(1)}, bf16[128,1024]{1,0:T(8,128)(2,1)S(1)}) fusion(bf16[1,128,4096]{2,1,0:T(8,128)(2,1)} %param.14, s32[]{:T(128)S(6)} %select_n.21, s32[]{:T(128)S(6)} %select_n.22, s32[]{:T(128)S(6)} %select_n.19, s32[]{:T(128)S(6)} %select_n.20), kind=kLoop, calls=%fused_computation.4 | loop fusion | bytes 2097168 | tf_op jit(solution)/shard_map/dynamic_slice | solution.py:379
  2.0 6.1 %collective-permute-start = (bf16[128,1024]{1,0:T(8,128)(2,1)S(1)}, bf16[128,1024]{1,0:T(8,128)(2,1)S(1)}, u32[]{:S(2)}, u32[]{:S(2)}) collective-permute-start(bf16[128,1024]{1,0:T(8,128)(2,1)S(1)} %get-tuple-element.38), channel_id=1, source_target_pairs={{0,19},{1,16},{2,17},{3,18},{8,27},{9,24},{10,25},{11,26},{16,3},{... | collective-permute-start | bytes 786440 | tf_op jit(solution)/shard_map/ppermute | solution.py:376
  8.9 0.7 add_add_fusion
  9.6 10.6 %all-to-all-start = ((s32[64,3,128]{2,1,0:T(4,128)}), s32[64,3,128]{2,1,0:T(4,128)S(1)}, u32[]{:S(2)}, u32[]{:S(2)}) async-start(s32[64,3,128]{2,1,0:T(4,128)} %add_add_fusion), calls=%async_computation | async-start | bytes 262144 | tf_op jit(solution)/shard_map/all_to_all | solution.py:386
  20.2 0.5 collective-permute-start.5
  20.7 1.3 %collective-permute-start.6 = (bf16[128,1024]{1,0:T(8,128)(2,1)S(1)}, bf16[128,1024]{1,0:T(8,128)(2,1)S(1)}, u32[]{:S(2)}, u32[]{:S(2)}) collective-permute-start(bf16[128,1024]{1,0:T(8,128)(2,1)S(1)} %get-tuple-element.39), channel_id=1, source_target_pairs={{0,11},{1,8},{2,9},{3,10},{8,19},{9,16},{10,17},{11,18},{16,27},{1... | collective-permute-start | bytes 786440 | tf_op jit(solution)/shard_map/ppermute | solution.py:376
  22.0 1.4 %collective-permute-start.7 = (bf16[128,1024]{1,0:T(8,128)(2,1)S(1)}, bf16[128,1024]{1,0:T(8,128)(2,1)S(1)}, u32[]{:S(2)}, u32[]{:S(2)}) collective-permute-start(bf16[128,1024]{1,0:T(8,128)(2,1)S(1)} %get-tuple-element.36), channel_id=1, source_target_pairs={{0,27},{1,24},{2,25},{3,26},{8,3},{9,0},{10,1},{11,2},{16,11},{17,... | collective-permute-start | bytes 786440 | tf_op jit(solution)/shard_map/ppermute | solution.py:376
  23.4 2.2 %copy-done = bf16[1,512,4096]{2,1,0:T(8,128)(2,1)S(1)} copy-done((bf16[1,512,4096]{2,1,0:T(8,128)(2,1)S(1)}, bf16[1,512,4096]{2,1,0:T(8,128)(2,1)}, u32[]{:S(2)}) %copy-start) | copy-done | bytes 4194328
  25.6 1.5 %prepare.1 = (bf16[512,2048]{1,0:T(8,128)(2,1)S(1)}, f32[512,128]{1,0:T(8,128)S(1)}, f32[64,128]{1,0:T(8,128)S(1)}) custom-call(bf16[512,4096]{1,0:T(8,128)(2,1)S(1)} %bitcast.26, f32[1,4096]{1,0:T(1,128)S(1)} %copy-done.3, f32[32,64]{1,0:T(8,128)S(1)} %bitcast.27, f32[32,128]{1,0:T(8,128)S(1)} %copy-done.5), custom_call_target="tpu_custom_call" | custom-call | flops 5000000000 | bytes 7340032 | tf_op jit(solution)/shard_map/prepare/pallas_call | solution.py:80
  27.1 1.3 %copy-done.8 = bf16[512,2048]{1,0:T(8,128)(2,1)} copy-done((bf16[512,2048]{1,0:T(8,128)(2,1)}, bf16[512,2048]{1,0:T(8,128)(2,1)S(1)}, u32[]{:S(2)}) %copy-start.8) | copy-done | bytes 2097176
  28.5 2.8 %all-to-all-done.notes_ref = s32[64,3,128]{2,1,0:T(4,128)S(1)} async-done(((s32[64,3,128]{2,1,0:T(4,128)}), s32[64,3,128]{2,1,0:T(4,128)S(1)}, u32[]{:S(2)}, u32[]{:S(2)}) %all-to-all-start) | async-done | bytes 98336 | tf_op jit(solution)/shard_map/all_to_all | solution.py:386
  31.3 1.6 %copy-done.9 = bf16[512,2048]{1,0:T(8,128)(2,1)S(1)} copy-done((bf16[512,2048]{1,0:T(8,128)(2,1)S(1)}, bf16[512,2048]{1,0:T(8,128)(2,1)}, u32[]{:S(2)}) %copy-start.9) | copy-done | bytes 2097176
  32.9 4.1 %forward.1 = (bf16[128,1024]{1,0:T(8,128)(2,1)S(1)}, bf16[128,1024]{1,0:T(8,128)(2,1)S(1)}, bf16[128,1024]{1,0:T(8,128)(2,1)S(1)}, bf16[128,1024]{1,0:T(8,128)(2...) custom-call(s32[64,3,128]{2,1,0:T(4,128)S(1)} %all-to-all-done.notes_ref, ...), custom_call_target="tpu_custom_call" | custom-call | flops 8000000000 | bytes 7340032 | tf_op jit(solution)/shard_map/forward/pallas_call | solution.py:176
  37.0 0.7 copy-done.1
  37.7 1.2 %collective-permute-done.5.rest_0_ = bf16[128,1024]{1,0:T(8,128)(2,1)S(1)} collective-permute-done((bf16[128,1024]{1,0:T(8,128)(2,1)S(1)}, bf16[128,1024]{1,0:T(8,128)(2,1)S(1)}, u32[]{:S(2)}, u32[]{:S(2)}) %collective-permute-start.5) | collective-permute-done | bytes 262176 | tf_op jit(solution)/shard_map/ppermute | solution.py:376
  39.0 5.6 %backward.1 = (f32[10,32,8,128]{3,2,1,0:T(8,128)S(1)}, f32[10,32,8,128]{3,2,1,0:T(8,128)S(1)}) custom-call(s32[64,3,128]{2,1,0:T(4,128)S(1)} %all-to-all-done.notes_ref, bf16[512,2048]{1,0:T(8,128)(2,1)S(1)} %copy-done.10, f32[512,128]{1,0:T(8,128)S(1)} %get-tuple-element.27.r_ref, f32[1,4096]{1,0:T(1,128)S(1)} %copy-done.3, f32[128,128]{1,0:T(8,128)S(1)} %copy-done.4, ...), custom_call_target="tpu_custom_call" | custom-call | flops 10000000000 | bytes 10485760 | tf_op jit(solution)/shard_map/backward/pallas_call | solution.py:267
  44.5 1.1 %copy-done.6 = f32[10,32,8,128]{3,2,1,0:T(8,128)} copy-done((f32[10,32,8,128]{3,2,1,0:T(8,128)}, f32[10,32,8,128]{3,2,1,0:T(8,128)S(1)}, u32[]{:S(2)}) %copy-start.6) | copy-done | bytes 1310744
  45.6 1.3 %collective-permute-start.8 = (f32[10,32,8,128]{3,2,1,0:T(8,128)S(1)}, f32[10,32,8,128]{3,2,1,0:T(8,128)S(1)}, u32[]{:S(2)}, u32[]{:S(2)}) collective-permute-start(f32[10,32,8,128]{3,2,1,0:T(8,128)S(1)} %get-tuple-element.32), channel_id=1, source_target_pairs={{0,4},{4,0},{1,5},{5,1},{2,6},{6,2},{3,7},{7,3},{8,12},{12,8},{9,1... | collective-permute-start | bytes 3932168 | tf_op jit(solution)/shard_map/ppermute | solution.py:391
  46.9 1.9 %collective-permute-start.1 = (bf16[128,1024]{1,0:T(8,128)(2,1)}, bf16[128,1024]{1,0:T(8,128)(2,1)}, u32[]{:S(2)}, u32[]{:S(2)}) collective-permute-start(bf16[128,1024]{1,0:T(8,128)(2,1)} %copy-done.1), channel_id=1, source_target_pairs={{0,17},{1,18},{2,19},{3,16},{8,25},{9,26},{10,27},{11,24},{16,1},{... | collective-permute-start | bytes 786440 | tf_op jit(solution)/shard_map/ppermute | solution.py:376
  48.8 1.4 %collective-permute-start.2 = (bf16[128,1024]{1,0:T(8,128)(2,1)S(1)}, bf16[128,1024]{1,0:T(8,128)(2,1)}, u32[]{:S(2)}, u32[]{:S(2)}) collective-permute-start(bf16[128,1024]{1,0:T(8,128)(2,1)S(1)} %get-tuple-element.24), channel_id=1, source_target_pairs={{0,25},{1,26},{2,27},{3,24},{8,1},{9,2},{10,3},{11,0},{16,9},{17,1... | collective-permute-start | bytes 786440 | tf_op jit(solution)/shard_map/ppermute | solution.py:376
  50.2 1.3 %copy-done.7 = f32[10,32,8,128]{3,2,1,0:T(8,128)S(1)} copy-done((f32[10,32,8,128]{3,2,1,0:T(8,128)S(1)}, f32[10,32,8,128]{3,2,1,0:T(8,128)}, u32[]{:S(2)}) %copy-start.7) | copy-done | bytes 1310744
  51.5 1.3 %join.1 = bf16[32,10,8,128]{3,2,1,0:T(8,128)(2,1)} custom-call(f32[10,32,8,128]{3,2,1,0:T(8,128)S(1)} %copy-done.7, f32[10,32,8,128]{3,2,1,0:T(8,128)S(1)} %collective-permute-done.8.came_ref), custom_call_target="tpu_custom_call" | custom-call | flops 2000000000 | bytes 4194304 | tf_op jit(solution)/shard_map/join/pallas_call | solution.py:302
  52.7 9.0 %all-to-all-start.1 = ((bf16[32,10,8,128]{3,2,1,0:T(8,128)(2,1)}), bf16[32,10,8,128]{3,2,1,0:T(8,128)(2,1)S(1)}, u32[]{:S(2)}, u32[]{:S(2)}) async-start(bf16[32,10,8,128]{3,2,1,0:T(8,128)(2,1)} %join.1), calls=%async_computation.1 | async-start | bytes 1310720 | tf_op jit(solution)/shard_map/all_to_all | solution.py:396
  61.8 0.9 %dynamic-slice_bitcast_fusion.4.table_ref = bf16[8,4096]{1,0:T(8,128)(2,1)S(1)} fusion(bf16[1,512,4096]{2,1,0:T(8,128)(2,1)} %param.11, s32[]{:T(128)S(6)} %select_n.23), kind=kLoop, calls=%fused_computation.9 | loop fusion | bytes 131076 | tf_op jit(solution)/shard_map/dynamic_slice | solution.py:397
  62.6 2.3 %collective-permute-start.3 = (bf16[128,1024]{1,0:T(8,128)(2,1)S(1)}, bf16[128,1024]{1,0:T(8,128)(2,1)S(1)}, u32[]{:S(2)}, u32[]{:S(2)}) collective-permute-start(bf16[128,1024]{1,0:T(8,128)(2,1)S(1)} %get-tuple-element.25), channel_id=1, source_target_pairs={{0,9},{1,10},{2,11},{3,8},{8,17},{9,18},{10,19},{11,16},{16,25},{1... | collective-permute-start | bytes 786440 | tf_op jit(solution)/shard_map/ppermute | solution.py:376
  65.0 1.0 %collective-permute-start.4 = (bf16[128,1024]{1,0:T(8,128)(2,1)S(1)}, bf16[128,1024]{1,0:T(8,128)(2,1)S(1)}, u32[]{:S(2)}, u32[]{:S(2)}) collective-permute-start(bf16[128,1024]{1,0:T(8,128)(2,1)S(1)} %get-tuple-element.26), channel_id=1, source_target_pairs={{0,1},{1,2},{2,3},{3,0},{8,9},{9,10},{10,11},{11,8},{16,17},{17,18... | collective-permute-start | bytes 786440 | tf_op jit(solution)/shard_map/ppermute | solution.py:376
  66.1 1.0 %bitcast_dynamic-update-slice_fusion.3 = bf16[1,128,4096]{2,1,0:T(8,128)(2,1)S(1)} fusion(bf16[1,128,4096]{2,1,0:T(8,128)(2,1)S(1)} %broadcast_in_dim.33, s32[]{:T(128)S(6)} %select_n.19, bf16[128,1024]{1,0:T(8,128)(2,1)} %collective-permute-done.1), kind=kLoop, calls=%fused_computation.3 | loop fusion | bytes 524292 | tf_op jit(solution)/shard_map/dynamic_update_slice | solution.py:394
  67.1 1.0 %bitcast_dynamic-update-slice_fusion.2 = bf16[1,128,4096]{2,1,0:T(8,128)(2,1)S(1)} fusion(bf16[1,128,4096]{2,1,0:T(8,128)(2,1)S(1)} %bitcast_dynamic-update-slice_fusion.3, s32[]{:T(128)S(6)} %select_n.20, bf16[128,1024]{1,0:T(8,128)(2,1)} %collective-permute-done.2), kind=kLoop, calls=%fused_computation.2 | loop fusion | bytes 524292 | tf_op jit(solution)/shard_map/dynamic_update_slice | solution.py:394
  68.1 9.6 %collective-permute-done.3 = bf16[128,1024]{1,0:T(8,128)(2,1)S(1)} collective-permute-done((bf16[128,1024]{1,0:T(8,128)(2,1)S(1)}, bf16[128,1024]{1,0:T(8,128)(2,1)S(1)}, u32[]{:S(2)}, u32[]{:S(2)}) %collective-permute-start.3) | collective-permute-done | bytes 262176 | tf_op jit(solution)/shard_map/ppermute | solution.py:376
  77.7 1.7 %collective-permute-done.4 = bf16[128,1024]{1,0:T(8,128)(2,1)S(1)} collective-permute-done((bf16[128,1024]{1,0:T(8,128)(2,1)S(1)}, bf16[128,1024]{1,0:T(8,128)(2,1)S(1)}, u32[]{:S(2)}, u32[]{:S(2)}) %collective-permute-start.4) | collective-permute-done | bytes 262176 | tf_op jit(solution)/shard_map/ppermute | solution.py:376
  79.5 1.1 %all-to-all-done.1.parts_ref = bf16[32,10,8,128]{3,2,1,0:T(8,128)(2,1)S(1)} async-done(((bf16[32,10,8,128]{3,2,1,0:T(8,128)(2,1)}), bf16[32,10,8,128]{3,2,1,0:T(8,128)(2,1)S(1)}, u32[]{:S(2)}, u32[]{:S(2)}) %all-to-all-start.1) | async-done | bytes 655392 | tf_op jit(solution)/shard_map/all_to_all | solution.py:396
  80.5 0.9 %finish.1 = (f32[1,8,4096]{2,1,0:T(8,128)}, f32[1,4096]{1,0:T(1,128)}, f32[1,32,64]{2,1,0:T(8,128)}) custom-call(bf16[32,10,8,128]{3,2,1,0:T(8,128)(2,1)S(1)} %all-to-all-done.1.parts_ref, bf16[8,4096]{1,0:T(8,128)(2,1)S(1)} %dynamic-slice_bitcast_fusion.4.table_ref, f32[512,128]{1,0:T(8,128)S(1)} %copy-done.12), custom_call_target="tpu_custom_call" | custom-call | flops 2000000000 | bytes 2097152 | tf_op jit(solution)/shard_map/finish/pallas_call | solution.py:348
  (38 shorter events, 0.3 us)
Async XLA Ops:
  0.6 22.8 %copy-start.5 = (f32[32,128]{1,0:T(8,128)S(1)}, f32[32,128]{1,0:T(8,128)}, u32[]{:S(2)}) copy-start(f32[32,128]{1,0:T(8,128)} %constant.62.picks_ref) | copy-start | bytes 49156
  0.6 8.2 %copy-start.14 = (s32[1,1,128]{2,1,0:T(1,128)S(1)}, s32[1,1,128]{2,1,0:T(1,128)}, u32[]{:S(2)}) copy-start(s32[1,1,128]{2,1,0:T(1,128)} %param.9) | copy-start | bytes 1540
  0.7 8.2 %copy-start.15 = (s32[1,1,128]{2,1,0:T(1,128)S(1)}, s32[1,1,128]{2,1,0:T(1,128)}, u32[]{:S(2)}) copy-start(s32[1,1,128]{2,1,0:T(1,128)} %param.8) | copy-start | bytes 1540
  0.7 22.7 %copy-start.3 = (f32[1,4096]{1,0:T(1,128)S(1)}, f32[1,4096]{1,0:T(1,128)}, u32[]{:S(2)}) copy-start(f32[1,4096]{1,0:T(1,128)} %gain_ref.3) | copy-start | bytes 49156
  0.7 22.7 %copy-start.2 = (f32[1,32,64]{2,1,0:T(8,128)S(1)}, f32[1,32,64]{2,1,0:T(8,128)}, u32[]{:S(2)}) copy-start(f32[1,32,64]{2,1,0:T(8,128)} %param.13) | copy-start | bytes 24580
  2.0 21.4 %collective-permute-start = (bf16[128,1024]{1,0:T(8,128)(2,1)S(1)}, bf16[128,1024]{1,0:T(8,128)(2,1)S(1)}, u32[]{:S(2)}, u32[]{:S(2)}) collective-permute-start(bf16[128,1024]{1,0:T(8,128)(2,1)S(1)} %get-tuple-element.38), channel_id=1, source_target_pairs={{0,19},{1,16},{2,17},{3,18},{8,27},{9,24},{10,25},{11,26},{16,3},{... | collective-permute-start | bytes 786440 | tf_op jit(solution)/shard_map/ppermute | solution.py:376
  9.6 21.7 %all-to-all-start = ((s32[64,3,128]{2,1,0:T(4,128)}), s32[64,3,128]{2,1,0:T(4,128)S(1)}, u32[]{:S(2)}, u32[]{:S(2)}) async-start(s32[64,3,128]{2,1,0:T(4,128)} %add_add_fusion), calls=%async_computation | async-start | bytes 262144 | tf_op jit(solution)/shard_map/all_to_all | solution.py:386
  20.2 18.7 %collective-permute-start.5 = (bf16[128,1024]{1,0:T(8,128)(2,1)S(1)}, bf16[128,1024]{1,0:T(8,128)(2,1)S(1)}, u32[]{:S(2)}, u32[]{:S(2)}) collective-permute-start(bf16[128,1024]{1,0:T(8,128)(2,1)S(1)} %get-tuple-element.37), channel_id=1, source_target_pairs={{0,3},{1,0},{2,1},{3,2},{8,11},{9,8},{10,9},{11,10},{16,19},{17,16... | collective-permute-start | bytes 786440 | tf_op jit(solution)/shard_map/ppermute | solution.py:376
  20.7 18.2 %collective-permute-start.6 = (bf16[128,1024]{1,0:T(8,128)(2,1)S(1)}, bf16[128,1024]{1,0:T(8,128)(2,1)S(1)}, u32[]{:S(2)}, u32[]{:S(2)}) collective-permute-start(bf16[128,1024]{1,0:T(8,128)(2,1)S(1)} %get-tuple-element.39), channel_id=1, source_target_pairs={{0,11},{1,8},{2,9},{3,10},{8,19},{9,16},{10,17},{11,18},{16,27},{1... | collective-permute-start | bytes 786440 | tf_op jit(solution)/shard_map/ppermute | solution.py:376
  22.0 16.9 %collective-permute-start.7 = (bf16[128,1024]{1,0:T(8,128)(2,1)S(1)}, bf16[128,1024]{1,0:T(8,128)(2,1)S(1)}, u32[]{:S(2)}, u32[]{:S(2)}) collective-permute-start(bf16[128,1024]{1,0:T(8,128)(2,1)S(1)} %get-tuple-element.36), channel_id=1, source_target_pairs={{0,27},{1,24},{2,25},{3,26},{8,3},{9,0},{10,1},{11,2},{16,11},{17,... | collective-permute-start | bytes 786440 | tf_op jit(solution)/shard_map/ppermute | solution.py:376
  23.4 2.2 %copy-start = (bf16[1,512,4096]{2,1,0:T(8,128)(2,1)S(1)}, bf16[1,512,4096]{2,1,0:T(8,128)(2,1)}, u32[]{:S(2)}) copy-start(bf16[1,512,4096]{2,1,0:T(8,128)(2,1)} %param.11) | copy-start | bytes 12582916
  27.1 1.4 %copy-start.8 = (bf16[512,2048]{1,0:T(8,128)(2,1)}, bf16[512,2048]{1,0:T(8,128)(2,1)S(1)}, u32[]{:S(2)}) copy-start(bf16[512,2048]{1,0:T(8,128)(2,1)S(1)} %get-tuple-element.21.ne_hbm.ne_ref) | copy-start | bytes 6291460
  28.5 10.5 %copy-start.11 = (f32[512,128]{1,0:T(8,128)}, f32[512,128]{1,0:T(8,128)S(1)}, u32[]{:S(2)}) copy-start(f32[512,128]{1,0:T(8,128)S(1)} %get-tuple-element.27.r_ref) | copy-start | bytes 786436
  31.3 1.6 %copy-start.9 = (bf16[512,2048]{1,0:T(8,128)(2,1)S(1)}, bf16[512,2048]{1,0:T(8,128)(2,1)}, u32[]{:S(2)}) copy-start(bf16[512,2048]{1,0:T(8,128)(2,1)} %copy-done.8) | copy-start | bytes 6291460
  32.9 6.0 %copy-start.4 = (f32[128,128]{1,0:T(8,128)S(1)}, f32[128,128]{1,0:T(8,128)}, u32[]{:S(2)}) copy-start(f32[128,128]{1,0:T(8,128)} %constant.54.clone.picks_ref) | copy-start | bytes 196612
  32.9 6.1 %copy-start.10 = (bf16[512,2048]{1,0:T(8,128)(2,1)S(1)}, bf16[512,2048]{1,0:T(8,128)(2,1)}, u32[]{:S(2)}) copy-start(bf16[512,2048]{1,0:T(8,128)(2,1)} %copy-done.8) | copy-start | bytes 6291460
  37.0 0.7 copy-start.1
  44.5 1.1 %copy-start.6 = (f32[10,32,8,128]{3,2,1,0:T(8,128)}, f32[10,32,8,128]{3,2,1,0:T(8,128)S(1)}, u32[]{:S(2)}) copy-start(f32[10,32,8,128]{3,2,1,0:T(8,128)S(1)} %get-tuple-element.31.mine_ref) | copy-start | bytes 3932164
  45.6 4.5 %collective-permute-start.8 = (f32[10,32,8,128]{3,2,1,0:T(8,128)S(1)}, f32[10,32,8,128]{3,2,1,0:T(8,128)S(1)}, u32[]{:S(2)}, u32[]{:S(2)}) collective-permute-start(f32[10,32,8,128]{3,2,1,0:T(8,128)S(1)} %get-tuple-element.32), channel_id=1, source_target_pairs={{0,4},{4,0},{1,5},{5,1},{2,6},{6,2},{3,7},{7,3},{8,12},{12,8},{9,1... | collective-permute-start | bytes 3932168 | tf_op jit(solution)/shard_map/ppermute | solution.py:391
  46.9 19.1 %collective-permute-start.1 = (bf16[128,1024]{1,0:T(8,128)(2,1)}, bf16[128,1024]{1,0:T(8,128)(2,1)}, u32[]{:S(2)}, u32[]{:S(2)}) collective-permute-start(bf16[128,1024]{1,0:T(8,128)(2,1)} %copy-done.1), channel_id=1, source_target_pairs={{0,17},{1,18},{2,19},{3,16},{8,25},{9,26},{10,27},{11,24},{16,1},{... | collective-permute-start | bytes 786440 | tf_op jit(solution)/shard_map/ppermute | solution.py:376
  48.8 18.3 %collective-permute-start.2 = (bf16[128,1024]{1,0:T(8,128)(2,1)S(1)}, bf16[128,1024]{1,0:T(8,128)(2,1)}, u32[]{:S(2)}, u32[]{:S(2)}) collective-permute-start(bf16[128,1024]{1,0:T(8,128)(2,1)S(1)} %get-tuple-element.24), channel_id=1, source_target_pairs={{0,25},{1,26},{2,27},{3,24},{8,1},{9,2},{10,3},{11,0},{16,9},{17,1... | collective-permute-start | bytes 786440 | tf_op jit(solution)/shard_map/ppermute | solution.py:376
  50.2 1.3 %copy-start.7 = (f32[10,32,8,128]{3,2,1,0:T(8,128)S(1)}, f32[10,32,8,128]{3,2,1,0:T(8,128)}, u32[]{:S(2)}) copy-start(f32[10,32,8,128]{3,2,1,0:T(8,128)} %copy-done.6) | copy-start | bytes 3932164
  52.7 27.8 %copy-start.12 = (f32[512,128]{1,0:T(8,128)S(1)}, f32[512,128]{1,0:T(8,128)}, u32[]{:S(2)}) copy-start(f32[512,128]{1,0:T(8,128)} %copy-done.11) | copy-start | bytes 786436
  52.7 27.8 %all-to-all-start.1 = ((bf16[32,10,8,128]{3,2,1,0:T(8,128)(2,1)}), bf16[32,10,8,128]{3,2,1,0:T(8,128)(2,1)S(1)}, u32[]{:S(2)}, u32[]{:S(2)}) async-start(bf16[32,10,8,128]{3,2,1,0:T(8,128)(2,1)} %join.1), calls=%async_computation.1 | async-start | bytes 1310720 | tf_op jit(solution)/shard_map/all_to_all | solution.py:396
  62.6 15.0 %collective-permute-start.3 = (bf16[128,1024]{1,0:T(8,128)(2,1)S(1)}, bf16[128,1024]{1,0:T(8,128)(2,1)S(1)}, u32[]{:S(2)}, u32[]{:S(2)}) collective-permute-start(bf16[128,1024]{1,0:T(8,128)(2,1)S(1)} %get-tuple-element.25), channel_id=1, source_target_pairs={{0,9},{1,10},{2,11},{3,8},{8,17},{9,18},{10,19},{11,16},{16,25},{1... | collective-permute-start | bytes 786440 | tf_op jit(solution)/shard_map/ppermute | solution.py:376
  65.0 14.4 %collective-permute-start.4 = (bf16[128,1024]{1,0:T(8,128)(2,1)S(1)}, bf16[128,1024]{1,0:T(8,128)(2,1)S(1)}, u32[]{:S(2)}, u32[]{:S(2)}) collective-permute-start(bf16[128,1024]{1,0:T(8,128)(2,1)S(1)} %get-tuple-element.26), channel_id=1, source_target_pairs={{0,1},{1,2},{2,3},{3,0},{8,9},{9,10},{10,11},{11,8},{16,17},{17,18... | collective-permute-start | bytes 786440 | tf_op jit(solution)/shard_map/ppermute | solution.py:376
  79.4 2.0 %copy-start.13 = (bf16[1,128,4096]{2,1,0:T(8,128)(2,1)}, bf16[1,128,4096]{2,1,0:T(8,128)(2,1)S(1)}, u32[]{:S(2)}) copy-start(bf16[1,128,4096]{2,1,0:T(8,128)(2,1)S(1)} %bitcast_dynamic-update-slice_fusion) | copy-start | bytes 3145732

commit v5 on v4

--- a/solution.py
+++ b/solution.py
@@ -15,6 +15,7 @@
 L = 128
 NX = 4
 MIB = 1024 * 1024
+SPARE = 24
 
 
 def bucket_picks():
@@ -92,7 +93,7 @@
             pl.BlockSpec((heads, L), lambda i: (0, 0)),
         ],
         out_shape=[
-            jax.ShapeDtypeStruct((vocab, 2 * part), BF16),
+            jax.ShapeDtypeStruct((vocab * SPARE, 2 * part), BF16),
             jax.ShapeDtypeStruct((vocab, L), F32),
             jax.ShapeDtypeStruct((heads, L), F32),
         ],
@@ -169,7 +170,7 @@
             a_refs[s][:, cols] = (e_ref[s, :, cols].astype(F32) + mixed).astype(BF16)
 
 
-def forward(notes, ne, bvec):
+def forward(notes, ne, bvec, vocab):
     part = ne.shape[1] // 2
     pairs = part // L
     vmem, hbm = pl.BlockSpec(memory_space=pltpu.VMEM), pl.BlockSpec(memory_space=pltpu.HBM)
@@ -185,7 +186,7 @@
         scratch_shapes=[
             pltpu.VMEM((NX, L, part), BF16),
             pltpu.VMEM((NX, L, L), F32),
-            pltpu.VMEM(ne.shape, BF16),
+            pltpu.VMEM((vocab, 2 * part), BF16),
             pltpu.VMEM(bvec.shape, F32),
             pltpu.SemaphoreType.DMA((9,)),
         ],
@@ -195,10 +196,12 @@
     )(notes, ne, bvec)
 
 
-def bwd_kernel(notes_ref, ne_ref, r_ref, gain_ref, picks_ref, n_ref, p_ref, *rest):
-    g_refs, (mine_ref, other_ref), rest = rest[:NX], rest[NX : NX + 2], rest[NX + 2 :]
-    d_ref, rg_ref, o_ref, diag_ref = rest
-    vocab, part = ne_ref.shape[0], ne_ref.shape[1] // 2
+def bwd_kernel(notes_ref, ne_hbm, r_ref, gain_ref, picks_ref, n_ref, p_ref, *rest):
+    g_refs, (mine_hbm, other_ref), rest = rest[:NX], rest[NX : NX + 2], rest[NX + 2 :]
+    d_ref, rg_ref, o_ref, diag_ref, own_ref, mine_ref, own_sem, sems = rest
+    vocab, part = own_ref.shape
+    fetch = pltpu.make_async_copy(ne_hbm.at[pl.ds(0, vocab), pl.ds(part, part)], own_ref, own_sem)
+    fetch.start()
     pairs = part // L
     blocks = vocab // 16
     _, x, core = place()
@@ -230,11 +233,19 @@
     for s in range(NX):
         o_ref[:, s * L : (s + 1) * L] = onehot_t(packed(notes_ref, s, 0), vocab)
 
+    fetch.wait()
+    copies = []
+
+    def out(tile):
+        copies.append(pltpu.make_async_copy(mine_ref.at[tile], mine_hbm.at[tile], sems.at[tile]))
+        copies[-1].start()
+
     def put(tile, value):
         value = value.reshape(blocks, 2, 8, L)
         first, second = value[:, 0], value[:, 1]
         mine_ref[tile] = jnp.where(core == 0, first, second)
         other_ref[tile] = jnp.where(core == 0, second, first)
+        out(tile)
 
     r = r_ref[...]
     along = jnp.zeros((vocab, L), F32)
@@ -243,7 +254,7 @@
         d_act = dot(o_ref[...], rg_ref[:, cols], NN)
         d_norm = dot(o_ref[...], d_ref[:, cols], NN)
         gain = gain_ref[:, pl.ds(pl.multiple_of(x * part + f * L, L), L)]
-        own = ne_ref[:, part + f * L : part + (f + 1) * L].astype(F32)
+        own = own_ref[:, cols].astype(F32)
         scaled = d_norm * r
         put(f, d_act + scaled * gain)
         along = along + own * (d_norm * gain)
@@ -256,24 +267,31 @@
         ref[pairs + 1, 1] = sums[:8]
         ref[pairs + 1, 2] = sums[8:]
         ref[pairs + 1, 3:] = jnp.zeros((blocks - 3, 8, L), F32)
+    out(pairs + 1)
+    for copy in copies:
+        copy.wait()
 
 
 def backward(notes, ne, r, gain, picks, n, probs, grads):
-    vocab, part = ne.shape[0], ne.shape[1] // 2
+    vocab, part = r.shape[0], ne.shape[1] // 2
     pairs = part // L
-    vmem = pl.BlockSpec(memory_space=pltpu.VMEM)
+    vmem, hbm = pl.BlockSpec(memory_space=pltpu.VMEM), pl.BlockSpec(memory_space=pltpu.HBM)
     stacked = (pairs + 2, vocab // 16, 8, L)
-    out = jax.ShapeDtypeStruct(stacked, F32)
+    spare = (stacked[0] * 32,) + stacked[1:]
     return pl.pallas_call(
         bwd_kernel,
-        in_specs=[vmem] * (7 + NX),
-        out_specs=[vmem, vmem],
-        out_shape=[out, out],
+        in_specs=[vmem, hbm] + [vmem] * (5 + NX),
+        out_specs=[hbm, vmem],
+        out_shape=[jax.ShapeDtypeStruct(spare, F32), jax.ShapeDtypeStruct(stacked, F32)],
         scratch_shapes=[
             pltpu.VMEM((NX * L, part), BF16),
             pltpu.VMEM((NX * L, part), BF16),
             pltpu.VMEM((vocab, NX * L), BF16),
             pltpu.VMEM((2 * pairs, L), F32),
+            pltpu.VMEM((vocab, part), BF16),
+            pltpu.VMEM(stacked, F32),
+            pltpu.SemaphoreType.DMA,
+            pltpu.SemaphoreType.DMA((pairs + 2,)),
         ],
         compiler_params=pltpu.CompilerParams(vmem_limit_bytes=24 * MIB),
         cost_estimate=cost(10, 10),
@@ -281,10 +299,16 @@
     )(notes, ne, r, gain, picks, n, probs, *grads)
 
 
-def join_kernel(mine_ref, came_ref, out_ref):
+def join_kernel(mine_hbm, came_ref, out_ref, mine_ref, sems):
     tiles, blocks = mine_ref.shape[0] - 2, mine_ref.shape[1]
+    copies = [pltpu.make_async_copy(mine_hbm.at[t], mine_ref.at[t], sems.at[t]) for t in range(tiles + 2)]
+    for copy in copies:
+        copy.start()
     for t in range(tiles):
+        copies[t].wait()
         out_ref[:, t] = (mine_ref[t] + came_ref[t]).astype(BF16)
+    copies[tiles].wait()
+    copies[tiles + 1].wait()
     sums = [mine_ref[tiles + 1, t] + came_ref[tiles + 1, t] for t in range(3)]
     out_ref[:, tiles] = jnp.broadcast_to(sums[0].astype(BF16)[None], (blocks, 8, L))
     bias = sums[1] + pltpu.roll(sums[2], 32, 1)
@@ -297,14 +321,15 @@
 
 
 def join(mine, came):
-    tiles, blocks = mine.shape[:2]
-    vmem = pl.BlockSpec(memory_space=pltpu.VMEM)
+    tiles, blocks = came.shape[:2]
+    vmem, hbm = pl.BlockSpec(memory_space=pltpu.VMEM), pl.BlockSpec(memory_space=pltpu.HBM)
     return pl.pallas_call(
         join_kernel,
-        in_specs=[vmem, vmem],
+        in_specs=[hbm, vmem],
         out_specs=vmem,
         out_shape=jax.ShapeDtypeStruct((blocks, tiles, 8, L), BF16),
-        compiler_params=pltpu.CompilerParams(vmem_limit_bytes=8 * MIB),
+        scratch_shapes=[pltpu.VMEM(came.shape, F32), pltpu.SemaphoreType.DMA((tiles,))],
+        compiler_params=pltpu.CompilerParams(vmem_limit_bytes=40 * MIB),
         cost_estimate=cost(2, 4),
         name="join",
     )(mine, came)
@@ -379,13 +404,13 @@
         send(lax.dynamic_slice(grad, (0, lax.rem(x + s, NX) * part), (L, part)), s, -1) for s in range(NX)
     ]
 
-    table_then, grads[2] = lax.optimization_barrier((table, grads[2]))
+    table_then, grads[1], grads[2] = lax.optimization_barrier((table, grads[1], grads[2]))
     ne, r, bvec = prepare(table_then, gain, pos, picks[:32])
     count = 64
     note = [jnp.broadcast_to(v.reshape(1, 1, -1), (count, 1, L)) for v in (token_ids, segment_ids, row_order)]
     notes = lax.all_to_all(jnp.concatenate(note, axis=1), ("z", "x", "c"), 0, 0)
 
-    *acts, normed, probs = forward(notes, ne, bvec)
+    *acts, normed, probs = forward(notes, ne, bvec, table.shape[0])
     pieces = {s: send(acts[s], -s, 1) for s in (2, 1, 3, 0)}
     mine, other = backward(notes, ne, r, gain, picks, normed, probs, grads)
     came = lax.ppermute(other, "c", [(0, 1), (1, 0)])

time: 83 us -> 85.7 us (1.033)
  Pallas kernels: 13.4 us -> 21 us
  starting transfers between devices: 36.8 us -> 34.7 us
  waiting for transfers between devices: 16.4 us -> 15 us
  local copies, waits for them, and re-layouts: 12.6 us -> 11.4 us
    pallas_call x2, Pallas kernels: 6.85 us -> 12.3 us  [the longest x1 9.6 us: backward(): pl.pallas_call(bwd_kernel, in_specs=[vmem, hbm] + [vmem] * (5 + NX), out_...]
    unnamed x32 -> x18, local copies, waits for them, and re-layouts: 8.25 us -> 5.76 us
    all_to_all x1, waiting for transfers between devices: 2.83 us -> 1.18 us  [local(): notes = lax.all_to_all(jnp.concatenate(note, axis=1), ('z', 'x', 'c'), 0, 0)]
    all_to_all x1, waiting for transfers between devices: 1.08 us -> 2.7 us  [local(): parts = lax.all_to_all(join(mine, came), ('z', 'x'), 0, 0)]
    ppermute x8, waiting for transfers between devices: 12.5 us -> 11.1 us  [send(): return lax.ppermute(value, ('x', 'section'), pairs)]
    broadcast_in_dim x2, local copies, waits for them, and re-layouts: 0.04 us -> 1.35 us  [local(): jnp.broadcast_to(v.reshape(1, 1, -1), (count, 1, L))]
    ppermute x8, starting transfers between devices: 15.9 us -> 14.6 us  [send(): return lax.ppermute(value, ('x', 'section'), pairs)]
    pallas_call x1, Pallas kernels: 1.49 us -> 2.75 us  [prepare(): pl.pallas_call(pre_kernel, grid=(vocab // rows,), in_specs=[pl.BlockSpec(...]
  transfers between devices with their start and end apart: 11 -> 11, of which waited for: 5 -> 3; matrix products, arithmetic and copies ran while one was open for 5% -> 6% of each run, Pallas kernels for 8% -> 13%
where the time goes in v5:
time: 85.7 us; the launch traced here: 84.4 us
  starting transfers between devices  34.7 us (40%)
  Pallas kernels  21 us (25%)
  waiting for transfers between devices  15 us (18%)
  local copies, waits for them, and re-layouts  11.4 us (13%)
  between operations  1.46 us (2%)
    ppermute x8, starting transfers between devices, send(): return lax.ppermute(value, ('x', 'section'), pairs)  14.6 us
    all_to_all x1, starting transfers between devices, local(): notes = lax.all_to_all(jnp.concatenate(note, axis=1), ('z', 'x', 'c'), 0, 0)  11.1 us
    ppermute x8, waiting for transfers between devices, send(): return lax.ppermute(value, ('x', 'section'), pairs)  11.1 us
    pallas_call x1, Pallas kernels, backward(): pl.pallas_call(bwd_kernel, in_specs=[vmem, hbm] + [vmem] * (5 + NX), out_...  9.6 us
    all_to_all x1, starting transfers between devices, local(): parts = lax.all_to_all(join(mine, came), ('z', 'x'), 0, 0)  8.49 us
    unnamed x18, local copies, waits for them, and re-layouts  5.76 us
    pallas_call x1, Pallas kernels, forward(): pl.pallas_call(fwd_kernel, in_specs=[vmem, hbm, hbm], out_specs=[vmem] *...  5.1 us
    pallas_call x1, Pallas kernels, prepare(): pl.pallas_call(pre_kernel, grid=(vocab // rows,), in_specs=[pl.BlockSpec(...  2.75 us
  transfers between devices with their start and end apart: 11, of which 3 were waited for; matrix products, arithmetic and copies ran while one was open for 6% of the time, Pallas kernels for 13%

profile of v5, /device:TPU:1, one launch (start us, length us, event | category | flops | bytes accessed | tf_op | source)
XLA Modules:
  0.0 84.4 jit_solution(17232553636663258131)
XLA Ops:
  0.7 1.3 %dynamic-slice_bitcast_fusion = (bf16[128,1024]{1,0:T(8,128)(2,1)S(1)}, bf16[128,1024]{1,0:T(8,128)(2,1)S(1)}, bf16[128,1024]{1,0:T(8,128)(2,1)S(1)}, bf16[128,1024]{1,0:T(8,128)(2,1)S(1)}) fusion(bf16[1,128,4096]{2,1,0:T(8,128)(2,1)} %param.14, s32[]{:T(128)S(6)} %select_n.21, s32[]{:T(128)S(6)} %select_n.20, s32[]{:T(128)S(6)} %select_n.19, s32[]{:T(128)S(6)} %select_n.22), kind=kLoop, calls=%fused_computation.4 | loop fusion | bytes 2097168 | tf_op jit(solution)/shard_map/dynamic_slice | solution.py:404
  2.0 4.6 %collective-permute-start = (bf16[128,1024]{1,0:T(8,128)(2,1)S(1)}, bf16[128,1024]{1,0:T(8,128)(2,1)S(1)}, u32[]{:S(2)}, u32[]{:S(2)}) collective-permute-start(bf16[128,1024]{1,0:T(8,128)(2,1)S(1)} %get-tuple-element.40), channel_id=1, source_target_pairs={{0,11},{1,8},{2,9},{3,10},{8,19},{9,16},{10,17},{11,18},{16,27},{1... | collective-permute-start | bytes 786440 | tf_op jit(solution)/shard_map/ppermute | solution.py:401
  6.5 2.6 %collective-permute-start.1 = (bf16[128,1024]{1,0:T(8,128)(2,1)S(1)}, bf16[128,1024]{1,0:T(8,128)(2,1)S(1)}, u32[]{:S(2)}, u32[]{:S(2)}) collective-permute-start(bf16[128,1024]{1,0:T(8,128)(2,1)S(1)} %get-tuple-element.39), channel_id=1, source_target_pairs={{0,19},{1,16},{2,17},{3,18},{8,27},{9,24},{10,25},{11,26},{16,3},{... | collective-permute-start | bytes 786440 | tf_op jit(solution)/shard_map/ppermute | solution.py:401
  9.9 0.7 broadcast_in_dim.37
  10.6 0.7 broadcast_in_dim.35
  11.2 0.7 add_add_fusion
  12.0 11.1 %all-to-all-start = ((s32[64,3,128]{2,1,0:T(4,128)}), s32[64,3,128]{2,1,0:T(4,128)S(1)}, u32[]{:S(2)}, u32[]{:S(2)}) async-start(s32[64,3,128]{2,1,0:T(4,128)} %add_add_fusion), calls=%async_computation | async-start | bytes 262144 | tf_op jit(solution)/shard_map/all_to_all | solution.py:411
  23.1 0.2 collective-permute-start.6
  23.4 2.6 %collective-permute-start.7 = (bf16[128,1024]{1,0:T(8,128)(2,1)S(1)}, bf16[128,1024]{1,0:T(8,128)(2,1)S(1)}, u32[]{:S(2)}, u32[]{:S(2)}) collective-permute-start(bf16[128,1024]{1,0:T(8,128)(2,1)S(1)} %get-tuple-element.38), channel_id=1, source_target_pairs={{0,27},{1,24},{2,25},{3,26},{8,3},{9,0},{10,1},{11,2},{16,11},{17,... | collective-permute-start | bytes 786440 | tf_op jit(solution)/shard_map/ppermute | solution.py:401
  26.0 0.7 copy-done.1
  26.7 2.2 %copy-done.3 = bf16[1,512,4096]{2,1,0:T(8,128)(2,1)S(1)} copy-done((bf16[1,512,4096]{2,1,0:T(8,128)(2,1)S(1)}, bf16[1,512,4096]{2,1,0:T(8,128)(2,1)}, u32[]{:S(2)}) %copy-start.3) | copy-done | bytes 4194328
  28.9 0.7 copy-done.6
  29.6 0.7 copy-done.7
  30.3 2.8 %prepare.1 = (bf16[12288,2048]{1,0:T(8,128)(2,1)}, f32[512,128]{1,0:T(8,128)S(1)}, f32[64,128]{1,0:T(8,128)S(1)}) custom-call(bf16[512,4096]{1,0:T(8,128)(2,1)S(1)} %bitcast.26, f32[1,4096]{1,0:T(1,128)S(1)} %copy-done.1, f32[32,64]{1,0:T(8,128)S(1)} %bitcast.27, f32[32,128]{1,0:T(8,128)S(1)} %copy-done.7), custom_call_target="tpu_custom_call" | custom-call | flops 5000000000 | bytes 7340032 | tf_op jit(solution)/shard_map/prepare/pallas_call | solution.py:81
  33.1 1.2 %all-to-all-done.notes_ref = s32[64,3,128]{2,1,0:T(4,128)S(1)} async-done(((s32[64,3,128]{2,1,0:T(4,128)}), s32[64,3,128]{2,1,0:T(4,128)S(1)}, u32[]{:S(2)}, u32[]{:S(2)}) %all-to-all-start) | async-done | bytes 98336 | tf_op jit(solution)/shard_map/all_to_all | solution.py:411
  34.2 5.1 %forward.1 = (bf16[128,1024]{1,0:T(8,128)(2,1)S(1)}, bf16[128,1024]{1,0:T(8,128)(2,1)S(1)}, bf16[128,1024]{1,0:T(8,128)(2,1)S(1)}, bf16[128,1024]{1,0:T(8,128)(2...) custom-call(s32[64,3,128]{2,1,0:T(4,128)S(1)} %all-to-all-done.notes_ref, ...), custom_call_target="tpu_custom_call" | custom-call | flops 8000000000 | bytes 7340032 | tf_op jit(solution)/shard_map/forward/pallas_call | solution.py:177
  39.4 0.7 copy-done.4
  40.1 0.7 copy-done.5
  40.8 9.6 %backward.1 = (f32[320,32,8,128]{3,2,1,0:T(8,128)}, f32[10,32,8,128]{3,2,1,0:T(8,128)S(1)}) custom-call(s32[64,3,128]{2,1,0:T(4,128)S(1)} %all-to-all-done.notes_ref, bf16[12288,2048]{1,0:T(8,128)(2,1)} %get-tuple-element.22.ne_hbm, f32[512,128]{1,0:T(8,128)S(1)} %get-tuple-element.28.r_ref, f32[1,4096]{1,0:T(1,128)S(1)} %copy-done.2, ...), custom_call_target="tpu_custom_call" | custom-call | flops 10000000000 | bytes 10485760 | tf_op jit(solution)/shard_map/backward/pallas_call | solution.py:281
  50.4 0.5 collective-permute-start.8
  50.9 1.9 %collective-permute-start.2 = (bf16[128,1024]{1,0:T(8,128)(2,1)}, bf16[128,1024]{1,0:T(8,128)(2,1)}, u32[]{:S(2)}, u32[]{:S(2)}) collective-permute-start(bf16[128,1024]{1,0:T(8,128)(2,1)} %copy-done.5), channel_id=1, source_target_pairs={{0,17},{1,18},{2,19},{3,16},{8,25},{9,26},{10,27},{11,24},{16,1},{... | collective-permute-start | bytes 786440 | tf_op jit(solution)/shard_map/ppermute | solution.py:401
  52.8 0.7 collective-permute-start.3
  53.5 2.7 %join.1 = bf16[32,10,8,128]{3,2,1,0:T(8,128)(2,1)} custom-call(f32[320,32,8,128]{3,2,1,0:T(8,128)} %get-tuple-element.33.mine_hbm, f32[10,32,8,128]{3,2,1,0:T(8,128)S(1)} %collective-permute-done.8.came_ref), custom_call_target="tpu_custom_call" | custom-call | flops 2000000000 | bytes 4194304 | tf_op jit(solution)/shard_map/join/pallas_call | solution.py:326
  56.3 8.5 %all-to-all-start.1 = ((bf16[32,10,8,128]{3,2,1,0:T(8,128)(2,1)}), bf16[32,10,8,128]{3,2,1,0:T(8,128)(2,1)S(1)}, u32[]{:S(2)}, u32[]{:S(2)}) async-start(bf16[32,10,8,128]{3,2,1,0:T(8,128)(2,1)} %join.1), calls=%async_computation.1 | async-start | bytes 1310720 | tf_op jit(solution)/shard_map/all_to_all | solution.py:421
  64.8 0.9 %dynamic-slice_bitcast_fusion.4.table_ref = bf16[8,4096]{1,0:T(8,128)(2,1)S(1)} fusion(bf16[1,512,4096]{2,1,0:T(8,128)(2,1)} %param.11, s32[]{:T(128)S(6)} %select_n.23), kind=kLoop, calls=%fused_computation.9 | loop fusion | bytes 131076 | tf_op jit(solution)/shard_map/dynamic_slice | solution.py:422
  65.6 1.9 %collective-permute-start.4 = (bf16[128,1024]{1,0:T(8,128)(2,1)S(1)}, bf16[128,1024]{1,0:T(8,128)(2,1)S(1)}, u32[]{:S(2)}, u32[]{:S(2)}) collective-permute-start(bf16[128,1024]{1,0:T(8,128)(2,1)S(1)} %get-tuple-element.26), channel_id=1, source_target_pairs={{0,9},{1,10},{2,11},{3,8},{8,17},{9,18},{10,19},{11,16},{16,25},{1... | collective-permute-start | bytes 786440 | tf_op jit(solution)/shard_map/ppermute | solution.py:401
  67.6 0.1 broadcast_in_dim.33
  67.7 1.0 %bitcast_dynamic-update-slice_fusion.3 = bf16[1,128,4096]{2,1,0:T(8,128)(2,1)S(1)} fusion(bf16[1,128,4096]{2,1,0:T(8,128)(2,1)S(1)} %broadcast_in_dim.33, s32[]{:T(128)S(6)} %select_n.20, bf16[128,1024]{1,0:T(8,128)(2,1)} %collective-permute-done.2), kind=kLoop, calls=%fused_computation.3 | loop fusion | bytes 524292 | tf_op jit(solution)/shard_map/dynamic_update_slice | solution.py:419
  68.7 1.0 %bitcast_dynamic-update-slice_fusion.2 = bf16[1,128,4096]{2,1,0:T(8,128)(2,1)S(1)} fusion(bf16[1,128,4096]{2,1,0:T(8,128)(2,1)S(1)} %bitcast_dynamic-update-slice_fusion.3, s32[]{:T(128)S(6)} %select_n.19, bf16[128,1024]{1,0:T(8,128)(2,1)} %collective-permute-done.3), kind=kLoop, calls=%fused_computation.2 | loop fusion | bytes 524292 | tf_op jit(solution)/shard_map/dynamic_update_slice | solution.py:419
  69.6 11.1 %collective-permute-done.4 = bf16[128,1024]{1,0:T(8,128)(2,1)S(1)} collective-permute-done((bf16[128,1024]{1,0:T(8,128)(2,1)S(1)}, bf16[128,1024]{1,0:T(8,128)(2,1)S(1)}, u32[]{:S(2)}, u32[]{:S(2)}) %collective-permute-start.4) | collective-permute-done | bytes 262176 | tf_op jit(solution)/shard_map/ppermute | solution.py:401
  80.8 2.7 %all-to-all-done.1.parts_ref = bf16[32,10,8,128]{3,2,1,0:T(8,128)(2,1)S(1)} async-done(((bf16[32,10,8,128]{3,2,1,0:T(8,128)(2,1)}), bf16[32,10,8,128]{3,2,1,0:T(8,128)(2,1)S(1)}, u32[]{:S(2)}, u32[]{:S(2)}) %all-to-all-start.1) | async-done | bytes 655392 | tf_op jit(solution)/shard_map/all_to_all | solution.py:421
  83.5 0.9 %finish.1 = (f32[1,8,4096]{2,1,0:T(8,128)}, f32[1,4096]{1,0:T(1,128)}, f32[1,32,64]{2,1,0:T(8,128)}) custom-call(bf16[32,10,8,128]{3,2,1,0:T(8,128)(2,1)S(1)} %all-to-all-done.1.parts_ref, bf16[8,4096]{1,0:T(8,128)(2,1)S(1)} %dynamic-slice_bitcast_fusion.4.table_ref, f32[512,128]{1,0:T(8,128)S(1)} %get-tuple-element.28.r_ref), custom_call_target="tpu_custom_call" | custom-call | flops 2000000000 | bytes 2097152 | tf_op jit(solution)/shard_map/finish/pallas_call | solution.py:373
  (24 shorter events, 0.2 us)
Async XLA Ops:
  2.0 24.0 %collective-permute-start = (bf16[128,1024]{1,0:T(8,128)(2,1)S(1)}, bf16[128,1024]{1,0:T(8,128)(2,1)S(1)}, u32[]{:S(2)}, u32[]{:S(2)}) collective-permute-start(bf16[128,1024]{1,0:T(8,128)(2,1)S(1)} %get-tuple-element.40), channel_id=1, source_target_pairs={{0,11},{1,8},{2,9},{3,10},{8,19},{9,16},{10,17},{11,18},{16,27},{1... | collective-permute-start | bytes 786440 | tf_op jit(solution)/shard_map/ppermute | solution.py:401
  6.5 19.4 %collective-permute-start.1 = (bf16[128,1024]{1,0:T(8,128)(2,1)S(1)}, bf16[128,1024]{1,0:T(8,128)(2,1)S(1)}, u32[]{:S(2)}, u32[]{:S(2)}) collective-permute-start(bf16[128,1024]{1,0:T(8,128)(2,1)S(1)} %get-tuple-element.39), channel_id=1, source_target_pairs={{0,19},{1,16},{2,17},{3,18},{8,27},{9,24},{10,25},{11,26},{16,3},{... | collective-permute-start | bytes 786440 | tf_op jit(solution)/shard_map/ppermute | solution.py:401
  12.0 22.2 %all-to-all-start = ((s32[64,3,128]{2,1,0:T(4,128)}), s32[64,3,128]{2,1,0:T(4,128)S(1)}, u32[]{:S(2)}, u32[]{:S(2)}) async-start(s32[64,3,128]{2,1,0:T(4,128)} %add_add_fusion), calls=%async_computation | async-start | bytes 262144 | tf_op jit(solution)/shard_map/all_to_all | solution.py:411
  23.1 17.6 %collective-permute-start.6 = (bf16[128,1024]{1,0:T(8,128)(2,1)S(1)}, bf16[128,1024]{1,0:T(8,128)(2,1)S(1)}, u32[]{:S(2)}, u32[]{:S(2)}) collective-permute-start(bf16[128,1024]{1,0:T(8,128)(2,1)S(1)} %get-tuple-element.41), channel_id=1, source_target_pairs={{0,3},{1,0},{2,1},{3,2},{8,11},{9,8},{10,9},{11,10},{16,19},{17,16... | collective-permute-start | bytes 786440 | tf_op jit(solution)/shard_map/ppermute | solution.py:401
  23.4 17.4 %collective-permute-start.7 = (bf16[128,1024]{1,0:T(8,128)(2,1)S(1)}, bf16[128,1024]{1,0:T(8,128)(2,1)S(1)}, u32[]{:S(2)}, u32[]{:S(2)}) collective-permute-start(bf16[128,1024]{1,0:T(8,128)(2,1)S(1)} %get-tuple-element.38), channel_id=1, source_target_pairs={{0,27},{1,24},{2,25},{3,26},{8,3},{9,0},{10,1},{11,2},{16,11},{17,... | collective-permute-start | bytes 786440 | tf_op jit(solution)/shard_map/ppermute | solution.py:401
  26.0 0.7 copy-start.1
  26.7 2.2 %copy-start.3 = (bf16[1,512,4096]{2,1,0:T(8,128)(2,1)S(1)}, bf16[1,512,4096]{2,1,0:T(8,128)(2,1)}, u32[]{:S(2)}) copy-start(bf16[1,512,4096]{2,1,0:T(8,128)(2,1)} %param.11) | copy-start | bytes 12582916
  28.9 0.7 copy-start.6
  29.6 0.7 copy-start.7
  34.2 6.5 %copy-start = (f32[128,128]{1,0:T(8,128)S(1)}, f32[128,128]{1,0:T(8,128)}, u32[]{:S(2)}) copy-start(f32[128,128]{1,0:T(8,128)} %constant.54.clone.picks_ref) | copy-start | bytes 196612
  34.2 6.5 %copy-start.2 = (f32[1,4096]{1,0:T(1,128)S(1)}, f32[1,4096]{1,0:T(1,128)}, u32[]{:S(2)}) copy-start(f32[1,4096]{1,0:T(1,128)} %gain_ref.3) | copy-start | bytes 49156
  39.3 0.7 copy-start.4
  40.1 0.7 copy-start.5
  50.4 3.2 %collective-permute-start.8 = (f32[10,32,8,128]{3,2,1,0:T(8,128)S(1)}, f32[10,32,8,128]{3,2,1,0:T(8,128)S(1)}, u32[]{:S(2)}, u32[]{:S(2)}) collective-permute-start(f32[10,32,8,128]{3,2,1,0:T(8,128)S(1)} %get-tuple-element.34), channel_id=1, source_target_pairs={{0,4},{4,0},{1,5},{5,1},{2,6},{6,2},{3,7},{7,3},{8,12},{12,8},{9,1... | collective-permute-start | bytes 3932168 | tf_op jit(solution)/shard_map/ppermute | solution.py:416
  50.9 16.7 %collective-permute-start.2 = (bf16[128,1024]{1,0:T(8,128)(2,1)}, bf16[128,1024]{1,0:T(8,128)(2,1)}, u32[]{:S(2)}, u32[]{:S(2)}) collective-permute-start(bf16[128,1024]{1,0:T(8,128)(2,1)} %copy-done.5), channel_id=1, source_target_pairs={{0,17},{1,18},{2,19},{3,16},{8,25},{9,26},{10,27},{11,24},{16,1},{... | collective-permute-start | bytes 786440 | tf_op jit(solution)/shard_map/ppermute | solution.py:401
  52.8 15.8 %collective-permute-start.3 = (bf16[128,1024]{1,0:T(8,128)(2,1)}, bf16[128,1024]{1,0:T(8,128)(2,1)}, u32[]{:S(2)}, u32[]{:S(2)}) collective-permute-start(bf16[128,1024]{1,0:T(8,128)(2,1)} %copy-done.4), channel_id=1, source_target_pairs={{0,25},{1,26},{2,27},{3,24},{8,1},{9,2},{10,3},{11,0},{16,9},{17,1... | collective-permute-start | bytes 786440 | tf_op jit(solution)/shard_map/ppermute | solution.py:401
  56.3 27.2 %all-to-all-start.1 = ((bf16[32,10,8,128]{3,2,1,0:T(8,128)(2,1)}), bf16[32,10,8,128]{3,2,1,0:T(8,128)(2,1)S(1)}, u32[]{:S(2)}, u32[]{:S(2)}) async-start(bf16[32,10,8,128]{3,2,1,0:T(8,128)(2,1)} %join.1), calls=%async_computation.1 | async-start | bytes 1310720 | tf_op jit(solution)/shard_map/all_to_all | solution.py:421
  65.6 15.1 %collective-permute-start.4 = (bf16[128,1024]{1,0:T(8,128)(2,1)S(1)}, bf16[128,1024]{1,0:T(8,128)(2,1)S(1)}, u32[]{:S(2)}, u32[]{:S(2)}) collective-permute-start(bf16[128,1024]{1,0:T(8,128)(2,1)S(1)} %get-tuple-element.26), channel_id=1, source_target_pairs={{0,9},{1,10},{2,11},{3,8},{8,17},{9,18},{10,19},{11,16},{16,25},{1... | collective-permute-start | bytes 786440 | tf_op jit(solution)/shard_map/ppermute | solution.py:401
  67.6 13.2 %collective-permute-start.5 = (bf16[128,1024]{1,0:T(8,128)(2,1)S(1)}, bf16[128,1024]{1,0:T(8,128)(2,1)S(1)}, u32[]{:S(2)}, u32[]{:S(2)}) collective-permute-start(bf16[128,1024]{1,0:T(8,128)(2,1)S(1)} %get-tuple-element.27), channel_id=1, source_target_pairs={{0,1},{1,2},{2,3},{3,0},{8,9},{9,10},{10,11},{11,8},{16,17},{17,18... | collective-permute-start | bytes 786440 | tf_op jit(solution)/shard_map/ppermute | solution.py:401
  80.8 3.6 %copy-start.8 = (bf16[1,128,4096]{2,1,0:T(8,128)(2,1)}, bf16[1,128,4096]{2,1,0:T(8,128)(2,1)S(1)}, u32[]{:S(2)}) copy-start(bf16[1,128,4096]{2,1,0:T(8,128)(2,1)S(1)} %bitcast_dynamic-update-slice_fusion) | copy-start | bytes 3145732

commit v6 on v4

--- a/solution.py
+++ b/solution.py
@@ -379,7 +379,7 @@
         send(lax.dynamic_slice(grad, (0, lax.rem(x + s, NX) * part), (L, part)), s, -1) for s in range(NX)
     ]
 
-    table_then, grads[2] = lax.optimization_barrier((table, grads[2]))
+    table_then, grads[0], grads[1] = lax.optimization_barrier((table, grads[0], grads[1]))
     ne, r, bvec = prepare(table_then, gain, pos, picks[:32])
     count = 64
     note = [jnp.broadcast_to(v.reshape(1, 1, -1), (count, 1, L)) for v in (token_ids, segment_ids, row_order)]

time: 83 us -> 80.5 us (0.970)
  waiting for transfers between devices: 16.4 us -> 14.6 us
    all_to_all x1, starting transfers between devices: 10.6 us -> 12.4 us  [local(): notes = lax.all_to_all(jnp.concatenate(note, axis=1), ('z', 'x', 'c'), 0, 0)]
    ppermute x8, waiting for transfers between devices: 12.5 us -> 10.9 us  [send(): return lax.ppermute(value, ('x', 'section'), pairs)]
    all_to_all x1, starting transfers between devices: 9.04 us -> 7.91 us  [local(): parts = lax.all_to_all(join(mine, came), ('z', 'x'), 0, 0)]
  transfers between devices with their start and end apart: 11 -> 11, of which waited for: 5 -> 4; matrix products, arithmetic and copies ran while one was open for 5% -> 5% of each run, Pallas kernels for 8% -> 9%
where the time goes in v6:
time: 80.5 us; the launch traced here: 79 us
  starting transfers between devices  36.2 us (45%)
  waiting for transfers between devices  14.6 us (18%)
  Pallas kernels  13.4 us (17%)
  local copies, waits for them, and re-layouts  12.6 us (16%)
  between operations  1.55 us (2%)
    ppermute x8, starting transfers between devices, send(): return lax.ppermute(value, ('x', 'section'), pairs)  15.3 us
    all_to_all x1, starting transfers between devices, local(): notes = lax.all_to_all(jnp.concatenate(note, axis=1), ('z', 'x', 'c'), 0, 0)  12.4 us
    ppermute x8, waiting for transfers between devices, send(): return lax.ppermute(value, ('x', 'section'), pairs)  10.9 us
    unnamed x32, local copies, waits for them, and re-layouts  8.25 us
    all_to_all x1, starting transfers between devices, local(): parts = lax.all_to_all(join(mine, came), ('z', 'x'), 0, 0)  7.91 us
    pallas_call x1, Pallas kernels, backward(): pl.pallas_call(bwd_kernel, in_specs=[vmem] * (7 + NX), out_specs=[vmem, v...  5.58 us
    pallas_call x1, Pallas kernels, forward(): pl.pallas_call(fwd_kernel, in_specs=[vmem, hbm, hbm], out_specs=[vmem] *...  4.12 us
    all_to_all x1, waiting for transfers between devices, local(): notes = lax.all_to_all(jnp.concatenate(note, axis=1), ('z', 'x', 'c'), 0, 0)  2.41 us
  transfers between devices with their start and end apart: 11, of which 4 were waited for; matrix products, arithmetic and copies ran while one was open for 5% of the time, Pallas kernels for 9%

profile of v6, /device:TPU:1, one launch (start us, length us, event | category | flops | bytes accessed | tf_op | source)
XLA Modules:
  0.0 79.0 jit_solution(7581812656079541266)
XLA Ops:
  0.7 1.3 %dynamic-slice_bitcast_fusion = (bf16[128,1024]{1,0:T(8,128)(2,1)S(1)}, bf16[128,1024]{1,0:T(8,128)(2,1)S(1)}, bf16[128,1024]{1,0:T(8,128)(2,1)S(1)}, bf16[128,1024]{1,0:T(8,128)(2,1)S(1)}) fusion(bf16[1,128,4096]{2,1,0:T(8,128)(2,1)} %param.14, s32[]{:T(128)S(6)} %select_n.22, s32[]{:T(128)S(6)} %select_n.20, s32[]{:T(128)S(6)} %select_n.19, s32[]{:T(128)S(6)} %select_n.21), kind=kLoop, calls=%fused_computation.4 | loop fusion | bytes 2097168 | tf_op jit(solution)/shard_map/dynamic_slice | solution.py:379
  2.0 3.6 %collective-permute-start = (bf16[128,1024]{1,0:T(8,128)(2,1)S(1)}, bf16[128,1024]{1,0:T(8,128)(2,1)S(1)}, u32[]{:S(2)}, u32[]{:S(2)}) collective-permute-start(bf16[128,1024]{1,0:T(8,128)(2,1)S(1)} %get-tuple-element.40), channel_id=1, source_target_pairs={{0,3},{1,0},{2,1},{3,2},{8,11},{9,8},{10,9},{11,10},{16,19},{17,16... | collective-permute-start | bytes 786440 | tf_op jit(solution)/shard_map/ppermute | solution.py:376
  5.6 1.4 %collective-permute-start.1 = (bf16[128,1024]{1,0:T(8,128)(2,1)S(1)}, bf16[128,1024]{1,0:T(8,128)(2,1)S(1)}, u32[]{:S(2)}, u32[]{:S(2)}) collective-permute-start(bf16[128,1024]{1,0:T(8,128)(2,1)S(1)} %get-tuple-element.39), channel_id=1, source_target_pairs={{0,11},{1,8},{2,9},{3,10},{8,19},{9,16},{10,17},{11,18},{16,27},{1... | collective-permute-start | bytes 786440 | tf_op jit(solution)/shard_map/ppermute | solution.py:376
  7.8 0.7 add_add_fusion
  8.6 12.4 %all-to-all-start = ((s32[64,3,128]{2,1,0:T(4,128)}), s32[64,3,128]{2,1,0:T(4,128)S(1)}, u32[]{:S(2)}, u32[]{:S(2)}) async-start(s32[64,3,128]{2,1,0:T(4,128)} %add_add_fusion), calls=%async_computation | async-start | bytes 262144 | tf_op jit(solution)/shard_map/all_to_all | solution.py:386
  21.0 2.9 %collective-permute-start.6 = (bf16[128,1024]{1,0:T(8,128)(2,1)S(1)}, bf16[128,1024]{1,0:T(8,128)(2,1)S(1)}, u32[]{:S(2)}, u32[]{:S(2)}) collective-permute-start(bf16[128,1024]{1,0:T(8,128)(2,1)S(1)} %get-tuple-element.41), channel_id=1, source_target_pairs={{0,19},{1,16},{2,17},{3,18},{8,27},{9,24},{10,25},{11,26},{16,3},{... | collective-permute-start | bytes 786440 | tf_op jit(solution)/shard_map/ppermute | solution.py:376
  23.8 0.8 collective-permute-start.7
  24.7 2.2 %copy-done = bf16[1,512,4096]{2,1,0:T(8,128)(2,1)S(1)} copy-done((bf16[1,512,4096]{2,1,0:T(8,128)(2,1)S(1)}, bf16[1,512,4096]{2,1,0:T(8,128)(2,1)}, u32[]{:S(2)}) %copy-start) | copy-done | bytes 4194328
  26.8 1.5 %prepare.1 = (bf16[512,2048]{1,0:T(8,128)(2,1)S(1)}, f32[512,128]{1,0:T(8,128)S(1)}, f32[64,128]{1,0:T(8,128)S(1)}) custom-call(bf16[512,4096]{1,0:T(8,128)(2,1)S(1)} %bitcast.26, f32[1,4096]{1,0:T(1,128)S(1)} %copy-done.3, f32[32,64]{1,0:T(8,128)S(1)} %bitcast.27, f32[32,128]{1,0:T(8,128)S(1)} %copy-done.5), custom_call_target="tpu_custom_call" | custom-call | flops 5000000000 | bytes 7340032 | tf_op jit(solution)/shard_map/prepare/pallas_call | solution.py:80
  28.3 1.3 %copy-done.8 = bf16[512,2048]{1,0:T(8,128)(2,1)} copy-done((bf16[512,2048]{1,0:T(8,128)(2,1)}, bf16[512,2048]{1,0:T(8,128)(2,1)S(1)}, u32[]{:S(2)}) %copy-start.8) | copy-done | bytes 2097176
  29.7 2.4 %all-to-all-done.notes_ref = s32[64,3,128]{2,1,0:T(4,128)S(1)} async-done(((s32[64,3,128]{2,1,0:T(4,128)}), s32[64,3,128]{2,1,0:T(4,128)S(1)}, u32[]{:S(2)}, u32[]{:S(2)}) %all-to-all-start) | async-done | bytes 98336 | tf_op jit(solution)/shard_map/all_to_all | solution.py:386
  32.1 1.6 %copy-done.9 = bf16[512,2048]{1,0:T(8,128)(2,1)S(1)} copy-done((bf16[512,2048]{1,0:T(8,128)(2,1)S(1)}, bf16[512,2048]{1,0:T(8,128)(2,1)}, u32[]{:S(2)}) %copy-start.9) | copy-done | bytes 2097176
  33.7 4.1 %forward.1 = (bf16[128,1024]{1,0:T(8,128)(2,1)S(1)}, bf16[128,1024]{1,0:T(8,128)(2,1)S(1)}, bf16[128,1024]{1,0:T(8,128)(2,1)S(1)}, bf16[128,1024]{1,0:T(8,128)(2...) custom-call(s32[64,3,128]{2,1,0:T(4,128)S(1)} %all-to-all-done.notes_ref, ...), custom_call_target="tpu_custom_call" | custom-call | flops 8000000000 | bytes 7340032 | tf_op jit(solution)/shard_map/forward/pallas_call | solution.py:176
  37.8 0.7 copy-done.1
  38.6 5.6 %backward.1 = (f32[10,32,8,128]{3,2,1,0:T(8,128)S(1)}, f32[10,32,8,128]{3,2,1,0:T(8,128)S(1)}) custom-call(s32[64,3,128]{2,1,0:T(4,128)S(1)} %all-to-all-done.notes_ref, bf16[512,2048]{1,0:T(8,128)(2,1)S(1)} %copy-done.10, f32[512,128]{1,0:T(8,128)S(1)} %get-tuple-element.28.r_ref, f32[1,4096]{1,0:T(1,128)S(1)} %copy-done.3, f32[128,128]{1,0:T(8,128)S(1)} %copy-done.4, ...), custom_call_target="tpu_custom_call" | custom-call | flops 10000000000 | bytes 10485760 | tf_op jit(solution)/shard_map/backward/pallas_call | solution.py:267
  44.2 1.1 %copy-done.6 = f32[10,32,8,128]{3,2,1,0:T(8,128)} copy-done((f32[10,32,8,128]{3,2,1,0:T(8,128)}, f32[10,32,8,128]{3,2,1,0:T(8,128)S(1)}, u32[]{:S(2)}) %copy-start.6) | copy-done | bytes 1310744
  45.2 0.6 collective-permute-start.8
  45.8 2.4 %collective-permute-start.2 = (bf16[128,1024]{1,0:T(8,128)(2,1)}, bf16[128,1024]{1,0:T(8,128)(2,1)}, u32[]{:S(2)}, u32[]{:S(2)}) collective-permute-start(bf16[128,1024]{1,0:T(8,128)(2,1)} %copy-done.1), channel_id=1, source_target_pairs={{0,17},{1,18},{2,19},{3,16},{8,25},{9,26},{10,27},{11,24},{16,1},{... | collective-permute-start | bytes 786440 | tf_op jit(solution)/shard_map/ppermute | solution.py:376
  48.2 0.6 collective-permute-start.3
  48.8 1.3 %copy-done.7 = f32[10,32,8,128]{3,2,1,0:T(8,128)S(1)} copy-done((f32[10,32,8,128]{3,2,1,0:T(8,128)S(1)}, f32[10,32,8,128]{3,2,1,0:T(8,128)}, u32[]{:S(2)}) %copy-start.7) | copy-done | bytes 1310744
  50.2 1.3 %join.1 = bf16[32,10,8,128]{3,2,1,0:T(8,128)(2,1)} custom-call(f32[10,32,8,128]{3,2,1,0:T(8,128)S(1)} %copy-done.7, f32[10,32,8,128]{3,2,1,0:T(8,128)S(1)} %collective-permute-done.8.came_ref), custom_call_target="tpu_custom_call" | custom-call | flops 2000000000 | bytes 4194304 | tf_op jit(solution)/shard_map/join/pallas_call | solution.py:302
  51.4 7.9 %all-to-all-start.1 = ((bf16[32,10,8,128]{3,2,1,0:T(8,128)(2,1)}), bf16[32,10,8,128]{3,2,1,0:T(8,128)(2,1)S(1)}, u32[]{:S(2)}, u32[]{:S(2)}) async-start(bf16[32,10,8,128]{3,2,1,0:T(8,128)(2,1)} %join.1), calls=%async_computation.1 | async-start | bytes 1310720 | tf_op jit(solution)/shard_map/all_to_all | solution.py:396
  59.4 0.9 %dynamic-slice_bitcast_fusion.4.table_ref = bf16[8,4096]{1,0:T(8,128)(2,1)S(1)} fusion(bf16[1,512,4096]{2,1,0:T(8,128)(2,1)} %param.11, s32[]{:T(128)S(6)} %select_n.23), kind=kLoop, calls=%fused_computation.9 | loop fusion | bytes 131076 | tf_op jit(solution)/shard_map/dynamic_slice | solution.py:397
  60.2 2.3 %collective-permute-start.4 = (bf16[128,1024]{1,0:T(8,128)(2,1)S(1)}, bf16[128,1024]{1,0:T(8,128)(2,1)S(1)}, u32[]{:S(2)}, u32[]{:S(2)}) collective-permute-start(bf16[128,1024]{1,0:T(8,128)(2,1)S(1)} %get-tuple-element.26), channel_id=1, source_target_pairs={{0,9},{1,10},{2,11},{3,8},{8,17},{9,18},{10,19},{11,16},{16,25},{1... | collective-permute-start | bytes 786440 | tf_op jit(solution)/shard_map/ppermute | solution.py:376
  62.5 1.2 %collective-permute-start.5 = (bf16[128,1024]{1,0:T(8,128)(2,1)S(1)}, bf16[128,1024]{1,0:T(8,128)(2,1)S(1)}, u32[]{:S(2)}, u32[]{:S(2)}) collective-permute-start(bf16[128,1024]{1,0:T(8,128)(2,1)S(1)} %get-tuple-element.27), channel_id=1, source_target_pairs={{0,1},{1,2},{2,3},{3,0},{8,9},{9,10},{10,11},{11,8},{16,17},{17,18... | collective-permute-start | bytes 786440 | tf_op jit(solution)/shard_map/ppermute | solution.py:376
  63.8 0.1 broadcast_in_dim.33
  63.9 1.0 %bitcast_dynamic-update-slice_fusion.3 = bf16[1,128,4096]{2,1,0:T(8,128)(2,1)S(1)} fusion(bf16[1,128,4096]{2,1,0:T(8,128)(2,1)S(1)} %broadcast_in_dim.33, s32[]{:T(128)S(6)} %select_n.21, bf16[128,1024]{1,0:T(8,128)(2,1)} %collective-permute-done.2), kind=kLoop, calls=%fused_computation.3 | loop fusion | bytes 524292 | tf_op jit(solution)/shard_map/dynamic_update_slice | solution.py:394
  64.9 1.0 %bitcast_dynamic-update-slice_fusion.2 = bf16[1,128,4096]{2,1,0:T(8,128)(2,1)S(1)} fusion(bf16[1,128,4096]{2,1,0:T(8,128)(2,1)S(1)} %bitcast_dynamic-update-slice_fusion.3, s32[]{:T(128)S(6)} %select_n.20, bf16[128,1024]{1,0:T(8,128)(2,1)} %collective-permute-done.3), kind=kLoop, calls=%fused_computation.2 | loop fusion | bytes 524292 | tf_op jit(solution)/shard_map/dynamic_update_slice | solution.py:394
  65.8 7.8 %collective-permute-done.4 = bf16[128,1024]{1,0:T(8,128)(2,1)S(1)} collective-permute-done((bf16[128,1024]{1,0:T(8,128)(2,1)S(1)}, bf16[128,1024]{1,0:T(8,128)(2,1)S(1)}, u32[]{:S(2)}, u32[]{:S(2)}) %collective-permute-start.4) | collective-permute-done | bytes 262176 | tf_op jit(solution)/shard_map/ppermute | solution.py:376
  73.7 3.1 %collective-permute-done.5 = bf16[128,1024]{1,0:T(8,128)(2,1)S(1)} collective-permute-done((bf16[128,1024]{1,0:T(8,128)(2,1)S(1)}, bf16[128,1024]{1,0:T(8,128)(2,1)S(1)}, u32[]{:S(2)}, u32[]{:S(2)}) %collective-permute-start.5) | collective-permute-done | bytes 262176 | tf_op jit(solution)/shard_map/ppermute | solution.py:376
  76.8 1.3 %all-to-all-done.1.parts_ref = bf16[32,10,8,128]{3,2,1,0:T(8,128)(2,1)S(1)} async-done(((bf16[32,10,8,128]{3,2,1,0:T(8,128)(2,1)}), bf16[32,10,8,128]{3,2,1,0:T(8,128)(2,1)S(1)}, u32[]{:S(2)}, u32[]{:S(2)}) %all-to-all-start.1) | async-done | bytes 655392 | tf_op jit(solution)/shard_map/all_to_all | solution.py:396
  78.1 0.9 %finish.1 = (f32[1,8,4096]{2,1,0:T(8,128)}, f32[1,4096]{1,0:T(1,128)}, f32[1,32,64]{2,1,0:T(8,128)}) custom-call(bf16[32,10,8,128]{3,2,1,0:T(8,128)(2,1)S(1)} %all-to-all-done.1.parts_ref, bf16[8,4096]{1,0:T(8,128)(2,1)S(1)} %dynamic-slice_bitcast_fusion.4.table_ref, f32[512,128]{1,0:T(8,128)S(1)} %copy-done.12), custom_call_target="tpu_custom_call" | custom-call | flops 2000000000 | bytes 2097152 | tf_op jit(solution)/shard_map/finish/pallas_call | solution.py:348
  (38 shorter events, 0.2 us)
Async XLA Ops:
  0.6 24.0 %copy-start.5 = (f32[32,128]{1,0:T(8,128)S(1)}, f32[32,128]{1,0:T(8,128)}, u32[]{:S(2)}) copy-start(f32[32,128]{1,0:T(8,128)} %constant.62.picks_ref) | copy-start | bytes 49156
  0.6 7.1 %copy-start.14 = (s32[1,1,128]{2,1,0:T(1,128)S(1)}, s32[1,1,128]{2,1,0:T(1,128)}, u32[]{:S(2)}) copy-start(s32[1,1,128]{2,1,0:T(1,128)} %param.9) | copy-start | bytes 1540
  0.7 7.1 %copy-start.15 = (s32[1,1,128]{2,1,0:T(1,128)S(1)}, s32[1,1,128]{2,1,0:T(1,128)}, u32[]{:S(2)}) copy-start(s32[1,1,128]{2,1,0:T(1,128)} %param.8) | copy-start | bytes 1540
  0.7 24.0 %copy-start.3 = (f32[1,4096]{1,0:T(1,128)S(1)}, f32[1,4096]{1,0:T(1,128)}, u32[]{:S(2)}) copy-start(f32[1,4096]{1,0:T(1,128)} %gain_ref.3) | copy-start | bytes 49156
  0.7 24.0 %copy-start.2 = (f32[1,32,64]{2,1,0:T(8,128)S(1)}, f32[1,32,64]{2,1,0:T(8,128)}, u32[]{:S(2)}) copy-start(f32[1,32,64]{2,1,0:T(8,128)} %param.13) | copy-start | bytes 24580
  2.0 22.6 %collective-permute-start = (bf16[128,1024]{1,0:T(8,128)(2,1)S(1)}, bf16[128,1024]{1,0:T(8,128)(2,1)S(1)}, u32[]{:S(2)}, u32[]{:S(2)}) collective-permute-start(bf16[128,1024]{1,0:T(8,128)(2,1)S(1)} %get-tuple-element.40), channel_id=1, source_target_pairs={{0,3},{1,0},{2,1},{3,2},{8,11},{9,8},{10,9},{11,10},{16,19},{17,16... | collective-permute-start | bytes 786440 | tf_op jit(solution)/shard_map/ppermute | solution.py:376
  5.6 19.0 %collective-permute-start.1 = (bf16[128,1024]{1,0:T(8,128)(2,1)S(1)}, bf16[128,1024]{1,0:T(8,128)(2,1)S(1)}, u32[]{:S(2)}, u32[]{:S(2)}) collective-permute-start(bf16[128,1024]{1,0:T(8,128)(2,1)S(1)} %get-tuple-element.39), channel_id=1, source_target_pairs={{0,11},{1,8},{2,9},{3,10},{8,19},{9,16},{10,17},{11,18},{16,27},{1... | collective-permute-start | bytes 786440 | tf_op jit(solution)/shard_map/ppermute | solution.py:376
  8.6 23.5 %all-to-all-start = ((s32[64,3,128]{2,1,0:T(4,128)}), s32[64,3,128]{2,1,0:T(4,128)S(1)}, u32[]{:S(2)}, u32[]{:S(2)}) async-start(s32[64,3,128]{2,1,0:T(4,128)} %add_add_fusion), calls=%async_computation | async-start | bytes 262144 | tf_op jit(solution)/shard_map/all_to_all | solution.py:386
  21.0 17.5 %collective-permute-start.6 = (bf16[128,1024]{1,0:T(8,128)(2,1)S(1)}, bf16[128,1024]{1,0:T(8,128)(2,1)S(1)}, u32[]{:S(2)}, u32[]{:S(2)}) collective-permute-start(bf16[128,1024]{1,0:T(8,128)(2,1)S(1)} %get-tuple-element.41), channel_id=1, source_target_pairs={{0,19},{1,16},{2,17},{3,18},{8,27},{9,24},{10,25},{11,26},{16,3},{... | collective-permute-start | bytes 786440 | tf_op jit(solution)/shard_map/ppermute | solution.py:376
  23.8 14.7 %collective-permute-start.7 = (bf16[128,1024]{1,0:T(8,128)(2,1)S(1)}, bf16[128,1024]{1,0:T(8,128)(2,1)S(1)}, u32[]{:S(2)}, u32[]{:S(2)}) collective-permute-start(bf16[128,1024]{1,0:T(8,128)(2,1)S(1)} %get-tuple-element.38), channel_id=1, source_target_pairs={{0,27},{1,24},{2,25},{3,26},{8,3},{9,0},{10,1},{11,2},{16,11},{17,... | collective-permute-start | bytes 786440 | tf_op jit(solution)/shard_map/ppermute | solution.py:376
  24.6 2.2 %copy-start = (bf16[1,512,4096]{2,1,0:T(8,128)(2,1)S(1)}, bf16[1,512,4096]{2,1,0:T(8,128)(2,1)}, u32[]{:S(2)}) copy-start(bf16[1,512,4096]{2,1,0:T(8,128)(2,1)} %param.11) | copy-start | bytes 12582916
  28.3 1.4 %copy-start.8 = (bf16[512,2048]{1,0:T(8,128)(2,1)}, bf16[512,2048]{1,0:T(8,128)(2,1)S(1)}, u32[]{:S(2)}) copy-start(bf16[512,2048]{1,0:T(8,128)(2,1)S(1)} %get-tuple-element.22.ne_hbm.ne_ref) | copy-start | bytes 6291460
  29.7 8.8 %copy-start.11 = (f32[512,128]{1,0:T(8,128)}, f32[512,128]{1,0:T(8,128)S(1)}, u32[]{:S(2)}) copy-start(f32[512,128]{1,0:T(8,128)S(1)} %get-tuple-element.28.r_ref) | copy-start | bytes 786436
  32.1 1.6 %copy-start.9 = (bf16[512,2048]{1,0:T(8,128)(2,1)S(1)}, bf16[512,2048]{1,0:T(8,128)(2,1)}, u32[]{:S(2)}) copy-start(bf16[512,2048]{1,0:T(8,128)(2,1)} %copy-done.8) | copy-start | bytes 6291460
  33.7 4.8 %copy-start.4 = (f32[128,128]{1,0:T(8,128)S(1)}, f32[128,128]{1,0:T(8,128)}, u32[]{:S(2)}) copy-start(f32[128,128]{1,0:T(8,128)} %constant.54.clone.picks_ref) | copy-start | bytes 196612
  33.7 4.9 %copy-start.10 = (bf16[512,2048]{1,0:T(8,128)(2,1)S(1)}, bf16[512,2048]{1,0:T(8,128)(2,1)}, u32[]{:S(2)}) copy-start(bf16[512,2048]{1,0:T(8,128)(2,1)} %copy-done.8) | copy-start | bytes 6291460
  37.8 0.7 copy-start.1
  44.1 1.1 %copy-start.6 = (f32[10,32,8,128]{3,2,1,0:T(8,128)}, f32[10,32,8,128]{3,2,1,0:T(8,128)S(1)}, u32[]{:S(2)}) copy-start(f32[10,32,8,128]{3,2,1,0:T(8,128)S(1)} %get-tuple-element.33.mine_ref) | copy-start | bytes 3932164
  45.2 3.6 %collective-permute-start.8 = (f32[10,32,8,128]{3,2,1,0:T(8,128)S(1)}, f32[10,32,8,128]{3,2,1,0:T(8,128)S(1)}, u32[]{:S(2)}, u32[]{:S(2)}) collective-permute-start(f32[10,32,8,128]{3,2,1,0:T(8,128)S(1)} %get-tuple-element.34), channel_id=1, source_target_pairs={{0,4},{4,0},{1,5},{5,1},{2,6},{6,2},{3,7},{7,3},{8,12},{12,8},{9,1... | collective-permute-start | bytes 3932168 | tf_op jit(solution)/shard_map/ppermute | solution.py:391
  45.8 18.0 %collective-permute-start.2 = (bf16[128,1024]{1,0:T(8,128)(2,1)}, bf16[128,1024]{1,0:T(8,128)(2,1)}, u32[]{:S(2)}, u32[]{:S(2)}) collective-permute-start(bf16[128,1024]{1,0:T(8,128)(2,1)} %copy-done.1), channel_id=1, source_target_pairs={{0,17},{1,18},{2,19},{3,16},{8,25},{9,26},{10,27},{11,24},{16,1},{... | collective-permute-start | bytes 786440 | tf_op jit(solution)/shard_map/ppermute | solution.py:376
  48.2 16.7 %collective-permute-start.3 = (bf16[128,1024]{1,0:T(8,128)(2,1)S(1)}, bf16[128,1024]{1,0:T(8,128)(2,1)}, u32[]{:S(2)}, u32[]{:S(2)}) collective-permute-start(bf16[128,1024]{1,0:T(8,128)(2,1)S(1)} %get-tuple-element.25), channel_id=1, source_target_pairs={{0,25},{1,26},{2,27},{3,24},{8,1},{9,2},{10,3},{11,0},{16,9},{17,1... | collective-permute-start | bytes 786440 | tf_op jit(solution)/shard_map/ppermute | solution.py:376
  48.8 1.3 %copy-start.7 = (f32[10,32,8,128]{3,2,1,0:T(8,128)S(1)}, f32[10,32,8,128]{3,2,1,0:T(8,128)}, u32[]{:S(2)}) copy-start(f32[10,32,8,128]{3,2,1,0:T(8,128)} %copy-done.6) | copy-start | bytes 3932164
  51.4 26.7 %copy-start.12 = (f32[512,128]{1,0:T(8,128)S(1)}, f32[512,128]{1,0:T(8,128)}, u32[]{:S(2)}) copy-start(f32[512,128]{1,0:T(8,128)} %copy-done.11) | copy-start | bytes 786436
  51.4 26.7 %all-to-all-start.1 = ((bf16[32,10,8,128]{3,2,1,0:T(8,128)(2,1)}), bf16[32,10,8,128]{3,2,1,0:T(8,128)(2,1)S(1)}, u32[]{:S(2)}, u32[]{:S(2)}) async-start(bf16[32,10,8,128]{3,2,1,0:T(8,128)(2,1)} %join.1), calls=%async_computation.1 | async-start | bytes 1310720 | tf_op jit(solution)/shard_map/all_to_all | solution.py:396
  60.2 13.4 %collective-permute-start.4 = (bf16[128,1024]{1,0:T(8,128)(2,1)S(1)}, bf16[128,1024]{1,0:T(8,128)(2,1)S(1)}, u32[]{:S(2)}, u32[]{:S(2)}) collective-permute-start(bf16[128,1024]{1,0:T(8,128)(2,1)S(1)} %get-tuple-element.26), channel_id=1, source_target_pairs={{0,9},{1,10},{2,11},{3,8},{8,17},{9,18},{10,19},{11,16},{16,25},{1... | collective-permute-start | bytes 786440 | tf_op jit(solution)/shard_map/ppermute | solution.py:376
  62.5 14.2 %collective-permute-start.5 = (bf16[128,1024]{1,0:T(8,128)(2,1)S(1)}, bf16[128,1024]{1,0:T(8,128)(2,1)S(1)}, u32[]{:S(2)}, u32[]{:S(2)}) collective-permute-start(bf16[128,1024]{1,0:T(8,128)(2,1)S(1)} %get-tuple-element.27), channel_id=1, source_target_pairs={{0,1},{1,2},{2,3},{3,0},{8,9},{9,10},{10,11},{11,8},{16,17},{17,18... | collective-permute-start | bytes 786440 | tf_op jit(solution)/shard_map/ppermute | solution.py:376
  76.8 2.2 %copy-start.13 = (bf16[1,128,4096]{2,1,0:T(8,128)(2,1)}, bf16[1,128,4096]{2,1,0:T(8,128)(2,1)S(1)}, u32[]{:S(2)}) copy-start(bf16[1,128,4096]{2,1,0:T(8,128)(2,1)S(1)} %bitcast_dynamic-update-slice_fusion) | copy-start | bytes 3145732

commit v7 on v6

--- a/solution.py
+++ b/solution.py
@@ -382,8 +382,9 @@
     table_then, grads[0], grads[1] = lax.optimization_barrier((table, grads[0], grads[1]))
     ne, r, bvec = prepare(table_then, gain, pos, picks[:32])
     count = 64
-    note = [jnp.broadcast_to(v.reshape(1, 1, -1), (count, 1, L)) for v in (token_ids, segment_ids, row_order)]
-    notes = lax.all_to_all(jnp.concatenate(note, axis=1), ("z", "x", "c"), 0, 0)
+    kind = lax.broadcasted_iota(jnp.int32, (count, 3, L), 1)
+    note = jnp.where(kind == 0, token_ids, jnp.where(kind == 1, segment_ids, row_order[:, :, None]))
+    notes = lax.all_to_all(note, ("z", "x", "c"), 0, 0)
 
     *acts, normed, probs = forward(notes, ne, bvec)
     pieces = {s: send(acts[s], -s, 1) for s in (2, 1, 3, 0)}

time: 80.5 us -> 80.4 us (level)
  no operation moved by 1% of the time
where the time goes in v7:
time: 80.4 us; the launch traced here: 78.9 us
  starting transfers between devices  36.2 us (45%)
  waiting for transfers between devices  14.6 us (18%)
  Pallas kernels  13.3 us (17%)
  local copies, waits for them, and re-layouts  12.5 us (16%)
  between operations  1.54 us (2%)
    ppermute x8, starting transfers between devices, send(): return lax.ppermute(value, ('x', 'section'), pairs)  15.3 us
    all_to_all x1, starting transfers between devices, local(): notes = lax.all_to_all(note, ('z', 'x', 'c'), 0, 0)  12.4 us
    ppermute x8, waiting for transfers between devices, send(): return lax.ppermute(value, ('x', 'section'), pairs)  10.9 us
    unnamed x32, local copies, waits for them, and re-layouts  8.25 us
    all_to_all x1, starting transfers between devices, local(): parts = lax.all_to_all(join(mine, came), ('z', 'x'), 0, 0)  7.93 us
    pallas_call x1, Pallas kernels, backward(): pl.pallas_call(bwd_kernel, in_specs=[vmem] * (7 + NX), out_specs=[vmem, v...  5.58 us
    pallas_call x1, Pallas kernels, forward(): pl.pallas_call(fwd_kernel, in_specs=[vmem, hbm, hbm], out_specs=[vmem] *...  4.12 us
    all_to_all x1, waiting for transfers between devices, local(): notes = lax.all_to_all(note, ('z', 'x', 'c'), 0, 0)  2.41 us
  transfers between devices with their start and end apart: 11, of which 4 were waited for; matrix products, arithmetic and copies ran while one was open for 5% of the time, Pallas kernels for 9%

profile of v7, /device:TPU:1, one launch (start us, length us, event | category | flops | bytes accessed | tf_op | source)
XLA Modules:
  0.0 78.9 jit_solution(4242360969148782116)
XLA Ops:
  0.7 1.3 %dynamic-slice_bitcast_fusion = (bf16[128,1024]{1,0:T(8,128)(2,1)S(1)}, bf16[128,1024]{1,0:T(8,128)(2,1)S(1)}, bf16[128,1024]{1,0:T(8,128)(2,1)S(1)}, bf16[128,1024]{1,0:T(8,128)(2,1)S(1)}) fusion(bf16[1,128,4096]{2,1,0:T(8,128)(2,1)} %param.14, s32[]{:T(128)S(6)} %select_n.32, s32[]{:T(128)S(6)} %select_n.30, s32[]{:T(128)S(6)} %select_n.29, s32[]{:T(128)S(6)} %select_n.31), kind=kLoop, calls=%fused_computation.4 | loop fusion | bytes 2097168 | tf_op jit(solution)/shard_map/dynamic_slice | solution.py:379
  2.0 3.6 %collective-permute-start = (bf16[128,1024]{1,0:T(8,128)(2,1)S(1)}, bf16[128,1024]{1,0:T(8,128)(2,1)S(1)}, u32[]{:S(2)}, u32[]{:S(2)}) collective-permute-start(bf16[128,1024]{1,0:T(8,128)(2,1)S(1)} %get-tuple-element.40), channel_id=1, source_target_pairs={{0,3},{1,0},{2,1},{3,2},{8,11},{9,8},{10,9},{11,10},{16,19},{17,16... | collective-permute-start | bytes 786440 | tf_op jit(solution)/shard_map/ppermute | solution.py:376
  5.6 1.4 %collective-permute-start.1 = (bf16[128,1024]{1,0:T(8,128)(2,1)S(1)}, bf16[128,1024]{1,0:T(8,128)(2,1)S(1)}, u32[]{:S(2)}, u32[]{:S(2)}) collective-permute-start(bf16[128,1024]{1,0:T(8,128)(2,1)S(1)} %get-tuple-element.39), channel_id=1, source_target_pairs={{0,11},{1,8},{2,9},{3,10},{8,19},{9,16},{10,17},{11,18},{16,27},{1... | collective-permute-start | bytes 786440 | tf_op jit(solution)/shard_map/ppermute | solution.py:376
  7.7 0.7 select_select_fusion
  8.4 12.4 %all-to-all-start = ((s32[64,3,128]{2,1,0:T(4,128)}), s32[64,3,128]{2,1,0:T(4,128)S(1)}, u32[]{:S(2)}, u32[]{:S(2)}) async-start(s32[64,3,128]{2,1,0:T(4,128)} %select_select_fusion), calls=%async_computation | async-start | bytes 262144 | tf_op jit(solution)/shard_map/all_to_all | solution.py:387
  20.9 2.9 %collective-permute-start.6 = (bf16[128,1024]{1,0:T(8,128)(2,1)S(1)}, bf16[128,1024]{1,0:T(8,128)(2,1)S(1)}, u32[]{:S(2)}, u32[]{:S(2)}) collective-permute-start(bf16[128,1024]{1,0:T(8,128)(2,1)S(1)} %get-tuple-element.41), channel_id=1, source_target_pairs={{0,19},{1,16},{2,17},{3,18},{8,27},{9,24},{10,25},{11,26},{16,3},{... | collective-permute-start | bytes 786440 | tf_op jit(solution)/shard_map/ppermute | solution.py:376
  23.7 0.8 collective-permute-start.7
  24.5 2.2 %copy-done = bf16[1,512,4096]{2,1,0:T(8,128)(2,1)S(1)} copy-done((bf16[1,512,4096]{2,1,0:T(8,128)(2,1)S(1)}, bf16[1,512,4096]{2,1,0:T(8,128)(2,1)}, u32[]{:S(2)}) %copy-start) | copy-done | bytes 4194328
  26.7 1.5 %prepare.1 = (bf16[512,2048]{1,0:T(8,128)(2,1)S(1)}, f32[512,128]{1,0:T(8,128)S(1)}, f32[64,128]{1,0:T(8,128)S(1)}) custom-call(bf16[512,4096]{1,0:T(8,128)(2,1)S(1)} %bitcast.24, f32[1,4096]{1,0:T(1,128)S(1)} %copy-done.3, f32[32,64]{1,0:T(8,128)S(1)} %bitcast.25, f32[32,128]{1,0:T(8,128)S(1)} %copy-done.5), custom_call_target="tpu_custom_call" | custom-call | flops 5000000000 | bytes 7340032 | tf_op jit(solution)/shard_map/prepare/pallas_call | solution.py:80
  28.2 1.3 %copy-done.8 = bf16[512,2048]{1,0:T(8,128)(2,1)} copy-done((bf16[512,2048]{1,0:T(8,128)(2,1)}, bf16[512,2048]{1,0:T(8,128)(2,1)S(1)}, u32[]{:S(2)}) %copy-start.8) | copy-done | bytes 2097176
  29.6 2.4 %all-to-all-done.notes_ref = s32[64,3,128]{2,1,0:T(4,128)S(1)} async-done(((s32[64,3,128]{2,1,0:T(4,128)}), s32[64,3,128]{2,1,0:T(4,128)S(1)}, u32[]{:S(2)}, u32[]{:S(2)}) %all-to-all-start) | async-done | bytes 98336 | tf_op jit(solution)/shard_map/all_to_all | solution.py:387
  32.0 1.6 %copy-done.9 = bf16[512,2048]{1,0:T(8,128)(2,1)S(1)} copy-done((bf16[512,2048]{1,0:T(8,128)(2,1)S(1)}, bf16[512,2048]{1,0:T(8,128)(2,1)}, u32[]{:S(2)}) %copy-start.9) | copy-done | bytes 2097176
  33.6 4.1 %forward.1 = (bf16[128,1024]{1,0:T(8,128)(2,1)S(1)}, bf16[128,1024]{1,0:T(8,128)(2,1)S(1)}, bf16[128,1024]{1,0:T(8,128)(2,1)S(1)}, bf16[128,1024]{1,0:T(8,128)(2...) custom-call(s32[64,3,128]{2,1,0:T(4,128)S(1)} %all-to-all-done.notes_ref, ...), custom_call_target="tpu_custom_call" | custom-call | flops 8000000000 | bytes 7340032 | tf_op jit(solution)/shard_map/forward/pallas_call | solution.py:176
  37.7 0.7 copy-done.1
  38.4 5.6 %backward.1 = (f32[10,32,8,128]{3,2,1,0:T(8,128)S(1)}, f32[10,32,8,128]{3,2,1,0:T(8,128)S(1)}) custom-call(s32[64,3,128]{2,1,0:T(4,128)S(1)} %all-to-all-done.notes_ref, bf16[512,2048]{1,0:T(8,128)(2,1)S(1)} %copy-done.10, f32[512,128]{1,0:T(8,128)S(1)} %get-tuple-element.28.r_ref, f32[1,4096]{1,0:T(1,128)S(1)} %copy-done.3, f32[128,128]{1,0:T(8,128)S(1)} %copy-done.4, ...), custom_call_target="tpu_custom_call" | custom-call | flops 10000000000 | bytes 10485760 | tf_op jit(solution)/shard_map/backward/pallas_call | solution.py:267
  44.0 1.1 %copy-done.6 = f32[10,32,8,128]{3,2,1,0:T(8,128)} copy-done((f32[10,32,8,128]{3,2,1,0:T(8,128)}, f32[10,32,8,128]{3,2,1,0:T(8,128)S(1)}, u32[]{:S(2)}) %copy-start.6) | copy-done | bytes 1310744
  45.1 0.6 collective-permute-start.8
  45.7 2.4 %collective-permute-start.2 = (bf16[128,1024]{1,0:T(8,128)(2,1)}, bf16[128,1024]{1,0:T(8,128)(2,1)}, u32[]{:S(2)}, u32[]{:S(2)}) collective-permute-start(bf16[128,1024]{1,0:T(8,128)(2,1)} %copy-done.1), channel_id=1, source_target_pairs={{0,17},{1,18},{2,19},{3,16},{8,25},{9,26},{10,27},{11,24},{16,1},{... | collective-permute-start | bytes 786440 | tf_op jit(solution)/shard_map/ppermute | solution.py:376
  48.1 0.6 collective-permute-start.3
  48.7 1.3 %copy-done.7 = f32[10,32,8,128]{3,2,1,0:T(8,128)S(1)} copy-done((f32[10,32,8,128]{3,2,1,0:T(8,128)S(1)}, f32[10,32,8,128]{3,2,1,0:T(8,128)}, u32[]{:S(2)}) %copy-start.7) | copy-done | bytes 1310744
  50.0 1.3 %join.1 = bf16[32,10,8,128]{3,2,1,0:T(8,128)(2,1)} custom-call(f32[10,32,8,128]{3,2,1,0:T(8,128)S(1)} %copy-done.7, f32[10,32,8,128]{3,2,1,0:T(8,128)S(1)} %collective-permute-done.8.came_ref), custom_call_target="tpu_custom_call" | custom-call | flops 2000000000 | bytes 4194304 | tf_op jit(solution)/shard_map/join/pallas_call | solution.py:302
  51.3 7.9 %all-to-all-start.1 = ((bf16[32,10,8,128]{3,2,1,0:T(8,128)(2,1)}), bf16[32,10,8,128]{3,2,1,0:T(8,128)(2,1)S(1)}, u32[]{:S(2)}, u32[]{:S(2)}) async-start(bf16[32,10,8,128]{3,2,1,0:T(8,128)(2,1)} %join.1), calls=%async_computation.1 | async-start | bytes 1310720 | tf_op jit(solution)/shard_map/all_to_all | solution.py:397
  59.2 0.9 %dynamic-slice_bitcast_fusion.4.table_ref = bf16[8,4096]{1,0:T(8,128)(2,1)S(1)} fusion(bf16[1,512,4096]{2,1,0:T(8,128)(2,1)} %param.11, s32[]{:T(128)S(6)} %select_n.33), kind=kLoop, calls=%fused_computation.9 | loop fusion | bytes 131076 | tf_op jit(solution)/shard_map/dynamic_slice | solution.py:398
  60.1 2.3 %collective-permute-start.4 = (bf16[128,1024]{1,0:T(8,128)(2,1)S(1)}, bf16[128,1024]{1,0:T(8,128)(2,1)S(1)}, u32[]{:S(2)}, u32[]{:S(2)}) collective-permute-start(bf16[128,1024]{1,0:T(8,128)(2,1)S(1)} %get-tuple-element.26), channel_id=1, source_target_pairs={{0,9},{1,10},{2,11},{3,8},{8,17},{9,18},{10,19},{11,16},{16,25},{1... | collective-permute-start | bytes 786440 | tf_op jit(solution)/shard_map/ppermute | solution.py:376
  62.4 1.2 %collective-permute-start.5 = (bf16[128,1024]{1,0:T(8,128)(2,1)S(1)}, bf16[128,1024]{1,0:T(8,128)(2,1)S(1)}, u32[]{:S(2)}, u32[]{:S(2)}) collective-permute-start(bf16[128,1024]{1,0:T(8,128)(2,1)S(1)} %get-tuple-element.27), channel_id=1, source_target_pairs={{0,1},{1,2},{2,3},{3,0},{8,9},{9,10},{10,11},{11,8},{16,17},{17,18... | collective-permute-start | bytes 786440 | tf_op jit(solution)/shard_map/ppermute | solution.py:376
  63.7 0.1 broadcast_in_dim.43
  63.8 1.0 %bitcast_dynamic-update-slice_fusion.3 = bf16[1,128,4096]{2,1,0:T(8,128)(2,1)S(1)} fusion(bf16[1,128,4096]{2,1,0:T(8,128)(2,1)S(1)} %broadcast_in_dim.43, s32[]{:T(128)S(6)} %select_n.31, bf16[128,1024]{1,0:T(8,128)(2,1)} %collective-permute-done.2), kind=kLoop, calls=%fused_computation.3 | loop fusion | bytes 524292 | tf_op jit(solution)/shard_map/dynamic_update_slice | solution.py:395
  64.8 1.0 %bitcast_dynamic-update-slice_fusion.2 = bf16[1,128,4096]{2,1,0:T(8,128)(2,1)S(1)} fusion(bf16[1,128,4096]{2,1,0:T(8,128)(2,1)S(1)} %bitcast_dynamic-update-slice_fusion.3, s32[]{:T(128)S(6)} %select_n.30, bf16[128,1024]{1,0:T(8,128)(2,1)} %collective-permute-done.3), kind=kLoop, calls=%fused_computation.2 | loop fusion | bytes 524292 | tf_op jit(solution)/shard_map/dynamic_update_slice | solution.py:395
  65.7 7.9 %collective-permute-done.4 = bf16[128,1024]{1,0:T(8,128)(2,1)S(1)} collective-permute-done((bf16[128,1024]{1,0:T(8,128)(2,1)S(1)}, bf16[128,1024]{1,0:T(8,128)(2,1)S(1)}, u32[]{:S(2)}, u32[]{:S(2)}) %collective-permute-start.4) | collective-permute-done | bytes 262176 | tf_op jit(solution)/shard_map/ppermute | solution.py:376
  73.6 3.0 %collective-permute-done.5 = bf16[128,1024]{1,0:T(8,128)(2,1)S(1)} collective-permute-done((bf16[128,1024]{1,0:T(8,128)(2,1)S(1)}, bf16[128,1024]{1,0:T(8,128)(2,1)S(1)}, u32[]{:S(2)}, u32[]{:S(2)}) %collective-permute-start.5) | collective-permute-done | bytes 262176 | tf_op jit(solution)/shard_map/ppermute | solution.py:376
  76.7 1.3 %all-to-all-done.1.parts_ref = bf16[32,10,8,128]{3,2,1,0:T(8,128)(2,1)S(1)} async-done(((bf16[32,10,8,128]{3,2,1,0:T(8,128)(2,1)}), bf16[32,10,8,128]{3,2,1,0:T(8,128)(2,1)S(1)}, u32[]{:S(2)}, u32[]{:S(2)}) %all-to-all-start.1) | async-done | bytes 655392 | tf_op jit(solution)/shard_map/all_to_all | solution.py:397
  78.0 0.9 %finish.1 = (f32[1,8,4096]{2,1,0:T(8,128)}, f32[1,4096]{1,0:T(1,128)}, f32[1,32,64]{2,1,0:T(8,128)}) custom-call(bf16[32,10,8,128]{3,2,1,0:T(8,128)(2,1)S(1)} %all-to-all-done.1.parts_ref, bf16[8,4096]{1,0:T(8,128)(2,1)S(1)} %dynamic-slice_bitcast_fusion.4.table_ref, f32[512,128]{1,0:T(8,128)S(1)} %copy-done.12), custom_call_target="tpu_custom_call" | custom-call | flops 2000000000 | bytes 2097152 | tf_op jit(solution)/shard_map/finish/pallas_call | solution.py:348
  (36 shorter events, 0.1 us)
Async XLA Ops:
  0.6 23.9 %copy-start.5 = (f32[32,128]{1,0:T(8,128)S(1)}, f32[32,128]{1,0:T(8,128)}, u32[]{:S(2)}) copy-start(f32[32,128]{1,0:T(8,128)} %constant.64.picks_ref) | copy-start | bytes 49156
  0.6 7.0 %copy-start.14 = (s32[1,1,128]{2,1,0:T(1,128)S(1)}, s32[1,1,128]{2,1,0:T(1,128)}, u32[]{:S(2)}) copy-start(s32[1,1,128]{2,1,0:T(1,128)} %param.9) | copy-start | bytes 1540
  0.7 7.0 %copy-start.15 = (s32[1,1,128]{2,1,0:T(1,128)S(1)}, s32[1,1,128]{2,1,0:T(1,128)}, u32[]{:S(2)}) copy-start(s32[1,1,128]{2,1,0:T(1,128)} %param.8) | copy-start | bytes 1540
  0.7 23.9 %copy-start.3 = (f32[1,4096]{1,0:T(1,128)S(1)}, f32[1,4096]{1,0:T(1,128)}, u32[]{:S(2)}) copy-start(f32[1,4096]{1,0:T(1,128)} %gain_ref.3) | copy-start | bytes 49156
  0.7 23.9 %copy-start.2 = (f32[1,32,64]{2,1,0:T(8,128)S(1)}, f32[1,32,64]{2,1,0:T(8,128)}, u32[]{:S(2)}) copy-start(f32[1,32,64]{2,1,0:T(8,128)} %param.13) | copy-start | bytes 24580
  2.0 22.5 %collective-permute-start = (bf16[128,1024]{1,0:T(8,128)(2,1)S(1)}, bf16[128,1024]{1,0:T(8,128)(2,1)S(1)}, u32[]{:S(2)}, u32[]{:S(2)}) collective-permute-start(bf16[128,1024]{1,0:T(8,128)(2,1)S(1)} %get-tuple-element.40), channel_id=1, source_target_pairs={{0,3},{1,0},{2,1},{3,2},{8,11},{9,8},{10,9},{11,10},{16,19},{17,16... | collective-permute-start | bytes 786440 | tf_op jit(solution)/shard_map/ppermute | solution.py:376
  5.6 18.9 %collective-permute-start.1 = (bf16[128,1024]{1,0:T(8,128)(2,1)S(1)}, bf16[128,1024]{1,0:T(8,128)(2,1)S(1)}, u32[]{:S(2)}, u32[]{:S(2)}) collective-permute-start(bf16[128,1024]{1,0:T(8,128)(2,1)S(1)} %get-tuple-element.39), channel_id=1, source_target_pairs={{0,11},{1,8},{2,9},{3,10},{8,19},{9,16},{10,17},{11,18},{16,27},{1... | collective-permute-start | bytes 786440 | tf_op jit(solution)/shard_map/ppermute | solution.py:376
  8.4 23.5 %all-to-all-start = ((s32[64,3,128]{2,1,0:T(4,128)}), s32[64,3,128]{2,1,0:T(4,128)S(1)}, u32[]{:S(2)}, u32[]{:S(2)}) async-start(s32[64,3,128]{2,1,0:T(4,128)} %select_select_fusion), calls=%async_computation | async-start | bytes 262144 | tf_op jit(solution)/shard_map/all_to_all | solution.py:387
  20.9 17.5 %collective-permute-start.6 = (bf16[128,1024]{1,0:T(8,128)(2,1)S(1)}, bf16[128,1024]{1,0:T(8,128)(2,1)S(1)}, u32[]{:S(2)}, u32[]{:S(2)}) collective-permute-start(bf16[128,1024]{1,0:T(8,128)(2,1)S(1)} %get-tuple-element.41), channel_id=1, source_target_pairs={{0,19},{1,16},{2,17},{3,18},{8,27},{9,24},{10,25},{11,26},{16,3},{... | collective-permute-start | bytes 786440 | tf_op jit(solution)/shard_map/ppermute | solution.py:376
  23.7 14.7 %collective-permute-start.7 = (bf16[128,1024]{1,0:T(8,128)(2,1)S(1)}, bf16[128,1024]{1,0:T(8,128)(2,1)S(1)}, u32[]{:S(2)}, u32[]{:S(2)}) collective-permute-start(bf16[128,1024]{1,0:T(8,128)(2,1)S(1)} %get-tuple-element.38), channel_id=1, source_target_pairs={{0,27},{1,24},{2,25},{3,26},{8,3},{9,0},{10,1},{11,2},{16,11},{17,... | collective-permute-start | bytes 786440 | tf_op jit(solution)/shard_map/ppermute | solution.py:376
  24.5 2.2 %copy-start = (bf16[1,512,4096]{2,1,0:T(8,128)(2,1)S(1)}, bf16[1,512,4096]{2,1,0:T(8,128)(2,1)}, u32[]{:S(2)}) copy-start(bf16[1,512,4096]{2,1,0:T(8,128)(2,1)} %param.11) | copy-start | bytes 12582916
  28.2 1.4 %copy-start.8 = (bf16[512,2048]{1,0:T(8,128)(2,1)}, bf16[512,2048]{1,0:T(8,128)(2,1)S(1)}, u32[]{:S(2)}) copy-start(bf16[512,2048]{1,0:T(8,128)(2,1)S(1)} %get-tuple-element.22.ne_hbm.ne_ref) | copy-start | bytes 6291460
  29.6 8.8 %copy-start.11 = (f32[512,128]{1,0:T(8,128)}, f32[512,128]{1,0:T(8,128)S(1)}, u32[]{:S(2)}) copy-start(f32[512,128]{1,0:T(8,128)S(1)} %get-tuple-element.28.r_ref) | copy-start | bytes 786436
  32.0 1.6 %copy-start.9 = (bf16[512,2048]{1,0:T(8,128)(2,1)S(1)}, bf16[512,2048]{1,0:T(8,128)(2,1)}, u32[]{:S(2)}) copy-start(bf16[512,2048]{1,0:T(8,128)(2,1)} %copy-done.8) | copy-start | bytes 6291460
  33.6 4.8 %copy-start.4 = (f32[128,128]{1,0:T(8,128)S(1)}, f32[128,128]{1,0:T(8,128)}, u32[]{:S(2)}) copy-start(f32[128,128]{1,0:T(8,128)} %constant.56.clone.picks_ref) | copy-start | bytes 196612
  33.6 4.9 %copy-start.10 = (bf16[512,2048]{1,0:T(8,128)(2,1)S(1)}, bf16[512,2048]{1,0:T(8,128)(2,1)}, u32[]{:S(2)}) copy-start(bf16[512,2048]{1,0:T(8,128)(2,1)} %copy-done.8) | copy-start | bytes 6291460
  37.7 0.7 copy-start.1
  44.0 1.1 %copy-start.6 = (f32[10,32,8,128]{3,2,1,0:T(8,128)}, f32[10,32,8,128]{3,2,1,0:T(8,128)S(1)}, u32[]{:S(2)}) copy-start(f32[10,32,8,128]{3,2,1,0:T(8,128)S(1)} %get-tuple-element.33.mine_ref) | copy-start | bytes 3932164
  45.1 3.6 %collective-permute-start.8 = (f32[10,32,8,128]{3,2,1,0:T(8,128)S(1)}, f32[10,32,8,128]{3,2,1,0:T(8,128)S(1)}, u32[]{:S(2)}, u32[]{:S(2)}) collective-permute-start(f32[10,32,8,128]{3,2,1,0:T(8,128)S(1)} %get-tuple-element.34), channel_id=1, source_target_pairs={{0,4},{4,0},{1,5},{5,1},{2,6},{6,2},{3,7},{7,3},{8,12},{12,8},{9,1... | collective-permute-start | bytes 3932168 | tf_op jit(solution)/shard_map/ppermute | solution.py:392
  45.7 18.0 %collective-permute-start.2 = (bf16[128,1024]{1,0:T(8,128)(2,1)}, bf16[128,1024]{1,0:T(8,128)(2,1)}, u32[]{:S(2)}, u32[]{:S(2)}) collective-permute-start(bf16[128,1024]{1,0:T(8,128)(2,1)} %copy-done.1), channel_id=1, source_target_pairs={{0,17},{1,18},{2,19},{3,16},{8,25},{9,26},{10,27},{11,24},{16,1},{... | collective-permute-start | bytes 786440 | tf_op jit(solution)/shard_map/ppermute | solution.py:376
  48.1 16.7 %collective-permute-start.3 = (bf16[128,1024]{1,0:T(8,128)(2,1)S(1)}, bf16[128,1024]{1,0:T(8,128)(2,1)}, u32[]{:S(2)}, u32[]{:S(2)}) collective-permute-start(bf16[128,1024]{1,0:T(8,128)(2,1)S(1)} %get-tuple-element.25), channel_id=1, source_target_pairs={{0,25},{1,26},{2,27},{3,24},{8,1},{9,2},{10,3},{11,0},{16,9},{17,1... | collective-permute-start | bytes 786440 | tf_op jit(solution)/shard_map/ppermute | solution.py:376
  48.7 1.3 %copy-start.7 = (f32[10,32,8,128]{3,2,1,0:T(8,128)S(1)}, f32[10,32,8,128]{3,2,1,0:T(8,128)}, u32[]{:S(2)}) copy-start(f32[10,32,8,128]{3,2,1,0:T(8,128)} %copy-done.6) | copy-start | bytes 3932164
  51.3 26.7 %copy-start.12 = (f32[512,128]{1,0:T(8,128)S(1)}, f32[512,128]{1,0:T(8,128)}, u32[]{:S(2)}) copy-start(f32[512,128]{1,0:T(8,128)} %copy-done.11) | copy-start | bytes 786436
  51.3 26.7 %all-to-all-start.1 = ((bf16[32,10,8,128]{3,2,1,0:T(8,128)(2,1)}), bf16[32,10,8,128]{3,2,1,0:T(8,128)(2,1)S(1)}, u32[]{:S(2)}, u32[]{:S(2)}) async-start(bf16[32,10,8,128]{3,2,1,0:T(8,128)(2,1)} %join.1), calls=%async_computation.1 | async-start | bytes 1310720 | tf_op jit(solution)/shard_map/all_to_all | solution.py:397
  60.1 13.5 %collective-permute-start.4 = (bf16[128,1024]{1,0:T(8,128)(2,1)S(1)}, bf16[128,1024]{1,0:T(8,128)(2,1)S(1)}, u32[]{:S(2)}, u32[]{:S(2)}) collective-permute-start(bf16[128,1024]{1,0:T(8,128)(2,1)S(1)} %get-tuple-element.26), channel_id=1, source_target_pairs={{0,9},{1,10},{2,11},{3,8},{8,17},{9,18},{10,19},{11,16},{16,25},{1... | collective-permute-start | bytes 786440 | tf_op jit(solution)/shard_map/ppermute | solution.py:376
  62.4 14.2 %collective-permute-start.5 = (bf16[128,1024]{1,0:T(8,128)(2,1)S(1)}, bf16[128,1024]{1,0:T(8,128)(2,1)S(1)}, u32[]{:S(2)}, u32[]{:S(2)}) collective-permute-start(bf16[128,1024]{1,0:T(8,128)(2,1)S(1)} %get-tuple-element.27), channel_id=1, source_target_pairs={{0,1},{1,2},{2,3},{3,0},{8,9},{9,10},{10,11},{11,8},{16,17},{17,18... | collective-permute-start | bytes 786440 | tf_op jit(solution)/shard_map/ppermute | solution.py:376
  76.7 2.2 %copy-start.13 = (bf16[1,128,4096]{2,1,0:T(8,128)(2,1)}, bf16[1,128,4096]{2,1,0:T(8,128)(2,1)S(1)}, u32[]{:S(2)}) copy-start(bf16[1,128,4096]{2,1,0:T(8,128)(2,1)S(1)} %bitcast_dynamic-update-slice_fusion) | copy-start | bytes 3145732

commit v8 on v7

--- a/solution.py
+++ b/solution.py
@@ -197,7 +197,7 @@
 
 def bwd_kernel(notes_ref, ne_ref, r_ref, gain_ref, picks_ref, n_ref, p_ref, *rest):
     g_refs, (mine_ref, other_ref), rest = rest[:NX], rest[NX : NX + 2], rest[NX + 2 :]
-    d_ref, rg_ref, o_ref, diag_ref = rest
+    d_ref, rg_ref, o_ref, diag_ref, rows_ref = rest
     vocab, part = ne_ref.shape[0], ne_ref.shape[1] // 2
     pairs = part // L
     blocks = vocab // 16
@@ -233,8 +233,8 @@
     def put(tile, value):
         value = value.reshape(blocks, 2, 8, L)
         first, second = value[:, 0], value[:, 1]
-        mine_ref[tile] = jnp.where(core == 0, first, second)
-        other_ref[tile] = jnp.where(core == 0, second, first)
+        mine_ref[tile] = jnp.where(core == 0, first, second).astype(BF16)
+        other_ref[tile] = jnp.where(core == 0, second, first).astype(BF16)
 
     r = r_ref[...]
     along = jnp.zeros((vocab, L), F32)
@@ -247,15 +247,15 @@
         scaled = d_norm * r
         put(f, d_act + scaled * gain)
         along = along + own * (d_norm * gain)
-        g_row = jnp.sum(own * scaled, axis=0, keepdims=True)
-        for ref in (mine_ref, other_ref):
-            ref[pairs + 1, 0, pl.ds(f, 1), :] = g_row
+        rows_ref[pl.ds(f, 1), :] = jnp.sum(own * scaled, axis=0, keepdims=True)
     put(pairs, along)
     sums = dot(diag_ref[...], picks_ref[...], NT, lax.Precision.HIGHEST)
     for ref in (mine_ref, other_ref):
-        ref[pairs + 1, 1] = sums[:8]
-        ref[pairs + 1, 2] = sums[8:]
-        ref[pairs + 1, 3:] = jnp.zeros((blocks - 3, 8, L), F32)
+        for k, value in enumerate((rows_ref[...], sums[:8], sums[8:])):
+            high = value.astype(BF16)
+            ref[pairs + 1, k] = high
+            ref[pairs + 1, k + 3] = (value - high.astype(F32)).astype(BF16)
+        ref[pairs + 1, 6:] = jnp.zeros((blocks - 6, 8, L), BF16)
 
 
 def backward(notes, ne, r, gain, picks, n, probs, grads):
@@ -263,7 +263,7 @@
     pairs = part // L
     vmem = pl.BlockSpec(memory_space=pltpu.VMEM)
     stacked = (pairs + 2, vocab // 16, 8, L)
-    out = jax.ShapeDtypeStruct(stacked, F32)
+    out = jax.ShapeDtypeStruct(stacked, BF16)
     return pl.pallas_call(
         bwd_kernel,
         in_specs=[vmem] * (7 + NX),
@@ -274,6 +274,7 @@
             pltpu.VMEM((NX * L, part), BF16),
             pltpu.VMEM((vocab, NX * L), BF16),
             pltpu.VMEM((2 * pairs, L), F32),
+            pltpu.VMEM((8, L), F32),
         ],
         compiler_params=pltpu.CompilerParams(vmem_limit_bytes=24 * MIB),
         cost_estimate=cost(10, 10),
@@ -284,13 +285,14 @@
 def join_kernel(mine_ref, came_ref, out_ref):
     tiles, blocks = mine_ref.shape[0] - 2, mine_ref.shape[1]
     for t in range(tiles):
-        out_ref[:, t] = (mine_ref[t] + came_ref[t]).astype(BF16)
-    sums = [mine_ref[tiles + 1, t] + came_ref[tiles + 1, t] for t in range(3)]
+        out_ref[:, t] = (mine_ref[t].astype(F32) + came_ref[t].astype(F32)).astype(BF16)
+    both = [mine_ref[tiles + 1, t].astype(F32) + came_ref[tiles + 1, t].astype(F32) for t in range(6)]
+    sums = [both[t] + both[t + 3] for t in range(3)]
     out_ref[:, tiles] = jnp.broadcast_to(sums[0].astype(BF16)[None], (blocks, 8, L))
     bias = sums[1] + pltpu.roll(sums[2], 32, 1)
     lane = lax.broadcasted_iota(jnp.int32, (8, L), 1)
     for d in range(blocks):
-        along = jnp.sum(mine_ref[tiles, d] + came_ref[tiles, d], axis=1, keepdims=True)
+        along = jnp.sum(mine_ref[tiles, d].astype(F32) + came_ref[tiles, d].astype(F32), axis=1, keepdims=True)
         value = jnp.where(lane == 16, along, bias)
         high = value.astype(BF16).astype(F32)
         out_ref[d, tiles + 1] = (high + pltpu.roll(value - high, 64, 1)).astype(BF16)

time: 80.4 us -> 80.7 us (level)
  waiting for transfers between devices: 14.6 us -> 11.2 us
  local copies, waits for them, and re-layouts: 12.5 us -> 15.3 us
    all_to_all x1, waiting for transfers between devices: 2.41 us -> 0.3 us  [local(): notes = lax.all_to_all(note, ('z', 'x', 'c'), 0, 0)]
    all_to_all x1, starting transfers between devices: 7.93 us -> 6.89 us  [local(): parts = lax.all_to_all(join(mine, came), ('z', 'x'), 0, 0)]
    ppermute x8, waiting for transfers between devices: 10.9 us -> 9.86 us  [send(): return lax.ppermute(value, ('x', 'section'), pairs)]
    broadcast_in_dim x1, local copies, waits for them, and re-layouts: 0.1 us -> 1.07 us  [local(): return (handed[None],) + tuple(finish(parts, rows, r))]
    unnamed x32 -> x22, local copies, waits for them, and re-layouts: 8.25 us -> 9.19 us
    ppermute x8, starting transfers between devices: 15.3 us -> 16.2 us  [send(): return lax.ppermute(value, ('x', 'section'), pairs)]
    dynamic_update_slice x4, local copies, waits for them, and re-layouts: 1.99 us -> 2.88 us  [local(): lax.dynamic_update_slice(handed, pieces[s], (0, lax.rem(x + s, NX) * part))]
  transfers between devices with their start and end apart: 11 -> 11, of which waited for: 4 -> 4; matrix products, arithmetic and copies ran while one was open for 5% -> 8% of each run, Pallas kernels for 9% -> 9%
where the time goes in v8:
time: 80.7 us; the launch traced here: 79.2 us
  starting transfers between devices  36.5 us (45%)
  local copies, waits for them, and re-layouts  15.3 us (19%)
  Pallas kernels  13.4 us (17%)
  waiting for transfers between devices  11.2 us (14%)
  other arithmetic  1.42 us (2%)
  between operations  1.41 us (2%)
    ppermute x8, starting transfers between devices, send(): return lax.ppermute(value, ('x', 'section'), pairs)  16.2 us
    all_to_all x1, starting transfers between devices, local(): notes = lax.all_to_all(note, ('z', 'x', 'c'), 0, 0)  12.4 us
    ppermute x8, waiting for transfers between devices, send(): return lax.ppermute(value, ('x', 'section'), pairs)  9.86 us
    unnamed x22, local copies, waits for them, and re-layouts  9.19 us
    all_to_all x1, starting transfers between devices, local(): parts = lax.all_to_all(join(mine, came), ('z', 'x'), 0, 0)  6.89 us
    pallas_call x1, Pallas kernels, backward(): pl.pallas_call(bwd_kernel, in_specs=[vmem] * (7 + NX), out_specs=[vmem, v...  5.58 us
    pallas_call x1, Pallas kernels, forward(): pl.pallas_call(fwd_kernel, in_specs=[vmem, hbm, hbm], out_specs=[vmem] *...  4.11 us
    dynamic_update_slice x4, local copies, waits for them, and re-layouts, local(): lax.dynamic_update_slice(handed, pieces[s], (0, lax.rem(x + s, NX) * part))  2.88 us
  transfers between devices with their start and end apart: 11, of which 4 were waited for; matrix products, arithmetic and copies ran while one was open for 8% of the time, Pallas kernels for 9%

profile of v8, /device:TPU:1, one launch (start us, length us, event | category | flops | bytes accessed | tf_op | source)
XLA Modules:
  0.0 79.2 jit_solution(7973633315417092729)
XLA Ops:
  0.7 1.3 %dynamic-slice_bitcast_fusion = (bf16[128,1024]{1,0:T(8,128)(2,1)S(1)}, bf16[128,1024]{1,0:T(8,128)(2,1)S(1)}, bf16[128,1024]{1,0:T(8,128)(2,1)S(1)}, bf16[128,1024]{1,0:T(8,128)(2,1)S(1)}) fusion(bf16[1,128,4096]{2,1,0:T(8,128)(2,1)} %param.14, s32[]{:T(128)S(6)} %select_n.32, s32[]{:T(128)S(6)} %select_n.30, s32[]{:T(128)S(6)} %select_n.29, s32[]{:T(128)S(6)} %select_n.31), kind=kLoop, calls=%fused_computation.4 | loop fusion | bytes 2097168 | tf_op jit(solution)/shard_map/dynamic_slice | solution.py:381
  2.0 3.6 %collective-permute-start = (bf16[128,1024]{1,0:T(8,128)(2,1)S(1)}, bf16[128,1024]{1,0:T(8,128)(2,1)S(1)}, u32[]{:S(2)}, u32[]{:S(2)}) collective-permute-start(bf16[128,1024]{1,0:T(8,128)(2,1)S(1)} %get-tuple-element.40), channel_id=1, source_target_pairs={{0,3},{1,0},{2,1},{3,2},{8,11},{9,8},{10,9},{11,10},{16,19},{17,16... | collective-permute-start | bytes 786440 | tf_op jit(solution)/shard_map/ppermute | solution.py:378
  5.6 1.4 %collective-permute-start.1 = (bf16[128,1024]{1,0:T(8,128)(2,1)S(1)}, bf16[128,1024]{1,0:T(8,128)(2,1)S(1)}, u32[]{:S(2)}, u32[]{:S(2)}) collective-permute-start(bf16[128,1024]{1,0:T(8,128)(2,1)S(1)} %get-tuple-element.39), channel_id=1, source_target_pairs={{0,11},{1,8},{2,9},{3,10},{8,19},{9,16},{10,17},{11,18},{16,27},{1... | collective-permute-start | bytes 786440 | tf_op jit(solution)/shard_map/ppermute | solution.py:378
  7.7 1.4 %select_select_fusion = s32[64,3,128]{2,1,0:T(4,128)} fusion(s32[]{:T(128)} %bitcast.23, s32[128]{0:T(128)} %bitcast.26, s32[128]{0:T(128)} %bitcast.27, pred[3]{0:T(512)(128)(4,1)S(1)} %get-tuple-element.42, pred[3]{0:T(512)(128)(4,1)S(1)} %get-tuple-element.43), kind=kLoop, calls=%fused_computation.8 | loop fusion | flops 49152 | bytes 99338 | tf_op jit(solution)/shard_map/jit(_where)/select_n | solution.py:388
  9.1 12.4 %all-to-all-start = ((s32[64,3,128]{2,1,0:T(4,128)}), s32[64,3,128]{2,1,0:T(4,128)S(1)}, u32[]{:S(2)}, u32[]{:S(2)}) async-start(s32[64,3,128]{2,1,0:T(4,128)} %select_select_fusion), calls=%async_computation | async-start | bytes 262144 | tf_op jit(solution)/shard_map/all_to_all | solution.py:389
  21.5 2.9 %collective-permute-start.6 = (bf16[128,1024]{1,0:T(8,128)(2,1)S(1)}, bf16[128,1024]{1,0:T(8,128)(2,1)S(1)}, u32[]{:S(2)}, u32[]{:S(2)}) collective-permute-start(bf16[128,1024]{1,0:T(8,128)(2,1)S(1)} %get-tuple-element.41), channel_id=1, source_target_pairs={{0,19},{1,16},{2,17},{3,18},{8,27},{9,24},{10,25},{11,26},{16,3},{... | collective-permute-start | bytes 786440 | tf_op jit(solution)/shard_map/ppermute | solution.py:378
  24.4 0.8 collective-permute-start.7
  25.1 2.2 %copy-done = bf16[1,512,4096]{2,1,0:T(8,128)(2,1)S(1)} copy-done((bf16[1,512,4096]{2,1,0:T(8,128)(2,1)S(1)}, bf16[1,512,4096]{2,1,0:T(8,128)(2,1)}, u32[]{:S(2)}) %copy-start) | copy-done | bytes 4194328
  27.3 0.7 copy-done.1
  29.5 1.5 %prepare.1 = (bf16[512,2048]{1,0:T(8,128)(2,1)S(1)}, f32[512,128]{1,0:T(8,128)S(1)}, f32[64,128]{1,0:T(8,128)S(1)}) custom-call(bf16[512,4096]{1,0:T(8,128)(2,1)S(1)} %bitcast.24, f32[1,4096]{1,0:T(1,128)S(1)} %copy-done.2, f32[32,64]{1,0:T(8,128)S(1)} %bitcast.25, f32[32,128]{1,0:T(8,128)S(1)} %copy-done.5), custom_call_target="tpu_custom_call" | custom-call | flops 5000000000 | bytes 7340032 | tf_op jit(solution)/shard_map/prepare/pallas_call | solution.py:80
  31.0 1.3 %copy-done.8 = bf16[512,2048]{1,0:T(8,128)(2,1)} copy-done((bf16[512,2048]{1,0:T(8,128)(2,1)}, bf16[512,2048]{1,0:T(8,128)(2,1)S(1)}, u32[]{:S(2)}) %copy-start.8) | copy-done | bytes 2097176
  32.6 1.6 %copy-done.9 = bf16[512,2048]{1,0:T(8,128)(2,1)S(1)} copy-done((bf16[512,2048]{1,0:T(8,128)(2,1)S(1)}, bf16[512,2048]{1,0:T(8,128)(2,1)}, u32[]{:S(2)}) %copy-start.9) | copy-done | bytes 2097176
  34.2 4.1 %forward.1 = (bf16[128,1024]{1,0:T(8,128)(2,1)S(1)}, bf16[128,1024]{1,0:T(8,128)(2,1)S(1)}, bf16[128,1024]{1,0:T(8,128)(2,1)S(1)}, bf16[128,1024]{1,0:T(8,128)(2...) custom-call(s32[64,3,128]{2,1,0:T(4,128)S(1)} %all-to-all-done.notes_ref, ...), custom_call_target="tpu_custom_call" | custom-call | flops 8000000000 | bytes 7340032 | tf_op jit(solution)/shard_map/forward/pallas_call | solution.py:176
  38.6 5.6 %backward.1 = (bf16[10,32,8,128]{3,2,1,0:T(8,128)(2,1)S(1)}, bf16[10,32,8,128]{3,2,1,0:T(8,128)(2,1)S(1)}) custom-call(s32[64,3,128]{2,1,0:T(4,128)S(1)} %all-to-all-done.notes_ref, bf16[512,2048]{1,0:T(8,128)(2,1)S(1)} %copy-done.10, f32[512,128]{1,0:T(8,128)S(1)} %get-tuple-element.28.r_ref, f32[1,4096]{1,0:T(1,128)S(1)} %copy-done.3, ...), custom_call_target="tpu_custom_call" | custom-call | flops 10000000000 | bytes 10485760 | tf_op jit(solution)/shard_map/backward/pallas_call | solution.py:267
  44.2 0.8 %copy-done.6 = bf16[10,32,8,128]{3,2,1,0:T(8,128)(2,1)} copy-done((bf16[10,32,8,128]{3,2,1,0:T(8,128)(2,1)}, bf16[10,32,8,128]{3,2,1,0:T(8,128)(2,1)S(1)}, u32[]{:S(2)}) %copy-start.6) | copy-done | bytes 655384
  45.1 1.0 %collective-permute-start.8 = (bf16[10,32,8,128]{3,2,1,0:T(8,128)(2,1)S(1)}, bf16[10,32,8,128]{3,2,1,0:T(8,128)(2,1)S(1)}, u32[]{:S(2)}, u32[]{:S(2)}) collective-permute-start(bf16[10,32,8,128]{3,2,1,0:T(8,128)(2,1)S(1)} %get-tuple-element.34), channel_id=1, source_target_pairs={{0,4},{4,0},{1,5},{5,1},{2,6},{6,2},{3,7},{7,3},{8,12},{12,8},{9,1... | collective-permute-start | bytes 1966088 | tf_op jit(solution)/shard_map/ppermute | solution.py:394
  46.1 2.4 %collective-permute-start.2 = (bf16[128,1024]{1,0:T(8,128)(2,1)S(1)}, bf16[128,1024]{1,0:T(8,128)(2,1)S(1)}, u32[]{:S(2)}, u32[]{:S(2)}) collective-permute-start(bf16[128,1024]{1,0:T(8,128)(2,1)S(1)} %get-tuple-element.24), channel_id=1, source_target_pairs={{0,17},{1,18},{2,19},{3,16},{8,25},{9,26},{10,27},{11,24},{16,1},{... | collective-permute-start | bytes 786440 | tf_op jit(solution)/shard_map/ppermute | solution.py:378
  48.5 2.0 %collective-permute-start.3 = (bf16[128,1024]{1,0:T(8,128)(2,1)S(1)}, bf16[128,1024]{1,0:T(8,128)(2,1)S(1)}, u32[]{:S(2)}, u32[]{:S(2)}) collective-permute-start(bf16[128,1024]{1,0:T(8,128)(2,1)S(1)} %get-tuple-element.25), channel_id=1, source_target_pairs={{0,25},{1,26},{2,27},{3,24},{8,1},{9,2},{10,3},{11,0},{16,9},{17,1... | collective-permute-start | bytes 786440 | tf_op jit(solution)/shard_map/ppermute | solution.py:378
  50.4 1.1 %copy-done.7 = bf16[10,32,8,128]{3,2,1,0:T(8,128)(2,1)S(1)} copy-done((bf16[10,32,8,128]{3,2,1,0:T(8,128)(2,1)S(1)}, bf16[10,32,8,128]{3,2,1,0:T(8,128)(2,1)}, u32[]{:S(2)}) %copy-start.7) | copy-done | bytes 655384
  51.5 1.3 %join.1 = bf16[32,10,8,128]{3,2,1,0:T(8,128)(2,1)} custom-call(bf16[10,32,8,128]{3,2,1,0:T(8,128)(2,1)S(1)} %copy-done.7, bf16[10,32,8,128]{3,2,1,0:T(8,128)(2,1)S(1)} %collective-permute-done.8.came_ref), custom_call_target="tpu_custom_call" | custom-call | flops 2000000000 | bytes 4194304 | tf_op jit(solution)/shard_map/join/pallas_call | solution.py:304
  52.9 6.9 %all-to-all-start.1 = ((bf16[32,10,8,128]{3,2,1,0:T(8,128)(2,1)}), bf16[32,10,8,128]{3,2,1,0:T(8,128)(2,1)S(1)}, u32[]{:S(2)}, u32[]{:S(2)}) async-start(bf16[32,10,8,128]{3,2,1,0:T(8,128)(2,1)} %join.1), calls=%async_computation.1 | async-start | bytes 1310720 | tf_op jit(solution)/shard_map/all_to_all | solution.py:399
  59.7 0.9 %dynamic-slice_bitcast_fusion.4.table_ref = bf16[8,4096]{1,0:T(8,128)(2,1)S(1)} fusion(bf16[1,512,4096]{2,1,0:T(8,128)(2,1)} %param.11, s32[]{:T(128)S(6)} %select_n.33), kind=kLoop, calls=%fused_computation.9 | loop fusion | bytes 131076 | tf_op jit(solution)/shard_map/dynamic_slice | solution.py:400
  60.6 1.9 %collective-permute-start.4 = (bf16[128,1024]{1,0:T(8,128)(2,1)S(1)}, bf16[128,1024]{1,0:T(8,128)(2,1)S(1)}, u32[]{:S(2)}, u32[]{:S(2)}) collective-permute-start(bf16[128,1024]{1,0:T(8,128)(2,1)S(1)} %get-tuple-element.26), channel_id=1, source_target_pairs={{0,9},{1,10},{2,11},{3,8},{8,17},{9,18},{10,19},{11,16},{16,25},{1... | collective-permute-start | bytes 786440 | tf_op jit(solution)/shard_map/ppermute | solution.py:378
  62.6 1.2 %collective-permute-start.5 = (bf16[128,1024]{1,0:T(8,128)(2,1)S(1)}, bf16[128,1024]{1,0:T(8,128)(2,1)S(1)}, u32[]{:S(2)}, u32[]{:S(2)}) collective-permute-start(bf16[128,1024]{1,0:T(8,128)(2,1)S(1)} %get-tuple-element.27), channel_id=1, source_target_pairs={{0,1},{1,2},{2,3},{3,0},{8,9},{9,10},{10,11},{11,8},{16,17},{17,18... | collective-permute-start | bytes 786440 | tf_op jit(solution)/shard_map/ppermute | solution.py:378
  63.7 1.1 %broadcast_in_dim.43 = bf16[1,128,4096]{2,1,0:T(8,128)(2,1)} broadcast(bf16[]{:T(256)} %constant.41.clone.1), dimensions={} | broadcast | bytes 1048578 | tf_op jit(solution)/shard_map/broadcast_in_dim | solution.py:401
  64.8 0.7 bitcast_dynamic-update-slice_fusion.3
  65.5 0.7 bitcast_dynamic-update-slice_fusion.2
  66.3 9.6 %collective-permute-done.4 = bf16[128,1024]{1,0:T(8,128)(2,1)S(1)} collective-permute-done((bf16[128,1024]{1,0:T(8,128)(2,1)S(1)}, bf16[128,1024]{1,0:T(8,128)(2,1)S(1)}, u32[]{:S(2)}, u32[]{:S(2)}) %collective-permute-start.4) | collective-permute-done | bytes 262176 | tf_op jit(solution)/shard_map/ppermute | solution.py:378
  75.8 0.7 bitcast_dynamic-update-slice_fusion.1
  76.5 0.7 bitcast_dynamic-update-slice_fusion
  77.3 1.1 %all-to-all-done.1.parts_ref = bf16[32,10,8,128]{3,2,1,0:T(8,128)(2,1)S(1)} async-done(((bf16[32,10,8,128]{3,2,1,0:T(8,128)(2,1)}), bf16[32,10,8,128]{3,2,1,0:T(8,128)(2,1)S(1)}, u32[]{:S(2)}, u32[]{:S(2)}) %all-to-all-start.1) | async-done | bytes 655392 | tf_op jit(solution)/shard_map/all_to_all | solution.py:399
  78.3 0.9 %finish.1 = (f32[1,8,4096]{2,1,0:T(8,128)}, f32[1,4096]{1,0:T(1,128)}, f32[1,32,64]{2,1,0:T(8,128)}) custom-call(bf16[32,10,8,128]{3,2,1,0:T(8,128)(2,1)S(1)} %all-to-all-done.1.parts_ref, bf16[8,4096]{1,0:T(8,128)(2,1)S(1)} %dynamic-slice_bitcast_fusion.4.table_ref, f32[512,128]{1,0:T(8,128)S(1)} %get-tuple-element.28.r_ref), custom_call_target="tpu_custom_call" | custom-call | flops 2000000000 | bytes 2097152 | tf_op jit(solution)/shard_map/finish/pallas_call | solution.py:350
  (26 shorter events, 2.1 us)
Async XLA Ops:
  2.0 23.2 %collective-permute-start = (bf16[128,1024]{1,0:T(8,128)(2,1)S(1)}, bf16[128,1024]{1,0:T(8,128)(2,1)S(1)}, u32[]{:S(2)}, u32[]{:S(2)}) collective-permute-start(bf16[128,1024]{1,0:T(8,128)(2,1)S(1)} %get-tuple-element.40), channel_id=1, source_target_pairs={{0,3},{1,0},{2,1},{3,2},{8,11},{9,8},{10,9},{11,10},{16,19},{17,16... | collective-permute-start | bytes 786440 | tf_op jit(solution)/shard_map/ppermute | solution.py:378
  5.6 19.5 %collective-permute-start.1 = (bf16[128,1024]{1,0:T(8,128)(2,1)S(1)}, bf16[128,1024]{1,0:T(8,128)(2,1)S(1)}, u32[]{:S(2)}, u32[]{:S(2)}) collective-permute-start(bf16[128,1024]{1,0:T(8,128)(2,1)S(1)} %get-tuple-element.39), channel_id=1, source_target_pairs={{0,11},{1,8},{2,9},{3,10},{8,19},{9,16},{10,17},{11,18},{16,27},{1... | collective-permute-start | bytes 786440 | tf_op jit(solution)/shard_map/ppermute | solution.py:378
  9.1 23.5 %all-to-all-start = ((s32[64,3,128]{2,1,0:T(4,128)}), s32[64,3,128]{2,1,0:T(4,128)S(1)}, u32[]{:S(2)}, u32[]{:S(2)}) async-start(s32[64,3,128]{2,1,0:T(4,128)} %select_select_fusion), calls=%async_computation | async-start | bytes 262144 | tf_op jit(solution)/shard_map/all_to_all | solution.py:389
  21.5 16.8 %collective-permute-start.6 = (bf16[128,1024]{1,0:T(8,128)(2,1)S(1)}, bf16[128,1024]{1,0:T(8,128)(2,1)S(1)}, u32[]{:S(2)}, u32[]{:S(2)}) collective-permute-start(bf16[128,1024]{1,0:T(8,128)(2,1)S(1)} %get-tuple-element.41), channel_id=1, source_target_pairs={{0,19},{1,16},{2,17},{3,18},{8,27},{9,24},{10,25},{11,26},{16,3},{... | collective-permute-start | bytes 786440 | tf_op jit(solution)/shard_map/ppermute | solution.py:378
  24.4 14.3 %collective-permute-start.7 = (bf16[128,1024]{1,0:T(8,128)(2,1)S(1)}, bf16[128,1024]{1,0:T(8,128)(2,1)S(1)}, u32[]{:S(2)}, u32[]{:S(2)}) collective-permute-start(bf16[128,1024]{1,0:T(8,128)(2,1)S(1)} %get-tuple-element.38), channel_id=1, source_target_pairs={{0,27},{1,24},{2,25},{3,26},{8,3},{9,0},{10,1},{11,2},{16,11},{17,... | collective-permute-start | bytes 786440 | tf_op jit(solution)/shard_map/ppermute | solution.py:378
  25.1 2.2 %copy-start = (bf16[1,512,4096]{2,1,0:T(8,128)(2,1)S(1)}, bf16[1,512,4096]{2,1,0:T(8,128)(2,1)}, u32[]{:S(2)}) copy-start(bf16[1,512,4096]{2,1,0:T(8,128)(2,1)} %param.11) | copy-start | bytes 12582916
  27.3 0.7 copy-start.1
  28.0 0.7 copy-start.2
  28.8 0.7 copy-start.5
  31.0 1.3 %copy-start.8 = (bf16[512,2048]{1,0:T(8,128)(2,1)}, bf16[512,2048]{1,0:T(8,128)(2,1)S(1)}, u32[]{:S(2)}) copy-start(bf16[512,2048]{1,0:T(8,128)(2,1)S(1)} %get-tuple-element.22.ne_hbm.ne_ref) | copy-start | bytes 6291460
  32.6 1.6 %copy-start.9 = (bf16[512,2048]{1,0:T(8,128)(2,1)S(1)}, bf16[512,2048]{1,0:T(8,128)(2,1)}, u32[]{:S(2)}) copy-start(bf16[512,2048]{1,0:T(8,128)(2,1)} %copy-done.8) | copy-start | bytes 6291460
  34.2 4.4 %copy-start.3 = (f32[1,4096]{1,0:T(1,128)S(1)}, f32[1,4096]{1,0:T(1,128)}, u32[]{:S(2)}) copy-start(f32[1,4096]{1,0:T(1,128)} %gain_ref.3) | copy-start | bytes 49156
  34.2 4.4 %copy-start.4 = (f32[128,128]{1,0:T(8,128)S(1)}, f32[128,128]{1,0:T(8,128)}, u32[]{:S(2)}) copy-start(f32[128,128]{1,0:T(8,128)} %constant.56.clone.picks_ref) | copy-start | bytes 196612
  34.2 4.4 %copy-start.10 = (bf16[512,2048]{1,0:T(8,128)(2,1)S(1)}, bf16[512,2048]{1,0:T(8,128)(2,1)}, u32[]{:S(2)}) copy-start(bf16[512,2048]{1,0:T(8,128)(2,1)} %copy-done.8) | copy-start | bytes 6291460
  44.2 0.8 %copy-start.6 = (bf16[10,32,8,128]{3,2,1,0:T(8,128)(2,1)}, bf16[10,32,8,128]{3,2,1,0:T(8,128)(2,1)S(1)}, u32[]{:S(2)}) copy-start(bf16[10,32,8,128]{3,2,1,0:T(8,128)(2,1)S(1)} %get-tuple-element.33.mine_ref) | copy-start | bytes 1966084
  45.1 5.4 %collective-permute-start.8 = (bf16[10,32,8,128]{3,2,1,0:T(8,128)(2,1)S(1)}, bf16[10,32,8,128]{3,2,1,0:T(8,128)(2,1)S(1)}, u32[]{:S(2)}, u32[]{:S(2)}) collective-permute-start(bf16[10,32,8,128]{3,2,1,0:T(8,128)(2,1)S(1)} %get-tuple-element.34), channel_id=1, source_target_pairs={{0,4},{4,0},{1,5},{5,1},{2,6},{6,2},{3,7},{7,3},{8,12},{12,8},{9,1... | collective-permute-start | bytes 1966088 | tf_op jit(solution)/shard_map/ppermute | solution.py:394
  46.1 17.7 %collective-permute-start.2 = (bf16[128,1024]{1,0:T(8,128)(2,1)S(1)}, bf16[128,1024]{1,0:T(8,128)(2,1)S(1)}, u32[]{:S(2)}, u32[]{:S(2)}) collective-permute-start(bf16[128,1024]{1,0:T(8,128)(2,1)S(1)} %get-tuple-element.24), channel_id=1, source_target_pairs={{0,17},{1,18},{2,19},{3,16},{8,25},{9,26},{10,27},{11,24},{16,1},{... | collective-permute-start | bytes 786440 | tf_op jit(solution)/shard_map/ppermute | solution.py:378
  48.5 17.1 %collective-permute-start.3 = (bf16[128,1024]{1,0:T(8,128)(2,1)S(1)}, bf16[128,1024]{1,0:T(8,128)(2,1)S(1)}, u32[]{:S(2)}, u32[]{:S(2)}) collective-permute-start(bf16[128,1024]{1,0:T(8,128)(2,1)S(1)} %get-tuple-element.25), channel_id=1, source_target_pairs={{0,25},{1,26},{2,27},{3,24},{8,1},{9,2},{10,3},{11,0},{16,9},{17,1... | collective-permute-start | bytes 786440 | tf_op jit(solution)/shard_map/ppermute | solution.py:378
  50.4 1.1 %copy-start.7 = (bf16[10,32,8,128]{3,2,1,0:T(8,128)(2,1)S(1)}, bf16[10,32,8,128]{3,2,1,0:T(8,128)(2,1)}, u32[]{:S(2)}) copy-start(bf16[10,32,8,128]{3,2,1,0:T(8,128)(2,1)} %copy-done.6) | copy-start | bytes 1966084
  52.9 25.5 %all-to-all-start.1 = ((bf16[32,10,8,128]{3,2,1,0:T(8,128)(2,1)}), bf16[32,10,8,128]{3,2,1,0:T(8,128)(2,1)S(1)}, u32[]{:S(2)}, u32[]{:S(2)}) async-start(bf16[32,10,8,128]{3,2,1,0:T(8,128)(2,1)} %join.1), calls=%async_computation.1 | async-start | bytes 1310720 | tf_op jit(solution)/shard_map/all_to_all | solution.py:399
  60.6 15.2 %collective-permute-start.4 = (bf16[128,1024]{1,0:T(8,128)(2,1)S(1)}, bf16[128,1024]{1,0:T(8,128)(2,1)S(1)}, u32[]{:S(2)}, u32[]{:S(2)}) collective-permute-start(bf16[128,1024]{1,0:T(8,128)(2,1)S(1)} %get-tuple-element.26), channel_id=1, source_target_pairs={{0,9},{1,10},{2,11},{3,8},{8,17},{9,18},{10,19},{11,16},{16,25},{1... | collective-permute-start | bytes 786440 | tf_op jit(solution)/shard_map/ppermute | solution.py:378
  62.6 14.0 %collective-permute-start.5 = (bf16[128,1024]{1,0:T(8,128)(2,1)S(1)}, bf16[128,1024]{1,0:T(8,128)(2,1)S(1)}, u32[]{:S(2)}, u32[]{:S(2)}) collective-permute-start(bf16[128,1024]{1,0:T(8,128)(2,1)S(1)} %get-tuple-element.27), channel_id=1, source_target_pairs={{0,1},{1,2},{2,3},{3,0},{8,9},{9,10},{10,11},{11,8},{16,17},{17,18... | collective-permute-start | bytes 786440 | tf_op jit(solution)/shard_map/ppermute | solution.py:378
